TPU v7x, 32 devices: a whole 2x2x4 slice. The times are simulated.
32 devices in a mesh: fsdp: 8 (over y, x, core), tp: 4 (over z).
Axes of the slice: x: 2, y: 2, z: 4, core: 2. Of those that a mesh axis runs over, the one named last changes fastest.
Arguments:
- inputs: bfloat16 [2, 4096, 1024], P(None, ('fsdp', 'tp')), may hold values from -6 to 6
- cotangent: bfloat16 [2, 4096, 1024], P(None, ('fsdp', 'tp')), may hold values from -6 to 6
- lengths: int32 [2], replicated, may hold values from 1024 to 4096, as said below
- routes: int32 [2, 4096, 8], P(None, 'fsdp'), may hold values from 0 to 15, all different within a row; in each aligned block of 512 rows (0 to 511, 512 to 1023, ..., all dimensions but the last counted through in order) at most 384 rows name the same one
- attn_gain: bfloat16 [1024], P(('fsdp', 'tp')), may hold values from 0.5 to 1.5
- moe_gain: bfloat16 [1024], P(('fsdp', 'tp')), may hold values from 0.5 to 1.5
- router_weight: bfloat16 [1024, 16], P(('fsdp', 'tp')), may hold values from -0.09375 to 0.09375
- query_weight: bfloat16 [1024, 1024], P('fsdp', 'tp'), may hold values from -0.1875 to 0.1875
- key_weight: bfloat16 [1024, 512], P('fsdp', 'tp'), may hold values from -0.1875 to 0.1875
- value_weight: bfloat16 [1024, 512], P('fsdp', 'tp'), may hold values from -0.1875 to 0.1875
- output_weight: bfloat16 [1024, 1024], P('tp', 'fsdp'), may hold values from -3 to 3
- gate_weight: bfloat16 [16, 1024, 512], P(None, 'fsdp', 'tp'), may hold values from -0.1875 to 0.1875
- up_weight: bfloat16 [16, 1024, 512], P(None, 'fsdp', 'tp'), may hold values from -0.1875 to 0.1875
- down_weight: bfloat16 [16, 512, 1024], P(None, 'tp', 'fsdp'), may hold values from -0.75 to 0.75
Outputs:
- outputs: bfloat16 [2, 4096, 1024], P(None, ('fsdp', 'tp'))
- input_grad: float32 [2, 4096, 1024], P(None, ('fsdp', 'tp'))
- attn_gain_grad: float32 [1024], P(('fsdp', 'tp'))
- moe_gain_grad: float32 [1024], P(('fsdp', 'tp'))
- router_grad: float32 [1024, 16], P(('fsdp', 'tp'))
- query_grad: float32 [1024, 1024], P('fsdp', 'tp')
- key_grad: float32 [1024, 512], P('fsdp', 'tp')
- value_grad: float32 [1024, 512], P('fsdp', 'tp')
- output_grad: float32 [1024, 1024], P('tp', 'fsdp')
- gate_grad: float32 [16, 1024, 512], P(None, 'fsdp', 'tp')
- up_grad: float32 [16, 1024, 512], P(None, 'fsdp', 'tp')
- down_grad: float32 [16, 512, 1024], P(None, 'tp', 'fsdp')
Inputs may be any that keep to these rules, and one draw needn't show every extreme that they name: `lengths`: one slot has exactly 4096 valid tokens; the others have 4096/4 to 4096. `routes`: each token names 8 different experts. Within the 512 tokens of one slot on one index of fsdp (aligned blocks), no expert is named by more than 384 tokens, a bound that some block reaches.
All inputs are finite; a program needn't handle non-finite values.
Results may differ from a plain program's by a relative error of at most 0.029.
Values may be sent and summed in bfloat16 or wider, within the bound.
A program may use at most 320 MiB of HBM per device.

v0:
```python
import functools

import jax
import jax.numpy as jnp
from jax import lax
from jax.experimental import pallas as pl
from jax.experimental.pallas import tpu as pltpu
from jax.sharding import PartitionSpec as P

HD = 64
LANES = 128
PAIR = 2
EPS = 1e-06
FILL = -1e30
THETA = 10000.0
VMEM_CAP = 60 * 1024 * 1024
f32 = jnp.float32
bf16 = jnp.bfloat16


def dot_nn(a, b):
    return lax.dot_general(a, b, (((1,), (0,)), ((), ())), preferred_element_type=f32)


def dot_nt(a, b):
    return lax.dot_general(a, b, (((1,), (1,)), ((), ())), preferred_element_type=f32)


def swap_halves(values):
    lane = lax.broadcasted_iota(jnp.int32, values.shape, values.ndim - 1)
    ahead = pltpu.roll(values, values.shape[-1] - HD // 2, values.ndim - 1)
    back = pltpu.roll(values, HD // 2, values.ndim - 1)
    return jnp.where(lane % HD < HD // 2, ahead, back)


def rope_tables(positions):
    half = HD // 2
    freqs = THETA ** (-jnp.arange(half, dtype=f32) * 2.0 / HD)
    angles = positions.astype(f32)[:, None] * freqs[None, :]
    cosine, sine = jnp.cos(angles), jnp.sin(angles)
    cos_row = jnp.concatenate([cosine] * 4, axis=1)
    sin_row = jnp.concatenate([-sine, sine] * 2, axis=1)
    return cos_row, sin_row


def head_rows(values, head):
    key_head, member = head // 2, head % 2
    pair = values[:, key_head * LANES : (key_head + 1) * LANES]
    if member != key_head:
        pair = pltpu.roll(pair, HD, 1)
    lane = lax.broadcasted_iota(jnp.int32, pair.shape, 1)
    return jnp.where(lane // HD == key_head, pair, jnp.zeros_like(pair))


def join_heads(first, second, key_head):
    if key_head == 0:
        second = pltpu.roll(second, HD, 1)
    else:
        first = pltpu.roll(first, HD, 1)
    lane = lax.broadcasted_iota(jnp.int32, first.shape, 1)
    return jnp.where(lane < HD, first, second)


def cost(microseconds):
    return pl.CostEstimate(flops=int(microseconds * 9e8), bytes_accessed=1024, transcendentals=0)


def params():
    return pltpu.CompilerParams(vmem_limit_bytes=VMEM_CAP)


def shape(dims, kind):
    return jax.ShapeDtypeStruct(dims, kind)


def normalised(x, gain):
    inverse = lax.rsqrt(jnp.mean(x * x, axis=-1, keepdims=True) + EPS)
    unit = x * inverse
    return inverse, unit, unit * gain


def qkv_kernel(*refs):
    x_refs = refs[:-6]
    gain_ref, w_ref, cos_ref, sin_ref, q_ref, kv_ref = refs[-6:]
    rows = x_refs[0].shape[0]
    for slot, x_ref in enumerate(x_refs):
        here = slice(slot * rows, (slot + 1) * rows)
        cos_row, sin_row = cos_ref[here, :], sin_ref[here, :]
        _, _, normed = normalised(x_ref[...].astype(f32), gain_ref[...])
        pre = dot_nn(normed.astype(bf16), w_ref[...])
        for part in range(3):
            cols = pre[:, part * LANES : (part + 1) * LANES]
            turned = cols * cos_row + swap_halves(cols) * sin_row
            if part < 2:
                q_ref[here, part * LANES : (part + 1) * LANES] = (turned * HD ** (-0.5)).astype(bf16)
            else:
                kv_ref[here, 0:LANES] = turned.astype(bf16)
        kv_ref[here, LANES : 2 * LANES] = pre[:, 3 * LANES : 4 * LANES].astype(bf16)


def project_qkv(x_slots, gain, weight, cos_row, sin_row):
    span = cos_row.shape[0]
    return pl.pallas_call(
        qkv_kernel,
        out_shape=[shape((span, 2 * LANES), bf16), shape((span, 2 * LANES), bf16)],
        compiler_params=params(),
        cost_estimate=cost(3),
        name="project_qkv",
    )(*x_slots, gain, weight, cos_row, sin_row)


def reversed_bits(index, count):
    result, bit = 0, 1
    while bit < count:
        result = result + ((index // bit) % 2) * (count // (2 * bit))
        bit *= 2
    return result


def places(rank, rows, dims, axis):
    index = lax.broadcasted_iota(jnp.int32, dims, axis)
    return (rank ^ (index // rows)) * rows + index % rows


def allowed_keys(rank, rows, span, key_start, query_start, length):
    key_pos = key_start + places(rank, rows, (span, span), 0)
    query_pos = query_start + places(rank, rows, (span, span), 1)
    return (key_pos <= query_pos) & (key_pos < length)


def block_kind(info_ref, j, span, count):
    mine, length = info_ref[0], info_ref[2]
    other = mine ^ reversed_bits(j, count)
    wanted = (other <= mine) & (mine * span < length) & (other * span < length)
    edge = (other == mine) | ((other + 1) * span > length)
    return other, wanted, edge


def attend_kernel(info_ref, q_ref, kv_ref, *refs):
    heads, best, total, accum = refs[-4:]
    out_refs, log_ref = refs[:-5], refs[-5]
    j = pl.program_id(0)
    count = pl.num_programs(0)
    mine, rank, length = info_ref[0], info_ref[1], info_ref[2]
    rows = out_refs[0].shape[0]
    span = q_ref.shape[0]
    other, wanted, edge = block_kind(info_ref, j, span, BLOCKS[0])

    @pl.when(j == 0)
    def _():
        values = q_ref[...].astype(f32)
        for head in range(4):
            heads[head] = head_rows(values, head).astype(bf16)
        best[...] = jnp.full(best.shape, FILL, f32)
        total[...] = jnp.zeros(total.shape, f32)
        accum[...] = jnp.zeros(accum.shape, f32)

    def block(masked):
        keys = kv_ref[0, :, :LANES]
        values_t = kv_ref[0, :, LANES:].astype(f32).T.astype(bf16)
        if masked:
            allowed = allowed_keys(rank, rows, span, other * span, mine * span, length)
        for head in range(4):
            scores = dot_nt(keys, heads[head])
            if masked:
                scores = jnp.where(allowed, scores, FILL)
            old = best[head : head + 1]
            new = jnp.maximum(old, jnp.max(scores, axis=0, keepdims=True))
            factor = jnp.exp(old - new)
            weights = jnp.exp(scores - new)
            if masked:
                weights = jnp.where(allowed, weights, 0.0)
            best[head : head + 1] = new
            total[head : head + 1] = total[head : head + 1] * factor + jnp.sum(weights, axis=0, keepdims=True)
            accum[head] = accum[head] * factor + dot_nn(values_t, weights.astype(bf16))

    @pl.when(wanted & edge)
    def _():
        block(True)

    @pl.when(wanted & jnp.logical_not(edge))
    def _():
        block(False)

    @pl.when(j == count - 1)
    def _():
        live = mine * span < length
        for key_head in range(2):
            pair = []
            for member in range(2):
                head = key_head * 2 + member
                sums = jnp.where(live, total[head : head + 1], 1.0)
                log_ref[head : head + 1] = best[head : head + 1] + jnp.log(sums)
                pair.append((accum[head] * (1.0 / sums)).T)
            joined = join_heads(pair[0], pair[1], key_head).astype(bf16)
            for slot, out_ref in enumerate(out_refs):
                out_ref[:, key_head * LANES : (key_head + 1) * LANES] = joined[slot * rows : (slot + 1) * rows]


BLOCKS = [0]


def attend(info, query, kv_all, rows):
    span, cols = query.shape
    blocks = kv_all.shape[0]
    slots = span // rows
    BLOCKS[0] = blocks
    return pl.pallas_call(
        attend_kernel,
        grid_spec=pltpu.PrefetchScalarGridSpec(
            num_scalar_prefetch=1,
            grid=(blocks,),
            in_specs=[
                pl.BlockSpec((span, cols), lambda j, info_ref: (0, 0)),
                pl.BlockSpec((1, span, 2 * LANES), lambda j, info_ref: (j, 0, 0)),
            ],
            out_specs=[pl.BlockSpec((rows, cols), lambda j, info_ref: (0, 0))] * slots
            + [pl.BlockSpec((8, span), lambda j, info_ref: (0, 0))],
            scratch_shapes=[
                pltpu.VMEM((4, span, LANES), bf16),
                pltpu.VMEM((8, span), f32),
                pltpu.VMEM((8, span), f32),
                pltpu.VMEM((4, LANES, span), f32),
            ],
        ),
        out_shape=[shape((rows, cols), bf16)] * slots + [shape((8, span), f32)],
        compiler_params=params(),
        cost_estimate=cost(12),
        name="attend",
    )(info, query, kv_all)


def attend_back_kernel(slots, info_ref, q_ref, kv_ref, log_ref, cos_ref, sin_ref, *refs):
    out_refs, grad_refs = refs[:slots], refs[slots : 2 * slots]
    dq_ref, keep_ref, send_ref, heads, grads, delta, accum, dkv = refs[2 * slots :]
    j = pl.program_id(0)
    count = pl.num_programs(0)
    mine, rank, length = info_ref[0], info_ref[1], info_ref[2]
    span, cols = q_ref.shape
    rows = span // slots
    other, wanted, edge = block_kind(info_ref, j, span, BLOCKS[0])

    @pl.when(j == 0)
    def _():
        values = q_ref[...].astype(f32)
        attended = jnp.concatenate([ref[...] for ref in out_refs], axis=0).astype(f32)
        grad = jnp.concatenate([ref[...] for ref in grad_refs], axis=0).astype(f32)
        product = grad * attended
        for head in range(4):
            heads[head] = head_rows(values, head).astype(bf16)
            grads[head] = head_rows(grad, head).astype(bf16)
            delta[head : head + 1] = jnp.sum(head_rows(product, head).T, axis=0, keepdims=True)
        accum[...] = jnp.zeros(accum.shape, f32)

    def block(masked):
        keys = kv_ref[0, :, :LANES]
        values = kv_ref[0, :, LANES:]
        keys_t = keys.astype(f32).T.astype(bf16)
        if masked:
            allowed = allowed_keys(rank, rows, span, other * span, mine * span, length)
        grad_keys = jnp.zeros((span, LANES), f32)
        grad_values = jnp.zeros((span, LANES), f32)
        for head in range(4):
            scores = dot_nt(keys, heads[head])
            probs = jnp.exp(scores - log_ref[head : head + 1])
            if masked:
                probs = jnp.where(allowed, probs, 0.0)
            grad_probs = dot_nt(values, grads[head])
            grad_scores = (probs * (grad_probs - delta[head : head + 1])).astype(bf16)
            grad_values = grad_values + dot_nn(probs.astype(bf16), grads[head])
            grad_keys = grad_keys + dot_nn(grad_scores, heads[head])
            accum[head] = accum[head] + dot_nn(keys_t, grad_scores)
        dkv[:, 0:LANES] = grad_keys.astype(bf16)
        dkv[:, LANES : 2 * LANES] = grad_values.astype(bf16)

    @pl.when(wanted & edge)
    def _():
        block(True)

    @pl.when(wanted & jnp.logical_not(edge))
    def _():
        block(False)

    @pl.when(jnp.logical_not(wanted))
    def _():
        dkv[...] = jnp.zeros(dkv.shape, bf16)

    @pl.when(j < count // 2)
    def _():
        keep_ref[0] = dkv[...]

    @pl.when(j >= count // 2)
    def _():
        send_ref[0] = dkv[...]

    @pl.when(j == count - 1)
    def _():
        for key_head in range(2):
            pair = [accum[key_head * 2 + member].T for member in range(2)]
            joined = join_heads(pair[0], pair[1], key_head) * HD ** (-0.5)
            turned = joined * cos_ref[...] - swap_halves(joined) * sin_ref[...]
            dq_ref[:, key_head * LANES : (key_head + 1) * LANES] = turned.astype(bf16)


def attend_back(info, query, kv_all, log_total, cos_row, sin_row, att_slots, grad_slots):
    span, cols = query.shape
    blocks, slots = kv_all.shape[0], len(att_slots)
    rows, half = span // slots, blocks // 2
    BLOCKS[0] = blocks
    fixed = lambda *dims: pl.BlockSpec(dims, lambda j, info_ref: (0,) * len(dims))
    return pl.pallas_call(
        functools.partial(attend_back_kernel, slots),
        grid_spec=pltpu.PrefetchScalarGridSpec(
            num_scalar_prefetch=1,
            grid=(blocks,),
            in_specs=[
                fixed(span, cols),
                pl.BlockSpec((1, span, 2 * LANES), lambda j, info_ref: (j, 0, 0)),
                fixed(8, span),
                fixed(span, LANES),
                fixed(span, LANES),
            ]
            + [fixed(rows, cols)] * (2 * slots),
            out_specs=[
                fixed(span, cols),
                pl.BlockSpec((1, span, 2 * LANES), lambda j, info_ref: (jnp.minimum(j, half - 1), 0, 0)),
                pl.BlockSpec((1, span, 2 * LANES), lambda j, info_ref: (jnp.maximum(j - half, 0), 0, 0)),
            ],
            scratch_shapes=[
                pltpu.VMEM((4, span, LANES), bf16),
                pltpu.VMEM((4, span, LANES), bf16),
                pltpu.VMEM((8, span), f32),
                pltpu.VMEM((4, LANES, span), f32),
                pltpu.VMEM((span, 2 * LANES), bf16),
            ],
        ),
        out_shape=[shape((span, cols), bf16)] + [shape((half, span, 2 * LANES), bf16)] * 2,
        compiler_params=params(),
        cost_estimate=cost(18),
        name="attend_back",
    )(info, query, kv_all, log_total, cos_row, sin_row, *att_slots, *grad_slots)


def middle_kernel(x_ref, gain_ref, w_ref, *refs):
    att_refs, (att_all, middle_ref, normed_ref) = refs[:-3], refs[-3:]
    cols = att_refs[0].shape[1]
    for slot, att_ref in enumerate(att_refs):
        att_all[:, slot * cols : (slot + 1) * cols] = att_ref[...]
    middle = x_ref[...].astype(f32) + dot_nt(att_all[...], w_ref[...])
    middle_ref[...] = middle
    normed_ref[...] = normalised(middle, gain_ref[...])[2].astype(bf16)


def close_attention(x, gain, weight, att_slots):
    rows, width = x.shape
    return pl.pallas_call(
        middle_kernel,
        out_shape=[shape((rows, weight.shape[1]), bf16), shape((rows, width), f32), shape((rows, width), bf16)],
        compiler_params=params(),
        cost_estimate=cost(2),
        name="middle",
    )(x, gain, weight, *att_slots)


def expert_kernel(slots, info_ref, routes_ref, router_ref, w_ref, *refs):
    x_refs, gm_refs = refs[:slots], refs[slots : 2 * slots]
    gin_refs, mixed_refs = refs[2 * slots : 3 * slots], refs[3 * slots : 4 * slots]
    gates_ref, low_g, low_h, x_all, gm_all, gates, mixed, gin, gate_sums = refs[4 * slots :]
    step = pl.program_id(0)
    last = pl.num_programs(0) - 1
    span, width = x_all.shape
    rows = span // slots
    wide = PAIR * LANES
    chunk = 256
    rank = info_ref[1]

    @pl.when(step == 0)
    def _():
        lane = lax.broadcasted_iota(jnp.int32, (rows, LANES), 1)
        for slot in range(slots):
            here = slice(slot * rows, (slot + 1) * rows)
            x_all[here, :] = x_refs[slot][...]
            gm_all[here, :] = gm_refs[slot][...]
            named = routes_ref[pl.ds(pl.multiple_of((rank ^ slot) * rows, rows), rows), :]
            picked = lane == named[:, 0:1]
            for k in range(1, named.shape[1]):
                picked = picked | (lane == named[:, k : k + 1])
            logits = jnp.where(picked, dot_nn(x_refs[slot][...], router_ref[...]), FILL)
            peak = jnp.max(logits, axis=1, keepdims=True)
            exps = jnp.where(picked, jnp.exp(logits - peak), 0.0)
            gates[here, :] = exps / jnp.sum(exps, axis=1, keepdims=True)
        gates_ref[...] = gates[0:rows, :]
        mixed[...] = jnp.zeros(mixed.shape, f32)
        gin[...] = jnp.zeros(gin.shape, f32)
        gate_sums[...] = jnp.zeros(gate_sums.shape, f32)

    def rows_step(i, _):
        here = pl.ds(pl.multiple_of(i * chunk, chunk), chunk)
        pre = dot_nn(x_all[here, :], w_ref[:, : 2 * wide])
        gate_pre, up_pre = pre[:, :wide], pre[:, wide:]
        back = dot_nn(gm_all[here, :], w_ref[:, 2 * wide :])
        sig = 1.0 / (1.0 + jnp.exp(-gate_pre))
        silu = gate_pre * sig
        hidden = silu * up_pre
        lane = lax.broadcasted_iota(jnp.int32, (chunk, LANES), 1)
        product = hidden * back
        spread = []
        sums = gate_sums[here, :]
        for member in range(PAIR):
            hit = lane == step * PAIR + member
            gate = jnp.sum(jnp.where(hit, gates[here, :], 0.0), axis=1, keepdims=True)
            spread.append(jnp.broadcast_to(gate, (chunk, LANES)))
            amount = jnp.sum(product[:, member * LANES : (member + 1) * LANES], axis=1, keepdims=True)
            sums = sums + jnp.where(hit, amount, 0.0)
        gate_sums[here, :] = sums
        factor = jnp.concatenate(spread, axis=1)
        grad_hidden = factor * back
        low_hidden = (factor * hidden).astype(bf16)
        grad_up = (grad_hidden * silu).astype(bf16)
        grad_gate = (grad_hidden * up_pre * (sig * (1.0 + gate_pre * (1.0 - sig)))).astype(bf16)
        low_h[here, :] = low_hidden
        low_g[here, 0:wide] = grad_gate
        low_g[here, wide : 2 * wide] = grad_up
        mixed[here, :] += dot_nt(low_hidden, w_ref[:, 2 * wide :])
        gin[here, :] += dot_nt(low_g[here, :], w_ref[:, : 2 * wide])
        return 0

    lax.fori_loop(0, span // chunk, rows_step, 0)

    @pl.when(step == last)
    def _():
        for slot in range(slots):
            here = slice(slot * rows, (slot + 1) * rows)
            mixed_refs[slot][...] = mixed[here, :].astype(bf16)
            gin_refs[slot][:, 0:width] = gin[here, :].astype(bf16)
            gin_refs[slot][:, width : width + LANES] = gate_sums[here, :].astype(bf16)


def experts_both(info, routes, router, weight, x_slots, gm_slots):
    rows, width = x_slots[0].shape
    slots = len(x_slots)
    span = rows * slots
    wide = PAIR * LANES
    steps = weight.shape[1] // (3 * wide)
    fixed = lambda *dims: pl.BlockSpec(dims, lambda i, info_ref: (0,) * len(dims))
    moving = lambda height, cols: pl.BlockSpec((height, cols), lambda i, info_ref: (0, i))
    return pl.pallas_call(
        functools.partial(expert_kernel, slots),
        grid_spec=pltpu.PrefetchScalarGridSpec(
            num_scalar_prefetch=1,
            grid=(steps,),
            in_specs=[fixed(*routes.shape), fixed(*router.shape), moving(width, 3 * wide)]
            + [fixed(rows, width)] * (2 * slots),
            out_specs=[fixed(rows, width + LANES)] * slots
            + [fixed(rows, width)] * slots
            + [fixed(rows, LANES), moving(span, 2 * wide), moving(span, wide)],
            scratch_shapes=[
                pltpu.VMEM((span, width), bf16),
                pltpu.VMEM((span, width), bf16),
                pltpu.VMEM((span, LANES), f32),
                pltpu.VMEM((span, width), f32),
                pltpu.VMEM((span, width), f32),
                pltpu.VMEM((span, LANES), f32),
            ],
        ),
        out_shape=[shape((rows, width + LANES), bf16)] * slots
        + [shape((rows, width), bf16)] * slots
        + [shape((rows, LANES), f32), shape((span, steps * 2 * wide), bf16), shape((span, steps * wide), bf16)],
        compiler_params=params(),
        cost_estimate=cost(24),
        name="experts",
    )(info, routes, router, weight, *x_slots, *gm_slots)


def expert_grad_kernel(micro, slots, *refs):
    count = micro * slots
    x_refs, gm_refs = refs[:count], refs[count : 2 * count]
    g_refs, h_refs = refs[2 * count : 2 * count + micro], refs[2 * count + micro : 2 * count + 2 * micro]
    dw_ref, x_t, gm_t = refs[2 * count + 2 * micro :]
    rows = x_refs[0].shape[0]
    width = x_t.shape[0]
    wide = PAIR * LANES
    chunk = 256

    @pl.when(pl.program_id(0) == 0)
    def _():
        for i in range(count):
            x_t[:, i * rows : (i + 1) * rows] = x_refs[i][...].T
            gm_t[:, i * rows : (i + 1) * rows] = gm_refs[i][...].T

    def weight_step(i, _):
        here = pl.ds(pl.multiple_of(i * chunk, chunk), chunk)
        g_sum, h_sum = 0.0, 0.0
        for m in range(micro):
            part = slice(m * slots * rows, (m + 1) * slots * rows)
            g_sum = g_sum + dot_nn(x_t[here, part], g_refs[m][...])
            h_sum = h_sum + dot_nn(gm_t[here, part], h_refs[m][...])
        dw_ref[here, 0 : 2 * wide] = g_sum.astype(bf16)
        dw_ref[here, 2 * wide : 3 * wide] = h_sum.astype(bf16)
        return 0

    lax.fori_loop(0, width // chunk, weight_step, 0)


def expert_grads(x_slots, gm_slots, lows_g, lows_h, part, parts):
    micro, slots = len(x_slots), len(x_slots[0])
    rows, width = x_slots[0][0].shape
    span = rows * slots
    wide = PAIR * LANES
    steps = lows_h[0].shape[1] // wide // parts
    first = part * steps
    fixed = pl.BlockSpec((rows, width), lambda i: (0, 0))
    moving = lambda height, cols: pl.BlockSpec((height, cols), lambda i: (0, first + i))
    flat = [block for part in x_slots for block in part] + [block for part in gm_slots for block in part]
    return pl.pallas_call(
        functools.partial(expert_grad_kernel, micro, slots),
        grid=(steps,),
        in_specs=[fixed] * len(flat) + [moving(span, 2 * wide)] * micro + [moving(span, wide)] * micro,
        out_specs=pl.BlockSpec((width, 3 * wide), lambda i: (0, i)),
        out_shape=shape((width, steps * 3 * wide), bf16),
        scratch_shapes=[pltpu.VMEM((width, micro * span), bf16), pltpu.VMEM((width, micro * span), bf16)],
        compiler_params=params(),
        cost_estimate=cost(12),
        name="expert_grads",
    )(*flat, *lows_g, *lows_h)


def moe_back_kernel(
    slots, info_ref, p0, p1, p2, gates_ref, router_ref, middle_ref, normed_ref, gain_ref, cot_ref, w_ref, *refs
):
    grad_middle_ref, grad_attn_ref, sums_ref = refs[:3]
    out_refs = refs[3:]
    rows, width = middle_ref.shape
    gate = lambda ref: ref[:, width : width + LANES].astype(f32)
    gates = gates_ref[...]
    gate_grads = gate(p0) + gate(p1) + gate(p2)
    grad_logits = gates * (gate_grads - jnp.sum(gates * gate_grads, axis=1, keepdims=True))
    grad_logits = grad_logits.astype(bf16)
    main = lambda ref: ref[:, 0:width].astype(f32)
    grad_moe = main(p0) + main(p1) + main(p2) + dot_nt(grad_logits, router_ref[...])
    middle, gain = middle_ref[...], gain_ref[...]
    inverse, unit, _ = normalised(middle, gain)
    weighted = grad_moe * gain
    inner = jnp.mean(weighted * middle, axis=-1, keepdims=True)
    grad_norm = inverse * weighted - middle * (inverse * inverse * inverse) * inner
    start = info_ref[0] * rows * slots + info_ref[1] * rows
    row_pos = start + lax.broadcasted_iota(jnp.int32, (rows, width), 0)
    grad_out = jnp.where(row_pos < info_ref[2], cot_ref[...].astype(f32), 0.0)
    grad_middle = grad_out + grad_norm
    grad_middle_ref[...] = grad_middle
    low = grad_middle.astype(bf16)
    grad_attn_ref[...] = low
    router_part = dot_nn(grad_logits.astype(f32).T.astype(bf16), normed_ref[...])
    gain_part = jnp.sum(grad_moe * unit, axis=0, keepdims=True)
    first = lax.broadcasted_iota(jnp.int32, (8, width), 0) == 0
    sums_ref[0:8, :] = jnp.where(first, jnp.broadcast_to(gain_part, (8, width)), 0.0)
    sums_ref[8:24, :] = router_part[0:16, :]
    grads = dot_nn(low, w_ref[...]).astype(bf16)
    cols = grads.shape[1] // slots
    for slot in range(slots):
        out_refs[slot][...] = grads[:, slot * cols : (slot + 1) * cols]


def moe_back(info, parts, gates, router, middle, normed, gain, cot, weight, slots):
    rows, width = middle.shape
    fixed = lambda value: pl.BlockSpec(value.shape, lambda i, info_ref: (0, 0))
    outs = [shape((rows, width), f32), shape((rows, width), bf16), shape((24, width), f32)]
    outs = outs + [shape((rows, weight.shape[1] // slots), bf16)] * slots
    operands = [*parts, gates, router, middle, normed, gain, cot, weight]
    return pl.pallas_call(
        functools.partial(moe_back_kernel, slots),
        grid_spec=pltpu.PrefetchScalarGridSpec(
            num_scalar_prefetch=1, grid=(1,), in_specs=[fixed(v) for v in operands], out_specs=[fixed(v) for v in outs]
        ),
        out_shape=outs,
        compiler_params=params(),
        cost_estimate=cost(3),
        name="moe_back",
    )(info, *operands)


def qkv_back_kernel(slots, dq_ref, dkv_ref, cos_ref, sin_ref, gain_ref, w_ref, *refs):
    x_refs, part_refs = refs[:slots], refs[slots : 2 * slots]
    grads_ref, normed_ref, sums_ref = refs[2 * slots :]
    rows = x_refs[0].shape[0]
    width = w_ref.shape[0]
    cols = dq_ref.shape[1]
    dk = dkv_ref[:, 0:LANES].astype(f32)
    turned = dk * cos_ref[...] - swap_halves(dk) * sin_ref[...]
    grads_ref[:, 0:cols] = dq_ref[...]
    grads_ref[:, cols : cols + LANES] = turned.astype(bf16)
    grads_ref[:, cols + LANES : cols + 2 * LANES] = dkv_ref[:, LANES : 2 * LANES].astype(bf16)
    total = jnp.zeros((1, width), f32)
    for slot in range(slots):
        here = slice(slot * rows, (slot + 1) * rows)
        _, unit, normed = normalised(x_refs[slot][...].astype(f32), gain_ref[...])
        normed_ref[here, :] = normed.astype(bf16)
        part = dot_nt(grads_ref[here, :], w_ref[...])
        part_refs[slot][...] = part.astype(bf16)
        total = total + jnp.sum(part * unit, axis=0, keepdims=True)
    first = lax.broadcasted_iota(jnp.int32, (8, width), 0) == 0
    sums_ref[...] = jnp.where(first, jnp.broadcast_to(total, (8, width)), 0.0)


def qkv_back(dq, dkv, cos_row, sin_row, gain, weight, x_slots):
    slots = len(x_slots)
    rows, width = x_slots[0].shape
    span = rows * slots
    return pl.pallas_call(
        functools.partial(qkv_back_kernel, slots),
        out_shape=[shape((rows, width), bf16)] * slots
        + [shape((span, weight.shape[1]), bf16), shape((span, width), bf16), shape((8, width), f32)],
        compiler_params=params(),
        cost_estimate=cost(4),
        name="qkv_back",
    )(dq, dkv, cos_row, sin_row, gain, weight, *x_slots)


def input_grad_kernel(micro, *refs):
    part_refs, middle_refs = refs[: 3 * micro], refs[3 * micro : 4 * micro]
    x_ref, gain_ref, out_ref = refs[4 * micro :]
    for m in range(micro):
        p0, p1, p2 = (ref[...].astype(f32) for ref in part_refs[3 * m : 3 * m + 3])
        grad_normed = p0 + p1 + p2
        x = x_ref[m].astype(f32)
        inverse, _, _ = normalised(x, gain_ref[...])
        weighted = grad_normed * gain_ref[...]
        inner = jnp.mean(weighted * x, axis=-1, keepdims=True)
        out_ref[m] = middle_refs[m][...] + inverse * weighted - x * (inverse * inverse * inverse) * inner


def close_input_grad(parts, grad_middles, x, gain):
    micro = x.shape[0]
    return pl.pallas_call(
        functools.partial(input_grad_kernel, micro),
        out_shape=shape(x.shape, f32),
        compiler_params=params(),
        cost_estimate=cost(2),
        name="input_grad",
    )(*[part for group in parts for part in group], *grad_middles, x, gain)


def outputs_kernel(micro, slots, info_ref, *refs):
    part_refs, middle_refs, out_ref = refs[: 3 * micro], refs[3 * micro : 4 * micro], refs[4 * micro]
    rows, width = middle_refs[0].shape
    start = info_ref[0] * rows * slots + info_ref[1] * rows
    row_pos = start + lax.broadcasted_iota(jnp.int32, (rows, width), 0)
    for m in range(micro):
        p0, p1, p2 = (ref[...].astype(f32) for ref in part_refs[3 * m : 3 * m + 3])
        total = middle_refs[m][...] + (p0 + p1 + p2)
        out_ref[m] = jnp.where(row_pos < info_ref[2 + m], total, 0.0).astype(bf16)


def close_outputs(info, parts, middles, slots):
    micro = len(middles)
    rows, width = middles[0].shape
    operands = [part for group in parts for part in group] + middles
    fixed = pl.BlockSpec((rows, width), lambda i, info_ref: (0, 0))
    return pl.pallas_call(
        functools.partial(outputs_kernel, micro, slots),
        grid_spec=pltpu.PrefetchScalarGridSpec(
            num_scalar_prefetch=1,
            grid=(1,),
            in_specs=[fixed] * len(operands),
            out_specs=pl.BlockSpec((micro, rows, width), lambda i, info_ref: (0, 0, 0)),
        ),
        out_shape=shape((micro, rows, width), bf16),
        compiler_params=params(),
        cost_estimate=cost(2),
        name="outputs",
    )(info, *operands)


def weights_kernel(first, info_ref, all_ref, small_ref, weight_ref, router_ref, gains_ref, table):
    blocks, rows, _ = all_ref.shape
    slots, few = small_ref.shape[1:3]
    for j in range(blocks):
        place = info_ref[0] ^ reversed_bits(j, blocks)
        weight_ref[pl.ds(pl.multiple_of(place * rows, rows), rows), :] = all_ref[j]
        for slot in range(slots):
            start = place * rows + (info_ref[1] ^ slot) * few
            table[pl.ds(pl.multiple_of(start, few), few), :] = small_ref[j, slot]
    router_ref[...] = table[...].astype(bf16)
    gains_ref[...] = table[...].T[first : first + 8, :]


def place_weights(info, weight_all, small_all, first):
    blocks, rows, cols = weight_all.shape
    whole = lambda dims: pl.BlockSpec(dims, lambda i, info_ref: (0,) * len(dims))
    outs = [shape((blocks * rows, cols), bf16), shape((blocks * rows, LANES), bf16), shape((8, blocks * rows), f32)]
    return pl.pallas_call(
        functools.partial(weights_kernel, first),
        grid_spec=pltpu.PrefetchScalarGridSpec(
            num_scalar_prefetch=1,
            grid=(1,),
            in_specs=[whole(weight_all.shape), whole(small_all.shape)],
            out_specs=[whole(out.shape) for out in outs],
            scratch_shapes=[pltpu.VMEM((blocks * rows, LANES), f32)],
        ),
        out_shape=outs,
        compiler_params=params(),
        cost_estimate=cost(3),
        name="place_weights",
    )(info, weight_all, small_all)


def output_weight_kernel(info_ref, all_ref, weight_ref):
    blocks, slots, rows, cols = all_ref.shape
    for j in range(blocks):
        place = info_ref[0] ^ reversed_bits(j, blocks)
        here = pl.ds(pl.multiple_of(place * rows, rows), rows)
        for slot in range(slots):
            weight_ref[here, slot * cols : (slot + 1) * cols] = all_ref[j, slot]


def place_output_weight(info, weight_all):
    blocks, slots, rows, cols = weight_all.shape
    out = shape((blocks * rows, slots * cols), bf16)
    return pl.pallas_call(
        output_weight_kernel,
        grid_spec=pltpu.PrefetchScalarGridSpec(
            num_scalar_prefetch=1,
            grid=(1,),
            in_specs=[pl.BlockSpec(weight_all.shape, lambda i, info_ref: (0, 0, 0, 0))],
            out_specs=pl.BlockSpec(out.shape, lambda i, info_ref: (0, 0)),
        ),
        out_shape=out,
        compiler_params=params(),
        cost_estimate=cost(3),
        name="place_output_weight",
    )(info, weight_all)


def weight_grad_kernel(micro, blocks, info_ref, *refs):
    left_refs, right_refs = refs[:micro], refs[micro : 2 * micro]
    keep_ref, send_ref = refs[2 * micro : 2 * micro + 2]
    flipped = refs[2 * micro + 2 :]
    half, high, _ = keep_ref.shape
    for m in range(micro):
        flipped[m][...] = left_refs[m][...].T

    for j in range(blocks):
        place = info_ref[0] ^ reversed_bits(j, blocks)
        here = pl.ds(pl.multiple_of(place * high, high), high)
        total = dot_nn(flipped[0][here, :], right_refs[0][...])
        for m in range(1, micro):
            total = total + dot_nn(flipped[m][here, :], right_refs[m][...])
        if j < half:
            keep_ref[j] = total.astype(bf16)
        else:
            send_ref[j - half] = total.astype(bf16)


def weight_grad(info, lefts, rights, blocks):
    micro, half = len(lefts), blocks // 2
    rows, width = lefts[0].shape
    cols = rights[0].shape[1]
    whole = lambda dims: pl.BlockSpec(dims, lambda j, info_ref: (0,) * len(dims))
    out = (half, width // blocks, cols)
    return pl.pallas_call(
        functools.partial(weight_grad_kernel, micro, blocks),
        grid_spec=pltpu.PrefetchScalarGridSpec(
            num_scalar_prefetch=1,
            grid=(1,),
            in_specs=[whole(value.shape) for value in [*lefts, *rights]],
            out_specs=[whole(out)] * 2,
            scratch_shapes=[pltpu.VMEM((width, rows), bf16)] * micro,
        ),
        out_shape=[shape(out, bf16)] * 2,
        compiler_params=params(),
        cost_estimate=cost(4),
        name="weight_grad",
    )(info, *lefts, *rights)


def unpack_kernel(half, low_ref, high_ref, gate_ref, up_ref, down_ref):
    i = pl.program_id(0)

    def place(ref):
        for member in range(PAIR):
            cut = lambda kind: ref[:, (kind * PAIR + member) * LANES : (kind * PAIR + member + 1) * LANES].astype(f32)
            gate_ref[member] = cut(0)
            up_ref[member] = cut(1)
            down_ref[member] = cut(2).T

    @pl.when(i < half)
    def _():
        place(low_ref)

    @pl.when(i >= half)
    def _():
        place(high_ref)


def unpack_experts(halves):
    rows, cols = halves[0].shape
    part = 3 * PAIR * LANES
    half = cols // part
    experts = 2 * half * PAIR
    return pl.pallas_call(
        functools.partial(unpack_kernel, half),
        grid=(2 * half,),
        in_specs=[
            pl.BlockSpec((rows, part), lambda i: (0, jnp.minimum(i, half - 1))),
            pl.BlockSpec((rows, part), lambda i: (0, jnp.maximum(i - half, 0))),
        ],
        out_specs=[
            pl.BlockSpec((PAIR, rows, LANES), lambda i: (i, 0, 0)),
            pl.BlockSpec((PAIR, rows, LANES), lambda i: (i, 0, 0)),
            pl.BlockSpec((PAIR, LANES, rows), lambda i: (i, 0, 0)),
        ],
        out_shape=[
            shape((experts, rows, LANES), f32),
            shape((experts, rows, LANES), f32),
            shape((experts, LANES, rows), f32),
        ],
        compiler_params=params(),
        cost_estimate=cost(3),
        name="unpack",
    )(*halves)


def exchange(values, axis, bit):
    count = lax.axis_size(axis)
    return lax.ppermute(values, axis, [(i, i ^ bit) for i in range(count)])


def gather_slots(values, axis):
    count = lax.axis_size(axis)
    slots = {0: values}
    bit = count // 2
    while bit:
        for slot in sorted(slots):
            slots[slot | bit] = exchange(slots[slot], axis, bit)
        bit //= 2
    return [slots[slot] for slot in range(count)]


class Moves:
    def __init__(self):
        self.inputs, self.outputs, self.steps = [], [], []

    def take(self, value):
        self.inputs.append(value)
        return ("in", len(self.inputs) - 1)

    def make(self, dims, kind):
        self.outputs.append(shape(dims, kind))
        return ("out", len(self.outputs) - 1)

    def copy(self, source, target, place, needs, size):
        ready = max([self.steps[need][5] for need in needs], default=0.0)
        rate = 45e3 if place and place[1] != 1 or place and place[0] == "tp" else 150e3
        finish = ready + 1.0 + size / rate
        self.steps.append((source, target, place, needs, ready, finish))
        return len(self.steps) - 1

    def gather_tp(self, value, pieces=2):
        count = lax.axis_size("tp")
        rows, size = value.shape[0] // pieces, value.size * 2 // pieces
        arrays = [self.take(value)] + [self.make(value.shape, value.dtype) for _ in range(count - 1)]
        for piece in range(pieces):
            index = (pl.ds(piece * rows, rows),)
            came, bit = {0: []}, count // 2
            while bit:
                for slot in sorted(came):
                    step = self.copy(
                        (arrays[slot], index), (arrays[slot | bit], index), ("tp", bit), came[slot], size * (1 + bit // 2)
                    )
                    came[slot | bit] = [step]
                bit //= 2
        return arrays[1:]

    def trade_tp(self, blocks):
        made = []
        for slot in range(1, len(blocks)):
            made.append(self.make(blocks[slot].shape, blocks[slot].dtype))
            self.copy((self.take(blocks[slot]), ()), (made[-1], ()), ("tp", slot), [], blocks[slot].size * 4)
        return made

    def spread(self, source, target, rows, size, pieces, needs):
        count = lax.axis_size("fsdp")
        bits = []
        while count >> (len(bits) + 1):
            bits.append(count >> (len(bits) + 1))
        upper = bits[:-1]
        turned = upper[len(upper) // 2 :] + upper[: len(upper) // 2]
        orders = [upper + [1], turned + [1]]
        for piece in range(pieces):
            inner = (pl.ds(piece * (rows // pieces), rows // pieces),) if pieces > 1 else ()
            came = {0: list(needs)}
            for bit in orders[piece % 2]:
                for slot in sorted(came):
                    origin = source(inner) if slot == 0 else (target, (reversed_bits(slot, count),) + inner)
                    goal = (target, (reversed_bits(slot | bit, count),) + inner)
                    came[slot | bit] = [self.copy(origin, goal, ("fsdp", bit), came[slot], size // pieces)]

    def gather_fsdp(self, value, pieces=2):
        count = lax.axis_size("fsdp")
        held, target = self.take(value), self.make((count,) + value.shape, value.dtype)
        self.spread(lambda inner: (held, inner), target, value.shape[0], value.size * 2, pieces, [])
        self.copy((held, ()), (target, (0,)), None, [], value.size)
        return target

    def gather_both(self, value):
        count, slots = lax.axis_size("fsdp"), lax.axis_size("tp")
        held, target = self.take(value), self.make((count, slots) + value.shape, value.dtype)
        needs = [self.copy((held, ()), (target, (0, 0)), None, [], value.size)]
        for slot in range(1, slots):
            needs.append(self.copy((held, ()), (target, (0, slot)), ("tp", slot), [], value.size * 2))
        self.spread(lambda inner: (target, (0,) + inner), target, slots, value.size * 2 * slots, 1, needs)
        return target

    def kernel(self, *refs):
        ins, outs = refs[: len(self.inputs)], refs[len(self.inputs) : len(self.inputs) + len(self.outputs)]
        send, recv = refs[-2:]
        ranks = {axis: lax.axis_index(axis) for axis in ("fsdp", "tp")}
        partner = lambda place: {place[0]: ranks[place[0]] ^ place[1]}
        barrier = pltpu.get_barrier_semaphore()
        places = sorted({step[2] for step in self.steps if step[2]})
        for place in places:
            pl.semaphore_signal(barrier, inc=1, device_id=partner(place), device_id_type=pl.DeviceIdType.MESH)
        pl.semaphore_wait(barrier, len(places))

        def view(spot):
            (kind, number), index = spot
            ref = (ins if kind == "in" else outs)[number]
            return ref.at[index] if index else ref

        started, arrived = {}, set()

        def arrive(number):
            if number not in arrived:
                arrived.add(number)
                copy, place = started[number]
                if place:
                    copy.wait_recv()
                else:
                    copy.wait()

        for number in sorted(range(len(self.steps)), key=lambda i: self.steps[i][4]):
            source, target, place, needs, _, _ = self.steps[number]
            for need in needs:
                arrive(need)
            if place:
                copy = pltpu.make_async_remote_copy(
                    src_ref=view(source),
                    dst_ref=view(target),
                    send_sem=send.at[number],
                    recv_sem=recv.at[number],
                    device_id=partner(place),
                    device_id_type=pl.DeviceIdType.MESH,
                )
            else:
                copy = pltpu.make_async_copy(view(source), view(target), send.at[number])
            copy.start()
            started[number] = (copy, place)
        for number in sorted(range(len(self.steps)), key=lambda i: self.steps[i][5]):
            arrive(number)
            if self.steps[number][2]:
                started[number][0].wait_send()

    def run(self, number, time, name):
        count = len(self.steps)
        anywhere = pl.BlockSpec(memory_space=pl.ANY)
        made = pl.pallas_call(
            self.kernel,
            out_shape=self.outputs,
            in_specs=[anywhere] * len(self.inputs),
            out_specs=[anywhere] * len(self.outputs),
            scratch_shapes=[pltpu.SemaphoreType.DMA((count,)), pltpu.SemaphoreType.DMA((count,))],
            compiler_params=pltpu.CompilerParams(collective_id=number, has_side_effects=True),
            cost_estimate=cost(time),
            name=name,
        )(*self.inputs)
        self.made = list(made)

    def get(self, spot):
        return [self.made[part[1]] for part in spot] if isinstance(spot, list) else self.made[spot[1]]


def trade_slots(blocks, axis):
    return [blocks[0]] + [exchange(blocks[slot], axis, slot) for slot in range(1, len(blocks))]


def scatter_slots(blocks):
    if len(blocks) == 2:
        return [blocks[0], exchange(blocks[1], "tp", 1), jnp.zeros_like(blocks[0])]
    met = exchange(blocks[3], "tp", 1)
    near = exchange(blocks[1], "tp", 1)
    joined = (blocks[2].astype(f32) + met.astype(f32)).astype(bf16)
    return [blocks[0], near, exchange(joined, "tp", 2)]


def scatter_spans(keep, send):
    bit = 1
    while True:
        came = exchange(send, "fsdp", bit)
        half = keep.shape[0] // 2
        if half == 0:
            return keep[0].astype(f32) + came[0].astype(f32)
        send = (keep[half:].astype(f32) + came[half:].astype(f32)).astype(bf16)
        keep = (keep[:half].astype(f32) + came[:half].astype(f32)).astype(bf16)
        bit *= 2


def scatter_columns(values):
    for axis in ("fsdp", "tp"):
        rank = lax.axis_index(axis)
        bit = lax.axis_size(axis) // 2
        while bit:
            half = values.shape[1] // 2
            upper = (rank // bit) % 2 == 1
            low, high = values[:, :half], values[:, half:]
            came = exchange(jnp.where(upper, low, high), axis, bit)
            values = jnp.where(upper, high, low) + came
            bit //= 2
    return values


def after(value, *others):
    return lax.optimization_barrier((value, *others))[0]


def local(
    inputs,
    cotangent,
    lengths,
    routes,
    attn_gain,
    moe_gain,
    router_weight,
    query_weight,
    key_weight,
    value_weight,
    output_weight,
    gate_weight,
    up_weight,
    down_weight,
):
    tensor_count = lax.axis_size("tp")
    tensor_rank = lax.axis_index("tp")
    shard_rank = lax.axis_index("fsdp")
    micro, rows, width = inputs.shape
    span = rows * tensor_count
    experts, shard_width, hidden = gate_weight.shape
    steps = range(micro)
    slots, blocks = tensor_count, lax.axis_size("fsdp")
    slot_ranks = [tensor_rank ^ slot for slot in range(slots)]
    odd, upper = tensor_rank % 2 == 1, tensor_rank // 2 % 2 == 1
    info_all = jnp.concatenate([jnp.stack([shard_rank, tensor_rank]).astype(jnp.int32), lengths])
    infos = [jnp.stack([info_all[0], info_all[1], info_all[2 + m]]) for m in steps]

    small = jnp.concatenate([router_weight, attn_gain[:, None], moe_gain[:, None]], axis=1).astype(f32)
    small = jnp.pad(small, ((0, 0), (0, LANES - small.shape[1])))
    qkv_local = jnp.concatenate([query_weight, key_weight, value_weight], axis=1)
    qkv_cols = qkv_local.shape[1]

    stacked = jnp.stack(
        [gate_weight.transpose(1, 0, 2), up_weight.transpose(1, 0, 2), down_weight.transpose(2, 0, 1)], axis=1
    )
    expert_local = (
        stacked.reshape(shard_width, 3, experts // PAIR, PAIR, hidden)
        .transpose(0, 2, 1, 3, 4)
        .reshape(shard_width, 3 * experts * hidden)
    )
    expert_full = lax.all_gather(expert_local, "fsdp", axis=0, tiled=True)

    row_place = jnp.arange(rows, dtype=jnp.int32)
    span_pos = jnp.concatenate([shard_rank * span + rank * rows + row_place for rank in slot_ranks])
    cos_row, sin_row = rope_tables(span_pos)
    row_pos = shard_rank * span + tensor_rank * rows + row_place
    valid = row_pos[None, :] < lengths[:, None]
    own_grads = jnp.where(valid[:, :, None], cotangent, jnp.zeros_like(cotangent))

    x_slots, queries, kvs, kv_alls, gm_slots = [], [], [], [], []
    for m in range(micro + 1):
        moves = Moves()
        wanted = {}
        if m < micro:
            wanted["x"] = moves.gather_tp(after(inputs[m], kvs[-1]) if m else inputs[m])
        if m:
            wanted["kv"] = moves.gather_fsdp(kvs[m - 1])
        if m == 0:
            wanted["weights"] = moves.gather_fsdp(qkv_local)
            wanted["small"] = moves.gather_both(small)
        if m == micro:
            wanted["gm"] = moves.gather_tp(own_grads[0])
            wanted["out"] = moves.gather_both(output_weight.T)
        moves.run(m, 25, "open")
        if m == 0:
            qkv_full, router_full, gains = place_weights(
                info_all, moves.get(wanted["weights"]), moves.get(wanted["small"]), experts
            )
            gain_attn, gain_moe = gains[0:1], gains[1:2]
        if m:
            kv_alls.append(moves.get(wanted["kv"]))
        if m < micro:
            x_slots.append([inputs[m]] + moves.get(wanted["x"]))
            query, kv = project_qkv(x_slots[m], gain_attn, qkv_full, cos_row, sin_row)
            queries.append(query)
            kvs.append(kv)
        else:
            gm_slots.append([own_grads[0]] + moves.get(wanted["gm"]))
            out_all = moves.get(wanted["out"])
    for m in range(1, micro):
        gm_slots.append(gather_slots(after(own_grads[m], gm_slots[m - 1][-1]), "tp"))

    order = kv_alls[-1]
    attended, logs, att_owns, middles, normeds, moe_slots = [], [], [], [], [], []
    for m in steps:
        *att_slots, log_total = attend(after(infos[m], order), queries[m], kv_alls[m], rows)
        if m == 0:
            out_full = place_output_weight(after(info_all, log_total), out_all)
        moves = Moves()
        traded = moves.trade_tp(att_slots)
        moves.run(micro + 1 + m, 8, "trade")
        att_own, middle, normed = close_attention(
            inputs[m], gain_moe, out_full, [att_slots[0]] + moves.get(traded)
        )
        order = middle
        attended.append(att_slots)
        logs.append(log_total)
        att_owns.append(att_own)
        middles.append(middle)
        normeds.append(normed)
        moe_slots.append(gather_slots(normed, "tp"))

    expert_outs, gin_parts = [], []
    for m in steps:
        results = experts_both(
            after(infos[m], order), routes[m], router_full, expert_full, moe_slots[m], gm_slots[m]
        )
        expert_outs.append(results)
        gin_parts.append(scatter_slots(results[:slots]))
        order = results[2 * slots]
    lows_g = [results[2 * slots + 1] for results in expert_outs]
    lows_h = [results[2 * slots + 2] for results in expert_outs]

    sums = 0.0
    grad_middles, grad_attns, grad_slots = [], [], []
    expert_sums = []
    pieces = 2
    for m in range(max(pieces, micro)):
        if m < pieces:
            some_grad = expert_grads(
                [[after(moe_slots[0][0], order)] + moe_slots[0][1:]] + moe_slots[1:], gm_slots, lows_g, lows_h, m, pieces
            )
            expert_sums.append(lax.psum_scatter(some_grad, "fsdp", scatter_dimension=0, tiled=True))
            order = some_grad
        if m < micro:
            grad_middle, grad_attn, sums_moe, *grads = moe_back(
                after(infos[m], order),
                gin_parts[m],
                expert_outs[m][2 * slots],
                router_full,
                middles[m],
                normeds[m],
                gain_moe,
                cotangent[m],
                out_full,
                slots,
            )
            order = sums_moe
            sums = sums + sums_moe
            grad_middles.append(grad_middle)
            grad_attns.append(grad_attn)
            grad_slots.append(trade_slots(grads, "tp"))
    out_keep, out_send = weight_grad(after(info_all, order), grad_attns, att_owns, blocks)
    order = out_keep

    dqs, dkvs, mixed_parts = [], [], []
    for m in steps:
        dq, keep, send = attend_back(
            after(infos[m], order), queries[m], kv_alls[m], logs[m], cos_row, sin_row, attended[m], grad_slots[m]
        )
        mixed_parts.append(scatter_slots([after(part, order) for part in expert_outs[m][slots : 2 * slots]]))
        order = dq
        dqs.append(dq)
        dkvs.append(scatter_spans(keep, send))

    normed_all, qkv_grads, normed_parts = [], [], []
    for m in steps:
        *parts, grads, normed_attn, sums_attn = qkv_back(
            dqs[m], dkvs[m], cos_row, sin_row, after(gain_attn, order), qkv_full, x_slots[m]
        )
        order = sums_attn
        sums = sums + jnp.pad(sums_attn[0:1], ((1, 22), (0, 0)))
        normed_all.append(normed_attn)
        qkv_grads.append(grads)
        normed_parts.append(scatter_slots(parts))
    qkv_keep, qkv_send = weight_grad(after(info_all, order), normed_all, qkv_grads, blocks)
    qkv_sum = scatter_spans(qkv_keep, qkv_send)
    small_sum = scatter_columns(sums)
    out_sum = scatter_spans(out_keep, out_send).astype(bf16)
    head_cols = output_weight.shape[0]
    out_parts = [out_sum[:, slot * head_cols : (slot + 1) * head_cols] for slot in range(slots)]
    out_final = sum(part.astype(f32) for part in scatter_slots(out_parts))
    outputs = close_outputs(after(info_all, qkv_keep), mixed_parts, middles, slots)
    expert_sums[0] = after(expert_sums[0], outputs)
    gate_sum, up_sum, down_sum = unpack_experts(expert_sums)
    input_grad = close_input_grad(normed_parts, grad_middles, inputs, after(gain_attn, gate_sum))
    q_cols, k_cols = query_weight.shape[1], key_weight.shape[1]
    return (
        outputs,
        input_grad,
        small_sum[1],
        small_sum[0],
        small_sum[8 : 8 + experts].T,
        qkv_sum[:, :q_cols],
        qkv_sum[:, q_cols : q_cols + k_cols],
        qkv_sum[:, q_cols + k_cols : qkv_cols],
        out_final.T,
        gate_sum,
        up_sum,
        down_sum,
    )


def solution(mesh):
    rows_spec = P(None, ("fsdp", "tp"), None)
    small_specs = (P(("fsdp", "tp")), P(("fsdp", "tp")), P(("fsdp", "tp"), None))
    weight_specs = (
        P("fsdp", "tp"),
        P("fsdp", "tp"),
        P("fsdp", "tp"),
        P("tp", "fsdp"),
        P(None, "fsdp", "tp"),
        P(None, "fsdp", "tp"),
        P(None, "tp", "fsdp"),
    )
    in_specs = (rows_spec, rows_spec, P(), P(None, "fsdp", None)) + small_specs + weight_specs
    out_specs = (rows_spec, rows_spec) + small_specs + weight_specs
    return jax.shard_map(local, mesh=mesh, in_specs=in_specs, out_specs=out_specs, check_vma=False)
```

profile of v0, /device:TPU:0, one launch (start us, length us, event | category | flops | bytes accessed | tf_op | source)
XLA Modules:
  0.0 583.8 jit_solution(6800206841847254642)
XLA Ops:
  21.9 36.8 %open.3 = (bf16[128,1024]{1,0:T(8,128)(2,1)}, bf16[128,1024]{1,0:T(8,128)(2,1)}, bf16[128,1024]{1,0:T(8,128)(2,1)}, bf16[8,128,512]{2,1,0:T(8,128)(2,1)}, f32[8,4,32,128]{3,2,1,0:T(8,128)}) custom-call(bf16[128,1024]{1,0:T(8,128)(2,1)} %get-tuple-element.317.refs_0_.x_ref, bf16[128,512]{1,0:T(8,128)(2,1)} %pad_maximum_fusion.2.refs_1_, f32[32,128]{1,0:T(8,128)} %fusion.7.refs_2_), custom_call_target="tpu_custom_call" | custom-call | flops 22499999744 | bytes 1024 | tf_op jit(solution)/shard_map/open/pallas_call | solution.py:966
  58.7 3.3 place_weights.1
  63.4 3.6 project_qkv.2
  70.5 25.7 %open.4 = (bf16[128,1024]{1,0:T(8,128)(2,1)}, bf16[128,1024]{1,0:T(8,128)(2,1)}, bf16[128,1024]{1,0:T(8,128)(2,1)}, bf16[8,512,256]{2,1,0:T(8,128)(2,1)}) custom-call(bf16[128,1024]{1,0:T(8,128)(2,1)} %get-tuple-element.154.refs_0_.x_ref, bf16[512,256]{1,0:T(8,128)(2,1)} %get-tuple-element.153.refs_1_), custom_call_target="tpu_custom_call" | custom-call | flops 22499999744 | bytes 1024 | tf_op jit(solution)/shard_map/open/pallas_call | solution.py:966
  96.2 3.4 project_qkv.3
  99.7 39.7 %open.5 = (bf16[8,512,256]{2,1,0:T(8,128)(2,1)}, bf16[128,1024]{1,0:T(8,128)(2,1)}, bf16[128,1024]{1,0:T(8,128)(2,1)}, bf16[128,1024]{1,0:T(8,128)(2,1)}, bf16[8,4,128,256]{3,2,1,0:T(8,128)(2,1)}) custom-call(bf16[512,256]{1,0:T(8,128)(2,1)} %get-tuple-element.158.refs_0_, bf16[128,1024]{1,0:T(8,128)(2,1)} %get-tuple-element.315.refs_1_.refs_4_.refs_8_, ...), custom_call_target="tpu_custom_call" | custom-call | flops 22499999744 | bytes 1024 | tf_op jit(solution)/shard_map/open/pallas_call | solution.py:966
  139.4 9.2 %attend.2 = (bf16[128,256]{1,0:T(8,128)(2,1)}, bf16[128,256]{1,0:T(8,128)(2,1)}, bf16[128,256]{1,0:T(8,128)(2,1)}, bf16[128,256]{1,0:T(8,128)(2,1)}, f32[8,512]{1,0:T(8,128)}) custom-call(s32[3]{0:T(128)} %pad_add_fusion.4.info_ref, bf16[512,256]{1,0:T(8,128)(2,1)} %get-tuple-element.161.q_ref, bf16[8,512,256]{2,1,0:T(8,128)(2,1)} %get-tuple-element.162.kv_ref), custom_call_target="tpu_custom_call" | custom-call | flops 10800000000 | bytes 1024 | tf_op jit(solution)/shard_map/attend/pallas_call | solution.py:208
  148.6 3.8 place_output_weight.1.w_ref
  152.4 8.3 %trade.2 = (bf16[128,256]{1,0:T(8,128)(2,1)}, bf16[128,256]{1,0:T(8,128)(2,1)}, bf16[128,256]{1,0:T(8,128)(2,1)}) custom-call(bf16[128,256]{1,0:T(8,128)(2,1)} %get-tuple-element.167.refs_0_.refs_1_, bf16[128,256]{1,0:T(8,128)(2,1)} %get-tuple-element.168.refs_1_.refs_2_, bf16[128,256]{1,0:T(8,128)(2,1)} %get-tuple-element.169.refs_2_.refs_3_), custom_call_target="tpu_custom_call" | custom-call | flops 7200000000 | bytes 1024 | tf_op jit(solution)/shard_map/trade/pallas_call | solution.py:966
  160.7 3.5 middle.2
  167.9 9.4 %attend.3 = (bf16[128,256]{1,0:T(8,128)(2,1)}, bf16[128,256]{1,0:T(8,128)(2,1)}, bf16[128,256]{1,0:T(8,128)(2,1)}, bf16[128,256]{1,0:T(8,128)(2,1)}, f32[8,512]{1,0:T(8,128)}) custom-call(s32[3]{0:T(128)} %pad_add_fusion.2.info_ref, bf16[512,256]{1,0:T(8,128)(2,1)} %get-tuple-element.176.q_ref, bf16[8,512,256]{2,1,0:T(8,128)(2,1)} %get-tuple-element.159.kv_ref), custom_call_target="tpu_custom_call" | custom-call | flops 10800000000 | bytes 1024 | tf_op jit(solution)/shard_map/attend/pallas_call | solution.py:208
  177.3 8.1 %trade.3 = (bf16[128,256]{1,0:T(8,128)(2,1)}, bf16[128,256]{1,0:T(8,128)(2,1)}, bf16[128,256]{1,0:T(8,128)(2,1)}) custom-call(bf16[128,256]{1,0:T(8,128)(2,1)} %get-tuple-element.178.refs_0_.refs_1_, bf16[128,256]{1,0:T(8,128)(2,1)} %get-tuple-element.179.refs_1_.refs_2_, bf16[128,256]{1,0:T(8,128)(2,1)} %get-tuple-element.180.refs_2_.refs_3_), custom_call_target="tpu_custom_call" | custom-call | flops 7200000000 | bytes 1024 | tf_op jit(solution)/shard_map/trade/pallas_call | solution.py:966
  185.3 3.5 middle.3
  195.6 13.9 %collective-permute-done.4.refs_2_.refs_6_ = bf16[128,1024]{1,0:T(8,128)(2,1)S(1)} collective-permute-done((bf16[128,1024]{1,0:T(8,128)(2,1)}, bf16[128,1024]{1,0:T(8,128)(2,1)S(1)}, u32[]{:S(2)}, u32[]{:S(2)}) %collective-permute-start.4) | collective-permute-done | bytes 262176 | tf_op jit(solution)/shard_map/ppermute | solution.py:825
  209.5 5.6 collective-permute-done.7.refs_6_.refs_14_
  215.9 24.9 %experts.2 = (bf16[128,1152]{1,0:T(8,128)(2,1)}, bf16[128,1152]{1,0:T(8,128)(2,1)}, bf16[128,1152]{1,0:T(8,128)(2,1)}, bf16[128,1152]{1,0:T(8,128)(2,1)}, bf16[1...) custom-call(s32[3]{0:T(128)} %pad_add_fusion.4.info_ref, ...), custom_call_target="tpu_custom_call" | custom-call | flops 21600000000 | bytes 1024 | tf_op jit(solution)/shard_map/experts/pallas_call | solution.py:447
  241.9 24.9 %experts.3 = (bf16[128,1152]{1,0:T(8,128)(2,1)}, bf16[128,1152]{1,0:T(8,128)(2,1)}, bf16[128,1152]{1,0:T(8,128)(2,1)}, bf16[128,1152]{1,0:T(8,128)(2,1)}, bf16[1...) custom-call(s32[3]{0:T(128)} %pad_add_fusion.2.info_ref, ...), custom_call_target="tpu_custom_call" | custom-call | flops 21600000000 | bytes 1024 | tf_op jit(solution)/shard_map/experts/pallas_call | solution.py:447
  266.8 15.0 %expert_grads.2 = bf16[1024,3072]{1,0:T(8,128)(2,1)} custom-call(bf16[128,1024]{1,0:T(8,128)(2,1)} %get-tuple-element.206.refs_0_.normed_ref, bf16[128,1024]{1,0:T(8,128)(2,1)} %copy-done.38, bf16[128,1024]{1,0:T(8,128)(2,1)} %copy-done.37, bf16[128,1024]{1,0:T(8,128)(2,1)} %copy-done.42, bf16[128,1024]{1,0:T(8,128)(2,1)} %get-tuple-element.192.refs_0_.refs_4_.normed_ref, ...), custom_call_target="tpu_custom_call" | custom-call | flops 10800000000 | bytes 1024 | tf_op jit(solution)/shard_map/expert_grads/pallas_call | solution.py:515
  287.8 4.8 collective-permute-done.10
  295.3 10.0 %collective-permute-done.13 = bf16[128,1152]{1,0:T(8,128)(2,1)S(1)} collective-permute-done((bf16[128,1152]{1,0:T(8,128)(2,1)S(1)}, bf16[128,1152]{1,0:T(8,128)(2,1)S(1)}, u32[]{:S(2)}, u32[]{:S(2)}) %collective-permute-start.13) | collective-permute-done | bytes 294944 | tf_op jit(solution)/shard_map/ppermute | solution.py:825
  305.6 11.3 %collective-permute-done.9.p1 = bf16[128,1152]{1,0:T(8,128)(2,1)S(1)} collective-permute-done((bf16[128,1152]{1,0:T(8,128)(2,1)S(1)}, bf16[128,1152]{1,0:T(8,128)(2,1)S(1)}, u32[]{:S(2)}, u32[]{:S(2)}) %collective-permute-start.9) | collective-permute-done | bytes 294944 | tf_op jit(solution)/shard_map/ppermute | solution.py:825
  318.2 5.2 moe_back.2
  323.4 15.0 %expert_grads.3 = bf16[1024,3072]{1,0:T(8,128)(2,1)} custom-call(bf16[128,1024]{1,0:T(8,128)(2,1)} %get-tuple-element.206.refs_0_.normed_ref, bf16[128,1024]{1,0:T(8,128)(2,1)} %copy-done.38, bf16[128,1024]{1,0:T(8,128)(2,1)} %copy-done.37, bf16[128,1024]{1,0:T(8,128)(2,1)} %copy-done.42, bf16[128,1024]{1,0:T(8,128)(2,1)} %get-tuple-element.192.refs_0_.refs_4_.normed_ref, ...), custom_call_target="tpu_custom_call" | custom-call | flops 10800000000 | bytes 1024 | tf_op jit(solution)/shard_map/expert_grads/pallas_call | solution.py:515
  339.3 4.8 moe_back.3
  344.1 2.9 collective-permute-start.15
  349.4 4.4 weight_grad.2
  359.8 11.6 %attend_back.2 = (bf16[512,256]{1,0:T(8,128)(2,1)}, bf16[4,512,256]{2,1,0:T(8,128)(2,1)}, bf16[4,512,256]{2,1,0:T(8,128)(2,1)}) custom-call(s32[3]{0:T(128)} %pad_add_fusion.4.info_ref, bf16[512,256]{1,0:T(8,128)(2,1)} %get-tuple-element.161.q_ref, bf16[8,512,256]{2,1,0:T(8,128)(2,1)} %get-tuple-element.162.kv_ref, f32[8,512]{1,0:T(8,128)} %get-tuple-element.163.log_ref, ...), custom_call_target="tpu_custom_call" | custom-call | flops 16199999488 | bytes 1024 | tf_op jit(solution)/shard_map/attend_back/pallas_call | solution.py:311
  374.5 12.1 %attend_back.3 = (bf16[512,256]{1,0:T(8,128)(2,1)}, bf16[4,512,256]{2,1,0:T(8,128)(2,1)}, bf16[4,512,256]{2,1,0:T(8,128)(2,1)}) custom-call(s32[3]{0:T(128)} %pad_add_fusion.2.info_ref, bf16[512,256]{1,0:T(8,128)(2,1)} %get-tuple-element.176.q_ref, bf16[8,512,256]{2,1,0:T(8,128)(2,1)} %get-tuple-element.159.kv_ref, f32[8,512]{1,0:T(8,128)} %get-tuple-element.226.log_ref, ...), custom_call_target="tpu_custom_call" | custom-call | flops 16199999488 | bytes 1024 | tf_op jit(solution)/shard_map/attend_back/pallas_call | solution.py:311
  394.8 21.0 %collective-permute-start.48 = (bf16[2,128,1024]{2,1,0:T(8,128)(2,1)S(1)}, bf16[2,128,1024]{2,1,0:T(8,128)(2,1)S(1)}, u32[]{:S(2)}, u32[]{:S(2)}) collective-permute-start(bf16[2,128,1024]{2,1,0:T(8,128)(2,1)S(1)} %get-tuple-element.305), channel_id=1, source_target_pairs={{0,8},{4,12},{8,0},{12,4},{16,24},{20,28},{24,16},{28,20},{1,9},{5... | collective-permute-start | bytes 1572872 | tf_op jit(solution)/shard_map/ppermute | solution.py:825
  418.8 6.6 %collective-permute-start.22 = (bf16[2,512,256]{2,1,0:T(8,128)(2,1)S(1)}, bf16[2,512,256]{2,1,0:T(8,128)(2,1)S(1)}, u32[]{:S(2)}, u32[]{:S(2)}) collective-permute-start(bf16[2,512,256]{2,1,0:T(8,128)(2,1)S(1)} %get-tuple-element.309), channel_id=1, source_target_pairs={{0,8},{4,12},{8,0},{12,4},{16,24},{20,28},{24,16},{28,20},{1,9},{5... | collective-permute-start | bytes 1572872 | tf_op jit(solution)/shard_map/ppermute | solution.py:825
  425.6 8.1 %collective-permute-done.48 = bf16[2,128,1024]{2,1,0:T(8,128)(2,1)S(1)} collective-permute-done((bf16[2,128,1024]{2,1,0:T(8,128)(2,1)S(1)}, bf16[2,128,1024]{2,1,0:T(8,128)(2,1)S(1)}, u32[]{:S(2)}, u32[]{:S(2)}) %collective-permute-start.48) | collective-permute-done | bytes 524320 | tf_op jit(solution)/shard_map/ppermute | solution.py:825
  436.2 15.6 %collective-permute-done.25 = bf16[2,512,256]{2,1,0:T(8,128)(2,1)S(1)} collective-permute-done((bf16[2,512,256]{2,1,0:T(8,128)(2,1)S(1)}, bf16[2,512,256]{2,1,0:T(8,128)(2,1)S(1)}, u32[]{:S(2)}, u32[]{:S(2)}) %collective-permute-start.25) | collective-permute-done | bytes 524320 | tf_op jit(solution)/shard_map/ppermute | solution.py:825
  451.7 22.2 %collective-permute-start.49 = (bf16[1,128,1024]{2,1,0:T(8,128)(2,1)S(1)}, bf16[1,128,1024]{2,1,0:T(8,128)(2,1)S(1)}, u32[]{:S(2)}, u32[]{:S(2)}) collective-permute-start(bf16[1,128,1024]{2,1,0:T(8,128)(2,1)S(1)} %add_convert_fusion.9), channel_id=1, source_target_pairs={{0,16},{4,20},{8,24},{12,28},{16,0},{20,4},{24,8},{28,12},{1,17},{... | collective-permute-start | bytes 786440 | tf_op jit(solution)/shard_map/ppermute | solution.py:825
  474.0 9.8 %collective-permute-start.26 = (bf16[1,512,256]{2,1,0:T(8,128)(2,1)S(1)}, bf16[1,512,256]{2,1,0:T(8,128)(2,1)S(1)}, u32[]{:S(2)}, u32[]{:S(2)}) collective-permute-start(bf16[1,512,256]{2,1,0:T(8,128)(2,1)S(1)} %add_convert_fusion.17), channel_id=1, source_target_pairs={{0,16},{4,20},{8,24},{12,28},{16,0},{20,4},{24,8},{28,12},{1,17},{... | collective-permute-start | bytes 786440 | tf_op jit(solution)/shard_map/ppermute | solution.py:825
  485.1 4.0 collective-permute-done.26
  491.7 4.6 qkv_back.2
  498.0 4.6 qkv_back.3
  503.7 3.8 collective-permute-done.39
  509.1 5.1 weight_grad.3
  514.8 3.7 collective-permute-done.51
  525.5 3.4 outputs.1
  530.2 3.0 collective-permute-start.34
  536.2 8.8 %collective-permute-done.43 = f32[24,32]{1,0:T(8,128)S(1)} collective-permute-done((f32[24,32]{1,0:T(8,128)S(1)}, f32[24,32]{1,0:T(8,128)S(1)}, u32[]{:S(2)}, u32[]{:S(2)}) %collective-permute-start.43) | collective-permute-done | bytes 3104 | tf_op jit(solution)/shard_map/ppermute | solution.py:825
  549.6 4.5 collective-permute-done.45
  555.5 3.6 collective-permute-done.46
  560.5 6.2 %unpack.1 = (f32[16,128,128]{2,1,0:T(8,128)}, f32[16,128,128]{2,1,0:T(8,128)}, f32[16,128,128]{2,1,0:T(8,128)}) custom-call(bf16[128,3072]{1,0:T(8,128)(2,1)} %reduce-scatter.3.cloned.1.call-done.low_ref, bf16[128,3072]{1,0:T(8,128)(2,1)} %reduce-scatter.5.cloned.1.call-done.high_ref), custom_call_target="tpu_custom_call" | custom-call | flops 2700000000 | bytes 1024 | tf_op jit(solution)/shard_map/unpack/pallas_call | solution.py:800
  568.9 3.8 collective-permute-done.35.refs_2_
  573.5 3.4 input_grad.1
  (289 shorter events, 98.3 us)
Async XLA Ops:
  7.2 208.0 %all-gather.2.cloned.1.call-start = ((), (), s32[]{:S(2)}) async-start(), calls=%async_computation.2 | async-start | bytes 14155776 | tf_op jit(solution)/shard_map/all_gather | solution.py:1067
  15.8 544.7 %reduce-scatter.3.cloned.1.call-start = ((), (), s32[]{:S(2)}) async-start(), calls=%async_computation.3 | async-start | bytes 7077888 | tf_op jit(solution)/shard_map/reduce_scatter | solution.py:1149
  164.2 27.5 %collective-permute-start.1 = (bf16[128,1024]{1,0:T(8,128)(2,1)}, bf16[128,1024]{1,0:T(8,128)(2,1)S(1)}, u32[]{:S(2)}, u32[]{:S(2)}) collective-permute-start(bf16[128,1024]{1,0:T(8,128)(2,1)} %get-tuple-element.206.refs_0_.normed_ref), channel_id=1, source_target_pairs={{0,2},{1,3},{2,0},{3,1},{4,6},{5,7},{6,4},{7,5},{8,10},{9,11},{10,... | collective-permute-start | bytes 786440 | tf_op jit(solution)/shard_map/ppermute | solution.py:825
  164.2 31.3 %collective-permute-start = (bf16[128,1024]{1,0:T(8,128)(2,1)}, bf16[128,1024]{1,0:T(8,128)(2,1)S(1)}, u32[]{:S(2)}, u32[]{:S(2)}) collective-permute-start(bf16[128,1024]{1,0:T(8,128)(2,1)} %get-tuple-element.206.refs_0_.normed_ref), channel_id=1, source_target_pairs={{0,1},{1,0},{2,3},{3,2},{4,5},{5,4},{6,7},{7,6},{8,9},{9,8},{10,11... | collective-permute-start | bytes 786440 | tf_op jit(solution)/shard_map/ppermute | solution.py:825
  188.9 20.7 %collective-permute-start.4 = (bf16[128,1024]{1,0:T(8,128)(2,1)}, bf16[128,1024]{1,0:T(8,128)(2,1)S(1)}, u32[]{:S(2)}, u32[]{:S(2)}) collective-permute-start(bf16[128,1024]{1,0:T(8,128)(2,1)} %get-tuple-element.192.refs_0_.refs_4_.normed_ref), channel_id=1, source_target_pairs={{0,2},{1,3},{2,0},{3,1},{4,6},{5,7},{6,4},{7,5},{8,10},{9,11},{10,... | collective-permute-start | bytes 786440 | tf_op jit(solution)/shard_map/ppermute | solution.py:825
  189.1 26.0 %collective-permute-start.7 = (bf16[128,1024]{1,0:T(8,128)(2,1)S(1)}, bf16[128,1024]{1,0:T(8,128)(2,1)S(1)}, u32[]{:S(2)}, u32[]{:S(2)}) collective-permute-start(bf16[128,1024]{1,0:T(8,128)(2,1)S(1)} %get-tuple-element.193.refs_4_.refs_12_), channel_id=1, source_target_pairs={{0,2},{1,3},{2,0},{3,1},{4,6},{5,7},{6,4},{7,5},{8,10},{9,11},{10,... | collective-permute-start | bytes 786440 | tf_op jit(solution)/shard_map/ppermute | solution.py:825
  191.8 23.3 %collective-permute-start.2 = (bf16[128,1024]{1,0:T(8,128)(2,1)S(1)}, bf16[128,1024]{1,0:T(8,128)(2,1)S(1)}, u32[]{:S(2)}, u32[]{:S(2)}) collective-permute-start(bf16[128,1024]{1,0:T(8,128)(2,1)S(1)} %collective-permute-done.1.refs_2_), channel_id=1, source_target_pairs={{0,1},{1,0},{2,3},{3,2},{4,5},{5,4},{6,7},{7,6},{8,9},{9,8},{10,11... | collective-permute-start | bytes 786440 | tf_op jit(solution)/shard_map/ppermute | solution.py:825
  191.8 49.1 %collective-permute-start.3 = (bf16[128,1024]{1,0:T(8,128)(2,1)}, bf16[128,1024]{1,0:T(8,128)(2,1)S(1)}, u32[]{:S(2)}, u32[]{:S(2)}) collective-permute-start(bf16[128,1024]{1,0:T(8,128)(2,1)} %get-tuple-element.192.refs_0_.refs_4_.normed_ref), channel_id=1, source_target_pairs={{0,1},{1,0},{2,3},{3,2},{4,5},{5,4},{6,7},{7,6},{8,9},{9,8},{10,11... | collective-permute-start | bytes 786440 | tf_op jit(solution)/shard_map/ppermute | solution.py:825
  195.5 45.4 %collective-permute-start.6 = (bf16[128,1024]{1,0:T(8,128)(2,1)S(1)}, bf16[128,1024]{1,0:T(8,128)(2,1)S(1)}, u32[]{:S(2)}, u32[]{:S(2)}) collective-permute-start(bf16[128,1024]{1,0:T(8,128)(2,1)S(1)} %get-tuple-element.193.refs_4_.refs_12_), channel_id=1, source_target_pairs={{0,1},{1,0},{2,3},{3,2},{4,5},{5,4},{6,7},{7,6},{8,9},{9,8},{10,11... | collective-permute-start | bytes 786440 | tf_op jit(solution)/shard_map/ppermute | solution.py:825
  209.5 31.4 %collective-permute-start.5 = (bf16[128,1024]{1,0:T(8,128)(2,1)S(1)}, bf16[128,1024]{1,0:T(8,128)(2,1)S(1)}, u32[]{:S(2)}, u32[]{:S(2)}) collective-permute-start(bf16[128,1024]{1,0:T(8,128)(2,1)S(1)} %collective-permute-done.4.refs_2_.refs_6_), channel_id=1, source_target_pairs={{0,1},{1,0},{2,3},{3,2},{4,5},{5,4},{6,7},{7,6},{8,9},{9,8},{10,11... | collective-permute-start | bytes 786440 | tf_op jit(solution)/shard_map/ppermute | solution.py:825
  215.1 25.8 %collective-permute-start.8 = (bf16[128,1024]{1,0:T(8,128)(2,1)S(1)}, bf16[128,1024]{1,0:T(8,128)(2,1)S(1)}, u32[]{:S(2)}, u32[]{:S(2)}) collective-permute-start(bf16[128,1024]{1,0:T(8,128)(2,1)S(1)} %collective-permute-done.7.refs_6_.refs_14_), channel_id=1, source_target_pairs={{0,1},{1,0},{2,3},{3,2},{4,5},{5,4},{6,7},{7,6},{8,9},{9,8},{10,11... | collective-permute-start | bytes 786440 | tf_op jit(solution)/shard_map/ppermute | solution.py:825
  281.9 278.6 %reduce-scatter.5.cloned.1.call-start = ((), (), s32[]{:S(2)}) async-start(), calls=%async_computation.4 | async-start | bytes 7077888 | tf_op jit(solution)/shard_map/reduce_scatter | solution.py:1149
  282.8 9.9 %collective-permute-start.10 = (bf16[128,1152]{1,0:T(8,128)(2,1)S(1)}, bf16[128,1152]{1,0:T(8,128)(2,1)S(1)}, u32[]{:S(2)}, u32[]{:S(2)}) collective-permute-start(bf16[128,1152]{1,0:T(8,128)(2,1)S(1)} %copy-done.29), channel_id=1, source_target_pairs={{0,1},{1,0},{2,3},{3,2},{4,5},{5,4},{6,7},{7,6},{8,9},{9,8},{10,11... | collective-permute-start | bytes 884744 | tf_op jit(solution)/shard_map/ppermute | solution.py:825
  285.6 19.7 %collective-permute-start.13 = (bf16[128,1152]{1,0:T(8,128)(2,1)S(1)}, bf16[128,1152]{1,0:T(8,128)(2,1)S(1)}, u32[]{:S(2)}, u32[]{:S(2)}) collective-permute-start(bf16[128,1152]{1,0:T(8,128)(2,1)S(1)} %copy-done.31), channel_id=1, source_target_pairs={{0,1},{1,0},{2,3},{3,2},{4,5},{5,4},{6,7},{7,6},{8,9},{9,8},{10,11... | collective-permute-start | bytes 884744 | tf_op jit(solution)/shard_map/ppermute | solution.py:825
  285.8 31.0 %collective-permute-start.9 = (bf16[128,1152]{1,0:T(8,128)(2,1)S(1)}, bf16[128,1152]{1,0:T(8,128)(2,1)S(1)}, u32[]{:S(2)}, u32[]{:S(2)}) collective-permute-start(bf16[128,1152]{1,0:T(8,128)(2,1)S(1)} %copy-done.28), channel_id=1, source_target_pairs={{0,1},{1,0},{2,3},{3,2},{4,5},{5,4},{6,7},{7,6},{8,9},{9,8},{10,11... | collective-permute-start | bytes 884744 | tf_op jit(solution)/shard_map/ppermute | solution.py:825
  287.7 50.8 %collective-permute-start.12 = (bf16[128,1152]{1,0:T(8,128)(2,1)S(1)}, bf16[128,1152]{1,0:T(8,128)(2,1)S(1)}, u32[]{:S(2)}, u32[]{:S(2)}) collective-permute-start(bf16[128,1152]{1,0:T(8,128)(2,1)S(1)} %copy-done.26), channel_id=1, source_target_pairs={{0,1},{1,0},{2,3},{3,2},{4,5},{5,4},{6,7},{7,6},{8,9},{9,8},{10,11... | collective-permute-start | bytes 884744 | tf_op jit(solution)/shard_map/ppermute | solution.py:825
  292.8 24.7 %collective-permute-start.11 = (bf16[128,1152]{1,0:T(8,128)(2,1)S(1)}, bf16[128,1152]{1,0:T(8,128)(2,1)S(1)}, u32[]{:S(2)}, u32[]{:S(2)}) collective-permute-start(bf16[128,1152]{1,0:T(8,128)(2,1)S(1)} %add_convert_fusion.7), channel_id=1, source_target_pairs={{0,2},{1,3},{2,0},{3,1},{4,6},{5,7},{6,4},{7,5},{8,10},{9,11},{10,... | collective-permute-start | bytes 884744 | tf_op jit(solution)/shard_map/ppermute | solution.py:825
  305.4 33.1 %collective-permute-start.14 = (bf16[128,1152]{1,0:T(8,128)(2,1)S(1)}, bf16[128,1152]{1,0:T(8,128)(2,1)S(1)}, u32[]{:S(2)}, u32[]{:S(2)}) collective-permute-start(bf16[128,1152]{1,0:T(8,128)(2,1)S(1)} %add_convert_fusion.6), channel_id=1, source_target_pairs={{0,2},{1,3},{2,0},{3,1},{4,6},{5,7},{6,4},{7,5},{8,10},{9,11},{10,... | collective-permute-start | bytes 884744 | tf_op jit(solution)/shard_map/ppermute | solution.py:825
  344.1 10.9 %collective-permute-start.15 = (bf16[128,256]{1,0:T(8,128)(2,1)S(1)}, bf16[128,256]{1,0:T(8,128)(2,1)S(1)}, u32[]{:S(2)}, u32[]{:S(2)}) collective-permute-start(bf16[128,256]{1,0:T(8,128)(2,1)S(1)} %copy-done.54), channel_id=1, source_target_pairs={{0,1},{1,0},{2,3},{3,2},{4,5},{5,4},{6,7},{7,6},{8,9},{9,8},{10,11... | collective-permute-start | bytes 196616 | tf_op jit(solution)/shard_map/ppermute | solution.py:825
  347.0 10.1 %collective-permute-start.16 = (bf16[128,256]{1,0:T(8,128)(2,1)S(1)}, bf16[128,256]{1,0:T(8,128)(2,1)S(1)}, u32[]{:S(2)}, u32[]{:S(2)}) collective-permute-start(bf16[128,256]{1,0:T(8,128)(2,1)S(1)} %copy-done.51), channel_id=1, source_target_pairs={{0,2},{1,3},{2,0},{3,1},{4,6},{5,7},{6,4},{7,5},{8,10},{9,11},{10,... | collective-permute-start | bytes 196616 | tf_op jit(solution)/shard_map/ppermute | solution.py:825
  347.5 11.7 %collective-permute-start.17 = (bf16[128,256]{1,0:T(8,128)(2,1)S(1)}, bf16[128,256]{1,0:T(8,128)(2,1)S(1)}, u32[]{:S(2)}, u32[]{:S(2)}) collective-permute-start(bf16[128,256]{1,0:T(8,128)(2,1)S(1)} %copy-done.50), channel_id=1, source_target_pairs={{0,3},{1,2},{2,1},{3,0},{4,7},{5,6},{6,5},{7,4},{8,11},{9,10},{10,... | collective-permute-start | bytes 196616 | tf_op jit(solution)/shard_map/ppermute | solution.py:825
  353.8 39.4 %collective-permute-start.47 = (bf16[4,128,1024]{2,1,0:T(8,128)(2,1)}, bf16[4,128,1024]{2,1,0:T(8,128)(2,1)S(1)}, u32[]{:S(2)}, u32[]{:S(2)}) collective-permute-start(bf16[4,128,1024]{2,1,0:T(8,128)(2,1)} %get-tuple-element.277), channel_id=1, source_target_pairs={{0,4},{4,0},{8,12},{12,8},{16,20},{20,16},{24,28},{28,24},{1,5},{5... | collective-permute-start | bytes 3145736 | tf_op jit(solution)/shard_map/ppermute | solution.py:825
  353.8 17.5 %collective-permute-start.18 = (bf16[128,256]{1,0:T(8,128)(2,1)S(1)}, bf16[128,256]{1,0:T(8,128)(2,1)S(1)}, u32[]{:S(2)}, u32[]{:S(2)}) collective-permute-start(bf16[128,256]{1,0:T(8,128)(2,1)S(1)} %copy-done.55), channel_id=1, source_target_pairs={{0,1},{1,0},{2,3},{3,2},{4,5},{5,4},{6,7},{7,6},{8,9},{9,8},{10,11... | collective-permute-start | bytes 196616 | tf_op jit(solution)/shard_map/ppermute | solution.py:825
  355.7 18.1 %collective-permute-start.19 = (bf16[128,256]{1,0:T(8,128)(2,1)S(1)}, bf16[128,256]{1,0:T(8,128)(2,1)S(1)}, u32[]{:S(2)}, u32[]{:S(2)}) collective-permute-start(bf16[128,256]{1,0:T(8,128)(2,1)S(1)} %copy-done.53), channel_id=1, source_target_pairs={{0,2},{1,3},{2,0},{3,1},{4,6},{5,7},{6,4},{7,5},{8,10},{9,11},{10,... | collective-permute-start | bytes 196616 | tf_op jit(solution)/shard_map/ppermute | solution.py:825
  357.1 16.7 %collective-permute-start.20 = (bf16[128,256]{1,0:T(8,128)(2,1)S(1)}, bf16[128,256]{1,0:T(8,128)(2,1)S(1)}, u32[]{:S(2)}, u32[]{:S(2)}) collective-permute-start(bf16[128,256]{1,0:T(8,128)(2,1)S(1)} %copy-done.52), channel_id=1, source_target_pairs={{0,3},{1,2},{2,1},{3,0},{4,7},{5,6},{6,5},{7,4},{8,11},{9,10},{10,... | collective-permute-start | bytes 196616 | tf_op jit(solution)/shard_map/ppermute | solution.py:825
  359.2 31.4 %collective-permute-start.28 = (bf16[128,1024]{1,0:T(8,128)(2,1)}, bf16[128,1024]{1,0:T(8,128)(2,1)}, u32[]{:S(2)}, u32[]{:S(2)}) collective-permute-start(bf16[128,1024]{1,0:T(8,128)(2,1)} %get-tuple-element.254), channel_id=1, source_target_pairs={{0,1},{1,0},{2,3},{3,2},{4,5},{5,4},{6,7},{7,6},{8,9},{9,8},{10,11... | collective-permute-start | bytes 786440 | tf_op jit(solution)/shard_map/ppermute | solution.py:825
  371.4 23.4 %collective-permute-start.24 = (bf16[4,512,256]{2,1,0:T(8,128)(2,1)}, bf16[4,512,256]{2,1,0:T(8,128)(2,1)}, u32[]{:S(2)}, u32[]{:S(2)}) collective-permute-start(bf16[4,512,256]{2,1,0:T(8,128)(2,1)} %get-tuple-element.235), channel_id=1, source_target_pairs={{0,4},{4,0},{8,12},{12,8},{16,20},{20,16},{24,28},{28,24},{1,5},{5... | collective-permute-start | bytes 3145736 | tf_op jit(solution)/shard_map/ppermute | solution.py:825
  386.6 30.6 %collective-permute-start.21 = (bf16[4,512,256]{2,1,0:T(8,128)(2,1)}, bf16[4,512,256]{2,1,0:T(8,128)(2,1)}, u32[]{:S(2)}, u32[]{:S(2)}) collective-permute-start(bf16[4,512,256]{2,1,0:T(8,128)(2,1)} %get-tuple-element.233), channel_id=1, source_target_pairs={{0,4},{4,0},{8,12},{12,8},{16,20},{20,16},{24,28},{28,24},{1,5},{5... | collective-permute-start | bytes 3145736 | tf_op jit(solution)/shard_map/ppermute | solution.py:825
  389.5 130.8 %collective-permute-start.27 = (bf16[128,1024]{1,0:T(8,128)(2,1)}, bf16[128,1024]{1,0:T(8,128)(2,1)}, u32[]{:S(2)}, u32[]{:S(2)}) collective-permute-start(bf16[128,1024]{1,0:T(8,128)(2,1)} %get-tuple-element.250), channel_id=1, source_target_pairs={{0,1},{1,0},{2,3},{3,2},{4,5},{5,4},{6,7},{7,6},{8,9},{9,8},{10,11... | collective-permute-start | bytes 786440 | tf_op jit(solution)/shard_map/ppermute | solution.py:825
  390.5 28.3 %collective-permute-start.31 = (bf16[128,1024]{1,0:T(8,128)(2,1)}, bf16[128,1024]{1,0:T(8,128)(2,1)S(1)}, u32[]{:S(2)}, u32[]{:S(2)}) collective-permute-start(bf16[128,1024]{1,0:T(8,128)(2,1)} %get-tuple-element.262), channel_id=1, source_target_pairs={{0,1},{1,0},{2,3},{3,2},{4,5},{5,4},{6,7},{7,6},{8,9},{9,8},{10,11... | collective-permute-start | bytes 786440 | tf_op jit(solution)/shard_map/ppermute | solution.py:825
  393.2 128.9 %collective-permute-start.30 = (bf16[128,1024]{1,0:T(8,128)(2,1)}, bf16[128,1024]{1,0:T(8,128)(2,1)S(1)}, u32[]{:S(2)}, u32[]{:S(2)}) collective-permute-start(bf16[128,1024]{1,0:T(8,128)(2,1)} %get-tuple-element.258), channel_id=1, source_target_pairs={{0,1},{1,0},{2,3},{3,2},{4,5},{5,4},{6,7},{7,6},{8,9},{9,8},{10,11... | collective-permute-start | bytes 786440 | tf_op jit(solution)/shard_map/ppermute | solution.py:825
  394.8 38.9 %collective-permute-start.48 = (bf16[2,128,1024]{2,1,0:T(8,128)(2,1)S(1)}, bf16[2,128,1024]{2,1,0:T(8,128)(2,1)S(1)}, u32[]{:S(2)}, u32[]{:S(2)}) collective-permute-start(bf16[2,128,1024]{2,1,0:T(8,128)(2,1)S(1)} %get-tuple-element.305), channel_id=1, source_target_pairs={{0,8},{4,12},{8,0},{12,4},{16,24},{20,28},{24,16},{28,20},{1,9},{5... | collective-permute-start | bytes 1572872 | tf_op jit(solution)/shard_map/ppermute | solution.py:825
  417.2 34.5 %collective-permute-start.25 = (bf16[2,512,256]{2,1,0:T(8,128)(2,1)S(1)}, bf16[2,512,256]{2,1,0:T(8,128)(2,1)S(1)}, u32[]{:S(2)}, u32[]{:S(2)}) collective-permute-start(bf16[2,512,256]{2,1,0:T(8,128)(2,1)S(1)} %get-tuple-element.307), channel_id=1, source_target_pairs={{0,8},{4,12},{8,0},{12,4},{16,24},{20,28},{24,16},{28,20},{1,9},{5... | collective-permute-start | bytes 1572872 | tf_op jit(solution)/shard_map/ppermute | solution.py:825
  418.8 55.2 %collective-permute-start.22 = (bf16[2,512,256]{2,1,0:T(8,128)(2,1)S(1)}, bf16[2,512,256]{2,1,0:T(8,128)(2,1)S(1)}, u32[]{:S(2)}, u32[]{:S(2)}) collective-permute-start(bf16[2,512,256]{2,1,0:T(8,128)(2,1)S(1)} %get-tuple-element.309), channel_id=1, source_target_pairs={{0,8},{4,12},{8,0},{12,4},{16,24},{20,28},{24,16},{28,20},{1,9},{5... | collective-permute-start | bytes 1572872 | tf_op jit(solution)/shard_map/ppermute | solution.py:825
  433.7 88.4 %collective-permute-start.29 = (bf16[128,1024]{1,0:T(8,128)(2,1)}, bf16[128,1024]{1,0:T(8,128)(2,1)S(1)}, u32[]{:S(2)}, u32[]{:S(2)}) collective-permute-start(bf16[128,1024]{1,0:T(8,128)(2,1)} %add_convert_fusion.16), channel_id=1, source_target_pairs={{0,2},{1,3},{2,0},{3,1},{4,6},{5,7},{6,4},{7,5},{8,10},{9,11},{10,... | collective-permute-start | bytes 786440 | tf_op jit(solution)/shard_map/ppermute | solution.py:825
  451.7 32.2 %collective-permute-start.49 = (bf16[1,128,1024]{2,1,0:T(8,128)(2,1)S(1)}, bf16[1,128,1024]{2,1,0:T(8,128)(2,1)S(1)}, u32[]{:S(2)}, u32[]{:S(2)}) collective-permute-start(bf16[1,128,1024]{2,1,0:T(8,128)(2,1)S(1)} %add_convert_fusion.9), channel_id=1, source_target_pairs={{0,16},{4,20},{8,24},{12,28},{16,0},{20,4},{24,8},{28,12},{1,17},{... | collective-permute-start | bytes 786440 | tf_op jit(solution)/shard_map/ppermute | solution.py:825
  474.0 15.0 %collective-permute-start.26 = (bf16[1,512,256]{2,1,0:T(8,128)(2,1)S(1)}, bf16[1,512,256]{2,1,0:T(8,128)(2,1)S(1)}, u32[]{:S(2)}, u32[]{:S(2)}) collective-permute-start(bf16[1,512,256]{2,1,0:T(8,128)(2,1)S(1)} %add_convert_fusion.17), channel_id=1, source_target_pairs={{0,16},{4,20},{8,24},{12,28},{16,0},{20,4},{24,8},{28,12},{1,17},{... | collective-permute-start | bytes 786440 | tf_op jit(solution)/shard_map/ppermute | solution.py:825
  483.9 39.6 %collective-permute-start.32 = (bf16[128,1024]{1,0:T(8,128)(2,1)S(1)}, bf16[128,1024]{1,0:T(8,128)(2,1)}, u32[]{:S(2)}, u32[]{:S(2)}) collective-permute-start(bf16[128,1024]{1,0:T(8,128)(2,1)S(1)} %add_convert_fusion.15), channel_id=1, source_target_pairs={{0,2},{1,3},{2,0},{3,1},{4,6},{5,7},{6,4},{7,5},{8,10},{9,11},{10,... | collective-permute-start | bytes 786440 | tf_op jit(solution)/shard_map/ppermute | solution.py:825
  519.6 13.7 %collective-permute-start.50 = (bf16[128,256]{1,0:T(8,128)(2,1)S(1)}, bf16[128,256]{1,0:T(8,128)(2,1)S(1)}, u32[]{:S(2)}, u32[]{:S(2)}) collective-permute-start(bf16[128,256]{1,0:T(8,128)(2,1)S(1)} %get-tuple-element.318), channel_id=1, source_target_pairs={{0,1},{1,0},{2,3},{3,2},{4,5},{5,4},{6,7},{7,6},{8,9},{9,8},{10,11... | collective-permute-start | bytes 196616 | tf_op jit(solution)/shard_map/ppermute | solution.py:825
  520.3 13.1 %collective-permute-start.52 = (bf16[128,256]{1,0:T(8,128)(2,1)S(1)}, bf16[128,256]{1,0:T(8,128)(2,1)S(1)}, u32[]{:S(2)}, u32[]{:S(2)}) collective-permute-start(bf16[128,256]{1,0:T(8,128)(2,1)S(1)} %add_convert_fusion.23), channel_id=1, source_target_pairs={{0,2},{1,3},{2,0},{3,1},{4,6},{5,7},{6,4},{7,5},{8,10},{9,11},{10,... | collective-permute-start | bytes 196616 | tf_op jit(solution)/shard_map/ppermute | solution.py:825
  522.1 25.3 %collective-permute-start.44 = (bf16[4,128,512]{2,1,0:T(8,128)(2,1)}, bf16[4,128,512]{2,1,0:T(8,128)(2,1)S(1)}, u32[]{:S(2)}, u32[]{:S(2)}) collective-permute-start(bf16[4,128,512]{2,1,0:T(8,128)(2,1)} %get-tuple-element.276), channel_id=1, source_target_pairs={{0,4},{4,0},{8,12},{12,8},{16,20},{20,16},{24,28},{28,24},{1,5},{5... | collective-permute-start | bytes 1572872 | tf_op jit(solution)/shard_map/ppermute | solution.py:825
  522.9 25.9 %collective-permute-start.37 = (bf16[128,1024]{1,0:T(8,128)(2,1)}, bf16[128,1024]{1,0:T(8,128)(2,1)S(1)}, u32[]{:S(2)}, u32[]{:S(2)}) collective-permute-start(bf16[128,1024]{1,0:T(8,128)(2,1)} %get-tuple-element.270), channel_id=1, source_target_pairs={{0,1},{1,0},{2,3},{3,2},{4,5},{5,4},{6,7},{7,6},{8,9},{9,8},{10,11... | collective-permute-start | bytes 786440 | tf_op jit(solution)/shard_map/ppermute | solution.py:825
  530.2 24.3 %collective-permute-start.34 = (bf16[128,1024]{1,0:T(8,128)(2,1)}, bf16[128,1024]{1,0:T(8,128)(2,1)S(1)}, u32[]{:S(2)}, u32[]{:S(2)}) collective-permute-start(bf16[128,1024]{1,0:T(8,128)(2,1)} %get-tuple-element.266), channel_id=1, source_target_pairs={{0,1},{1,0},{2,3},{3,2},{4,5},{5,4},{6,7},{7,6},{8,9},{9,8},{10,11... | collective-permute-start | bytes 786440 | tf_op jit(solution)/shard_map/ppermute | solution.py:825
  533.3 33.3 %collective-permute-start.36 = (bf16[128,1024]{1,0:T(8,128)(2,1)S(1)}, bf16[128,1024]{1,0:T(8,128)(2,1)S(1)}, u32[]{:S(2)}, u32[]{:S(2)}) collective-permute-start(bf16[128,1024]{1,0:T(8,128)(2,1)S(1)} %copy-done.36), channel_id=1, source_target_pairs={{0,1},{1,0},{2,3},{3,2},{4,5},{5,4},{6,7},{7,6},{8,9},{9,8},{10,11... | collective-permute-start | bytes 786440 | tf_op jit(solution)/shard_map/ppermute | solution.py:825
  533.4 11.6 %collective-permute-start.43 = (f32[24,32]{1,0:T(8,128)S(1)}, f32[24,32]{1,0:T(8,128)S(1)}, u32[]{:S(2)}, u32[]{:S(2)}) collective-permute-start(f32[24,32]{1,0:T(8,128)S(1)} %slice_select_fusion.2), channel_id=1, source_target_pairs={{0,1},{1,0},{2,3},{3,2},{4,5},{5,4},{6,7},{7,6},{8,9},{9,8},{10,11... | collective-permute-start | bytes 9224 | tf_op jit(solution)/shard_map/ppermute | solution.py:825
  545.0 21.6 %collective-permute-start.33 = (bf16[128,1024]{1,0:T(8,128)(2,1)S(1)}, bf16[128,1024]{1,0:T(8,128)(2,1)}, u32[]{:S(2)}, u32[]{:S(2)}) collective-permute-start(bf16[128,1024]{1,0:T(8,128)(2,1)S(1)} %copy-done.34), channel_id=1, source_target_pairs={{0,1},{1,0},{2,3},{3,2},{4,5},{5,4},{6,7},{7,6},{8,9},{9,8},{10,11... | collective-permute-start | bytes 786440 | tf_op jit(solution)/shard_map/ppermute | solution.py:825
  548.8 20.1 %collective-permute-start.38 = (bf16[128,1024]{1,0:T(8,128)(2,1)S(1)}, bf16[128,1024]{1,0:T(8,128)(2,1)S(1)}, u32[]{:S(2)}, u32[]{:S(2)}) collective-permute-start(bf16[128,1024]{1,0:T(8,128)(2,1)S(1)} %add_convert_fusion.13), channel_id=1, source_target_pairs={{0,2},{1,3},{2,0},{3,1},{4,6},{5,7},{6,4},{7,5},{8,10},{9,11},{10,... | collective-permute-start | bytes 786440 | tf_op jit(solution)/shard_map/ppermute | solution.py:825
  554.5 18.2 %collective-permute-start.35 = (bf16[128,1024]{1,0:T(8,128)(2,1)S(1)}, bf16[128,1024]{1,0:T(8,128)(2,1)S(1)}, u32[]{:S(2)}, u32[]{:S(2)}) collective-permute-start(bf16[128,1024]{1,0:T(8,128)(2,1)S(1)} %add_convert_fusion.14), channel_id=1, source_target_pairs={{0,2},{1,3},{2,0},{3,1},{4,6},{5,7},{6,4},{7,5},{8,10},{9,11},{10,... | collective-permute-start | bytes 786440 | tf_op jit(solution)/shard_map/ppermute | solution.py:825
  (70 other events, 638.5 us)
Sparse Core Ops, SparseCore 0:
  15.9 87.2 all-gather.1
  282.0 86.5 reduce-scatter.2
  372.0 84.3 reduce-scatter.4
where the time goes:
time: 579 us; the launch traced here: 584 us
  Pallas kernels  303 us (52%)
  starting transfers between devices  115 us (20%)
  waiting for transfers between devices  107 us (18%)
  local copies, waits for them, and re-layouts  25.2 us (4%)
  other arithmetic  18.2 us (3%)
  between operations  15 us (3%)
    pallas_call x5, Pallas kernels, run(): pl.pallas_call(self.kernel, out_shape=self.outputs, in_specs=[anywhere] *...  119 us
    ppermute x53, starting transfers between devices, exchange(): return lax.ppermute(values, axis, [(i, i ^ bit) for i in range(count)])  115 us
    ppermute x53, waiting for transfers between devices, exchange(): return lax.ppermute(values, axis, [(i, i ^ bit) for i in range(count)])  107 us
    pallas_call x2, Pallas kernels, experts_both(): pl.pallas_call(functools.partial(expert_kernel, slots), grid_spec=pltpu.P...  49.9 us
    pallas_call x2, Pallas kernels, expert_grads(): pl.pallas_call(functools.partial(expert_grad_kernel, micro, slots), grid=...  30.1 us
    pallas_call x2, Pallas kernels, attend_back(): pl.pallas_call(functools.partial(attend_back_kernel, slots), grid_spec=pl...  23.7 us
    pallas_call x2, Pallas kernels, attend(): pl.pallas_call(attend_kernel, grid_spec=pltpu.PrefetchScalarGridSpec(num_...  18.6 us
  transfers between devices with their start and end apart: 56, of which 18 were waited for; matrix products, arithmetic and copies ran while one was open for 5% of the time, Pallas kernels for 45%

commit v1 on v0

--- a/solution.py
+++ b/solution.py
@@ -62,11 +62,15 @@
 
 
 def cost(microseconds):
-    return pl.CostEstimate(flops=int(microseconds * 9e8), bytes_accessed=1024, transcendentals=0)
+    return pl.CostEstimate(flops=int(microseconds * 6e7), bytes_accessed=1024, transcendentals=0)
 
 
 def params():
     return pltpu.CompilerParams(vmem_limit_bytes=VMEM_CAP)
+
+
+def riding(number):
+    return pltpu.CompilerParams(vmem_limit_bytes=VMEM_CAP, collective_id=number, has_side_effects=True)
 
 
 def shape(dims, kind):
@@ -232,7 +236,9 @@
 
 def attend_back_kernel(slots, info_ref, q_ref, kv_ref, log_ref, cos_ref, sin_ref, *refs):
     out_refs, grad_refs = refs[:slots], refs[slots : 2 * slots]
-    dq_ref, keep_ref, send_ref, heads, grads, delta, accum, dkv = refs[2 * slots :]
+    blocks = BLOCKS[0]
+    dq_ref, dkv_refs = refs[2 * slots], refs[2 * slots + 1 : 2 * slots + 1 + blocks]
+    heads, grads, delta, accum, dkv = refs[2 * slots + 1 + blocks :]
     j = pl.program_id(0)
     count = pl.num_programs(0)
     mine, rank, length = info_ref[0], info_ref[1], info_ref[2]
@@ -285,13 +291,11 @@
     def _():
         dkv[...] = jnp.zeros(dkv.shape, bf16)
 
-    @pl.when(j < count // 2)
-    def _():
-        keep_ref[0] = dkv[...]
-
-    @pl.when(j >= count // 2)
-    def _():
-        send_ref[0] = dkv[...]
+    for place in range(blocks):
+
+        @pl.when(j == place)
+        def _():
+            dkv_refs[place][...] = dkv[...]
 
     @pl.when(j == count - 1)
     def _():
@@ -305,7 +309,7 @@
 def attend_back(info, query, kv_all, log_total, cos_row, sin_row, att_slots, grad_slots):
     span, cols = query.shape
     blocks, slots = kv_all.shape[0], len(att_slots)
-    rows, half = span // slots, blocks // 2
+    rows = span // slots
     BLOCKS[0] = blocks
     fixed = lambda *dims: pl.BlockSpec(dims, lambda j, info_ref: (0,) * len(dims))
     return pl.pallas_call(
@@ -321,11 +325,7 @@
                 fixed(span, LANES),
             ]
             + [fixed(rows, cols)] * (2 * slots),
-            out_specs=[
-                fixed(span, cols),
-                pl.BlockSpec((1, span, 2 * LANES), lambda j, info_ref: (jnp.minimum(j, half - 1), 0, 0)),
-                pl.BlockSpec((1, span, 2 * LANES), lambda j, info_ref: (jnp.maximum(j - half, 0), 0, 0)),
-            ],
+            out_specs=[fixed(span, cols)] + [fixed(span, 2 * LANES)] * blocks,
             scratch_shapes=[
                 pltpu.VMEM((4, span, LANES), bf16),
                 pltpu.VMEM((4, span, LANES), bf16),
@@ -334,7 +334,7 @@
                 pltpu.VMEM((span, 2 * LANES), bf16),
             ],
         ),
-        out_shape=[shape((span, cols), bf16)] + [shape((half, span, 2 * LANES), bf16)] * 2,
+        out_shape=[shape((span, cols), bf16)] + [shape((span, 2 * LANES), bf16)] * blocks,
         compiler_params=params(),
         cost_estimate=cost(18),
         name="attend_back",
@@ -362,20 +362,24 @@
     )(x, gain, weight, *att_slots)
 
 
-def expert_kernel(slots, info_ref, routes_ref, router_ref, w_ref, *refs):
+def expert_kernel(slots, ride, info_ref, routes_ref, router_ref, w_ref, *refs):
     x_refs, gm_refs = refs[:slots], refs[slots : 2 * slots]
-    gin_refs, mixed_refs = refs[2 * slots : 3 * slots], refs[3 * slots : 4 * slots]
-    gates_ref, low_g, low_h, x_all, gm_all, gates, mixed, gin, gate_sums = refs[4 * slots :]
+    ride_in, refs = refs[2 * slots : 2 * slots + len(ride.inputs)], refs[2 * slots + len(ride.inputs) :]
+    gin_refs, mixed_refs, refs = refs[:slots], refs[slots : 2 * slots], refs[2 * slots :]
+    gates_ref, low_g, low_h = refs[:3]
+    ride_out, refs = refs[3 : 3 + len(ride.outputs)], refs[3 + len(ride.outputs) :]
+    x_all, gm_all, gates, mixed, gin, gate_sums, send, recv = refs
     step = pl.program_id(0)
     last = pl.num_programs(0) - 1
     span, width = x_all.shape
     rows = span // slots
     wide = PAIR * LANES
     chunk = 256
-    rank = info_ref[1]
+    rank = lax.axis_index("tp")
 
     @pl.when(step == 0)
     def _():
+        ride.begin(ride_in, ride_out, send, recv)
         lane = lax.broadcasted_iota(jnp.int32, (rows, LANES), 1)
         for slot in range(slots):
             here = slice(slot * rows, (slot + 1) * rows)
@@ -434,9 +438,10 @@
             mixed_refs[slot][...] = mixed[here, :].astype(bf16)
             gin_refs[slot][:, 0:width] = gin[here, :].astype(bf16)
             gin_refs[slot][:, width : width + LANES] = gate_sums[here, :].astype(bf16)
-
-
-def experts_both(info, routes, router, weight, x_slots, gm_slots):
+        ride.finish(ride_in, ride_out, send, recv)
+
+
+def experts_both(info, routes, router, weight, x_slots, gm_slots, ride, number):
     rows, width = x_slots[0].shape
     slots = len(x_slots)
     span = rows * slots
@@ -444,16 +449,19 @@
     steps = weight.shape[1] // (3 * wide)
     fixed = lambda *dims: pl.BlockSpec(dims, lambda i, info_ref: (0,) * len(dims))
     moving = lambda height, cols: pl.BlockSpec((height, cols), lambda i, info_ref: (0, i))
-    return pl.pallas_call(
-        functools.partial(expert_kernel, slots),
+    anywhere = pl.BlockSpec(memory_space=pl.ANY)
+    results = pl.pallas_call(
+        functools.partial(expert_kernel, slots, ride),
         grid_spec=pltpu.PrefetchScalarGridSpec(
             num_scalar_prefetch=1,
             grid=(steps,),
             in_specs=[fixed(*routes.shape), fixed(*router.shape), moving(width, 3 * wide)]
-            + [fixed(rows, width)] * (2 * slots),
+            + [fixed(rows, width)] * (2 * slots)
+            + [anywhere] * len(ride.inputs),
             out_specs=[fixed(rows, width + LANES)] * slots
             + [fixed(rows, width)] * slots
-            + [fixed(rows, LANES), moving(span, 2 * wide), moving(span, wide)],
+            + [fixed(rows, LANES), moving(span, 2 * wide), moving(span, wide)]
+            + [anywhere] * len(ride.outputs),
             scratch_shapes=[
                 pltpu.VMEM((span, width), bf16),
                 pltpu.VMEM((span, width), bf16),
@@ -461,22 +469,30 @@
                 pltpu.VMEM((span, width), f32),
                 pltpu.VMEM((span, width), f32),
                 pltpu.VMEM((span, LANES), f32),
-            ],
+            ]
+            + ride.semaphores(),
         ),
         out_shape=[shape((rows, width + LANES), bf16)] * slots
         + [shape((rows, width), bf16)] * slots
-        + [shape((rows, LANES), f32), shape((span, steps * 2 * wide), bf16), shape((span, steps * wide), bf16)],
-        compiler_params=params(),
+        + [shape((rows, LANES), f32), shape((span, steps * 2 * wide), bf16), shape((span, steps * wide), bf16)]
+        + ride.outputs,
+        compiler_params=riding(number),
         cost_estimate=cost(24),
         name="experts",
-    )(info, routes, router, weight, *x_slots, *gm_slots)
-
-
-def expert_grad_kernel(micro, slots, *refs):
+    )(info, routes, router, weight, *x_slots, *gm_slots, *ride.inputs)
+    ride.made = list(results[2 * slots + 3 :])
+    return results[: 2 * slots + 3]
+
+
+def expert_grad_kernel(micro, slots, ride, *refs):
     count = micro * slots
+    send, recv = refs[-2:]
+    given = 2 * count + 2 * micro
+    ride_in = refs[given : given + len(ride.inputs)]
+    ride_out = refs[given + len(ride.inputs) + 1 : given + len(ride.inputs) + 1 + len(ride.outputs)]
     x_refs, gm_refs = refs[:count], refs[count : 2 * count]
     g_refs, h_refs = refs[2 * count : 2 * count + micro], refs[2 * count + micro : 2 * count + 2 * micro]
-    dw_ref, x_t, gm_t = refs[2 * count + 2 * micro :]
+    dw_ref, (x_t, gm_t) = refs[given + len(ride.inputs)], refs[-4:-2]
     rows = x_refs[0].shape[0]
     width = x_t.shape[0]
     wide = PAIR * LANES
@@ -484,6 +500,7 @@
 
     @pl.when(pl.program_id(0) == 0)
     def _():
+        ride.begin(ride_in, ride_out, send, recv)
         for i in range(count):
             x_t[:, i * rows : (i + 1) * rows] = x_refs[i][...].T
             gm_t[:, i * rows : (i + 1) * rows] = gm_refs[i][...].T
@@ -501,43 +518,53 @@
 
     lax.fori_loop(0, width // chunk, weight_step, 0)
 
-
-def expert_grads(x_slots, gm_slots, lows_g, lows_h, part, parts):
+    @pl.when(pl.program_id(0) == pl.num_programs(0) - 1)
+    def _():
+        ride.finish(ride_in, ride_out, send, recv)
+
+
+def expert_grads(x_slots, gm_slots, lows_g, lows_h, ride, number):
     micro, slots = len(x_slots), len(x_slots[0])
     rows, width = x_slots[0][0].shape
     span = rows * slots
     wide = PAIR * LANES
-    steps = lows_h[0].shape[1] // wide // parts
-    first = part * steps
+    steps = lows_h[0].shape[1] // wide
     fixed = pl.BlockSpec((rows, width), lambda i: (0, 0))
-    moving = lambda height, cols: pl.BlockSpec((height, cols), lambda i: (0, first + i))
+    moving = lambda height, cols: pl.BlockSpec((height, cols), lambda i: (0, i))
     flat = [block for part in x_slots for block in part] + [block for part in gm_slots for block in part]
-    return pl.pallas_call(
-        functools.partial(expert_grad_kernel, micro, slots),
+    anywhere = pl.BlockSpec(memory_space=pl.ANY)
+    summed, *ride.made = pl.pallas_call(
+        functools.partial(expert_grad_kernel, micro, slots, ride),
         grid=(steps,),
-        in_specs=[fixed] * len(flat) + [moving(span, 2 * wide)] * micro + [moving(span, wide)] * micro,
-        out_specs=pl.BlockSpec((width, 3 * wide), lambda i: (0, i)),
-        out_shape=shape((width, steps * 3 * wide), bf16),
-        scratch_shapes=[pltpu.VMEM((width, micro * span), bf16), pltpu.VMEM((width, micro * span), bf16)],
-        compiler_params=params(),
+        in_specs=[fixed] * len(flat) + [moving(span, 2 * wide)] * micro + [moving(span, wide)] * micro
+        + [anywhere] * len(ride.inputs),
+        out_specs=[pl.BlockSpec((width, 3 * wide), lambda i: (0, i))] + [anywhere] * len(ride.outputs),
+        out_shape=[shape((width, steps * 3 * wide), bf16)] + ride.outputs,
+        scratch_shapes=[pltpu.VMEM((width, micro * span), bf16), pltpu.VMEM((width, micro * span), bf16)]
+        + ride.semaphores(),
+        compiler_params=riding(number),
         cost_estimate=cost(12),
         name="expert_grads",
-    )(*flat, *lows_g, *lows_h)
+    )(*flat, *lows_g, *lows_h, *ride.inputs)
+    return summed
 
 
 def moe_back_kernel(
-    slots, info_ref, p0, p1, p2, gates_ref, router_ref, middle_ref, normed_ref, gain_ref, cot_ref, w_ref, *refs
+    slots, info_ref, *refs
 ):
+    parts, refs = refs[:slots], refs[slots:]
+    gates_ref, router_ref, middle_ref, normed_ref, gain_ref, cot_ref, w_ref = refs[:7]
+    refs = refs[7:]
     grad_middle_ref, grad_attn_ref, sums_ref = refs[:3]
     out_refs = refs[3:]
     rows, width = middle_ref.shape
     gate = lambda ref: ref[:, width : width + LANES].astype(f32)
     gates = gates_ref[...]
-    gate_grads = gate(p0) + gate(p1) + gate(p2)
+    gate_grads = sum(gate(part) for part in parts)
     grad_logits = gates * (gate_grads - jnp.sum(gates * gate_grads, axis=1, keepdims=True))
     grad_logits = grad_logits.astype(bf16)
     main = lambda ref: ref[:, 0:width].astype(f32)
-    grad_moe = main(p0) + main(p1) + main(p2) + dot_nt(grad_logits, router_ref[...])
+    grad_moe = sum(main(part) for part in parts) + dot_nt(grad_logits, router_ref[...])
     middle, gain = middle_ref[...], gain_ref[...]
     inverse, unit, _ = normalised(middle, gain)
     weighted = grad_moe * gain
@@ -579,17 +606,19 @@
     )(info, *operands)
 
 
-def qkv_back_kernel(slots, dq_ref, dkv_ref, cos_ref, sin_ref, gain_ref, w_ref, *refs):
+def qkv_back_kernel(slots, blocks, dq_ref, cos_ref, sin_ref, gain_ref, w_ref, *refs):
+    dkv_refs, refs = refs[:blocks], refs[blocks:]
+    dkv = sum(ref[...].astype(f32) for ref in dkv_refs)
     x_refs, part_refs = refs[:slots], refs[slots : 2 * slots]
     grads_ref, normed_ref, sums_ref = refs[2 * slots :]
     rows = x_refs[0].shape[0]
     width = w_ref.shape[0]
     cols = dq_ref.shape[1]
-    dk = dkv_ref[:, 0:LANES].astype(f32)
+    dk = dkv[:, 0:LANES]
     turned = dk * cos_ref[...] - swap_halves(dk) * sin_ref[...]
     grads_ref[:, 0:cols] = dq_ref[...]
     grads_ref[:, cols : cols + LANES] = turned.astype(bf16)
-    grads_ref[:, cols + LANES : cols + 2 * LANES] = dkv_ref[:, LANES : 2 * LANES].astype(bf16)
+    grads_ref[:, cols + LANES : cols + 2 * LANES] = dkv[:, LANES : 2 * LANES].astype(bf16)
     total = jnp.zeros((1, width), f32)
     for slot in range(slots):
         here = slice(slot * rows, (slot + 1) * rows)
@@ -602,26 +631,25 @@
     sums_ref[...] = jnp.where(first, jnp.broadcast_to(total, (8, width)), 0.0)
 
 
-def qkv_back(dq, dkv, cos_row, sin_row, gain, weight, x_slots):
+def qkv_back(dq, dkv_parts, cos_row, sin_row, gain, weight, x_slots):
     slots = len(x_slots)
     rows, width = x_slots[0].shape
     span = rows * slots
     return pl.pallas_call(
-        functools.partial(qkv_back_kernel, slots),
+        functools.partial(qkv_back_kernel, slots, len(dkv_parts)),
         out_shape=[shape((rows, width), bf16)] * slots
         + [shape((span, weight.shape[1]), bf16), shape((span, width), bf16), shape((8, width), f32)],
         compiler_params=params(),
         cost_estimate=cost(4),
         name="qkv_back",
-    )(dq, dkv, cos_row, sin_row, gain, weight, *x_slots)
-
-
-def input_grad_kernel(micro, *refs):
-    part_refs, middle_refs = refs[: 3 * micro], refs[3 * micro : 4 * micro]
-    x_ref, gain_ref, out_ref = refs[4 * micro :]
+    )(dq, cos_row, sin_row, gain, weight, *dkv_parts, *x_slots)
+
+
+def input_grad_kernel(micro, slots, *refs):
+    part_refs, middle_refs = refs[: slots * micro], refs[slots * micro : (slots + 1) * micro]
+    x_ref, gain_ref, out_ref = refs[(slots + 1) * micro :]
     for m in range(micro):
-        p0, p1, p2 = (ref[...].astype(f32) for ref in part_refs[3 * m : 3 * m + 3])
-        grad_normed = p0 + p1 + p2
+        grad_normed = sum(ref[...].astype(f32) for ref in part_refs[slots * m : slots * (m + 1)])
         x = x_ref[m].astype(f32)
         inverse, _, _ = normalised(x, gain_ref[...])
         weighted = grad_normed * gain_ref[...]
@@ -632,7 +660,7 @@
 def close_input_grad(parts, grad_middles, x, gain):
     micro = x.shape[0]
     return pl.pallas_call(
-        functools.partial(input_grad_kernel, micro),
+        functools.partial(input_grad_kernel, micro, len(parts[0])),
         out_shape=shape(x.shape, f32),
         compiler_params=params(),
         cost_estimate=cost(2),
@@ -641,13 +669,13 @@
 
 
 def outputs_kernel(micro, slots, info_ref, *refs):
-    part_refs, middle_refs, out_ref = refs[: 3 * micro], refs[3 * micro : 4 * micro], refs[4 * micro]
+    part_refs, middle_refs, out_ref = refs[: slots * micro], refs[slots * micro : -1], refs[-1]
     rows, width = middle_refs[0].shape
     start = info_ref[0] * rows * slots + info_ref[1] * rows
     row_pos = start + lax.broadcasted_iota(jnp.int32, (rows, width), 0)
     for m in range(micro):
-        p0, p1, p2 = (ref[...].astype(f32) for ref in part_refs[3 * m : 3 * m + 3])
-        total = middle_refs[m][...] + (p0 + p1 + p2)
+        mixed = sum(ref[...].astype(f32) for ref in part_refs[slots * m : slots * (m + 1)])
+        total = middle_refs[m][...] + mixed
         out_ref[m] = jnp.where(row_pos < info_ref[2 + m], total, 0.0).astype(bf16)
 
 
@@ -773,37 +801,23 @@
     )(info, *lefts, *rights)
 
 
-def unpack_kernel(half, low_ref, high_ref, gate_ref, up_ref, down_ref):
-    i = pl.program_id(0)
-
-    def place(ref):
-        for member in range(PAIR):
-            cut = lambda kind: ref[:, (kind * PAIR + member) * LANES : (kind * PAIR + member + 1) * LANES].astype(f32)
-            gate_ref[member] = cut(0)
-            up_ref[member] = cut(1)
-            down_ref[member] = cut(2).T
-
-    @pl.when(i < half)
-    def _():
-        place(low_ref)
-
-    @pl.when(i >= half)
-    def _():
-        place(high_ref)
-
-
-def unpack_experts(halves):
-    rows, cols = halves[0].shape
+def unpack_kernel(sum_ref, gate_ref, up_ref, down_ref):
+    for member in range(PAIR):
+        cut = lambda kind: sum_ref[:, (kind * PAIR + member) * LANES : (kind * PAIR + member + 1) * LANES].astype(f32)
+        gate_ref[member] = cut(0)
+        up_ref[member] = cut(1)
+        down_ref[member] = cut(2).T
+
+
+def unpack_experts(summed):
+    rows, cols = summed.shape
     part = 3 * PAIR * LANES
-    half = cols // part
-    experts = 2 * half * PAIR
+    count = cols // part
+    experts = count * PAIR
     return pl.pallas_call(
-        functools.partial(unpack_kernel, half),
-        grid=(2 * half,),
-        in_specs=[
-            pl.BlockSpec((rows, part), lambda i: (0, jnp.minimum(i, half - 1))),
-            pl.BlockSpec((rows, part), lambda i: (0, jnp.maximum(i - half, 0))),
-        ],
+        unpack_kernel,
+        grid=(count,),
+        in_specs=[pl.BlockSpec((rows, part), lambda i: (0, i))],
         out_specs=[
             pl.BlockSpec((PAIR, rows, LANES), lambda i: (i, 0, 0)),
             pl.BlockSpec((PAIR, rows, LANES), lambda i: (i, 0, 0)),
@@ -815,25 +829,14 @@
             shape((experts, LANES, rows), f32),
         ],
         compiler_params=params(),
-        cost_estimate=cost(3),
+        cost_estimate=cost(5),
         name="unpack",
-    )(*halves)
+    )(summed)
 
 
 def exchange(values, axis, bit):
     count = lax.axis_size(axis)
     return lax.ppermute(values, axis, [(i, i ^ bit) for i in range(count)])
-
-
-def gather_slots(values, axis):
-    count = lax.axis_size(axis)
-    slots = {0: values}
-    bit = count // 2
-    while bit:
-        for slot in sorted(slots):
-            slots[slot | bit] = exchange(slots[slot], axis, bit)
-        bit //= 2
-    return [slots[slot] for slot in range(count)]
 
 
 class Moves:
@@ -877,6 +880,37 @@
             made.append(self.make(blocks[slot].shape, blocks[slot].dtype))
             self.copy((self.take(blocks[slot]), ()), (made[-1], ()), ("tp", slot), [], blocks[slot].size * 4)
         return made
+
+    def share_tp(self, value):
+        held, made = self.take(value), []
+        for slot in range(1, lax.axis_size("tp")):
+            made.append(self.make(value.shape, value.dtype))
+            self.copy((held, ()), (made[-1], ()), ("tp", slot), [], value.size * 4)
+        return made
+
+    def trade_fsdp(self, blocks):
+        made = []
+        for place in range(1, len(blocks)):
+            made.append(self.make(blocks[place].shape, blocks[place].dtype))
+            slot = reversed_bits(place, len(blocks))
+            self.copy((self.take(blocks[place]), ()), (made[-1], ()), ("fsdp", slot), [], blocks[place].size * 4)
+        return made
+
+    def trade_stack(self, value, first, count):
+        skip = int(first == 0)
+        held, target = self.take(value), self.make((value.shape[0] - skip,) + value.shape[1:], value.dtype)
+        for j in range(skip, value.shape[0]):
+            slot = reversed_bits(first + j, count)
+            self.copy((held, (j,)), (target, (j - skip,)), ("fsdp", slot), [], value[0].size * 4)
+        return target
+
+    def trade_rows(self, value, count):
+        rows = value.shape[0] // count
+        held, target = self.take(value), self.make((count - 1, rows) + value.shape[1:], value.dtype)
+        for slot in range(1, count):
+            source = lambda ranks, slot=slot: (pl.ds(pl.multiple_of((ranks["fsdp"] ^ slot) * rows, rows), rows),)
+            self.copy((held, source), (target, (slot - 1,)), ("fsdp", slot), [], rows * 512)
+        return target
 
     def spread(self, source, target, rows, size, pieces, needs):
         count = lax.axis_size("fsdp")
@@ -908,57 +942,76 @@
         needs = [self.copy((held, ()), (target, (0, 0)), None, [], value.size)]
         for slot in range(1, slots):
             needs.append(self.copy((held, ()), (target, (0, slot)), ("tp", slot), [], value.size * 2))
-        self.spread(lambda inner: (target, (0,) + inner), target, slots, value.size * 2 * slots, 1, needs)
+        self.spread(lambda inner: (target, (0,) + inner), target, slots, value.size * 2 * slots, 2, needs)
         return target
+
+    def meet(self):
+        ranks = {axis: lax.axis_index(axis) for axis in ("fsdp", "tp")}
+        barrier = pltpu.get_barrier_semaphore()
+        places = sorted({step[2] for step in self.steps if step[2]})
+        for axis, bit in places:
+            pl.semaphore_signal(
+                barrier, inc=1, device_id={axis: ranks[axis] ^ bit}, device_id_type=pl.DeviceIdType.MESH
+            )
+        pl.semaphore_wait(barrier, len(places))
+
+    def describe(self, number, ins, outs, send, recv):
+        ranks = {axis: lax.axis_index(axis) for axis in ("fsdp", "tp")}
+
+        def view(spot):
+            (kind, which), index = spot
+            ref = (ins if kind == "in" else outs)[which]
+            index = index(ranks) if callable(index) else index
+            return ref.at[index] if index else ref
+
+        source, target, place = self.steps[number][:3]
+        if place is None:
+            return pltpu.make_async_copy(view(source), view(target), send.at[number])
+        axis, bit = place
+        return pltpu.make_async_remote_copy(
+            src_ref=view(source),
+            dst_ref=view(target),
+            send_sem=send.at[number],
+            recv_sem=recv.at[number],
+            device_id={axis: ranks[axis] ^ bit},
+            device_id_type=pl.DeviceIdType.MESH,
+        )
+
+    def begin(self, ins, outs, send, recv):
+        self.meet()
+        for number in range(len(self.steps)):
+            self.describe(number, ins, outs, send, recv).start()
+
+    def finish(self, ins, outs, send, recv):
+        for number in range(len(self.steps)):
+            self.describe(number, ins, outs, send, recv).wait()
 
     def kernel(self, *refs):
         ins, outs = refs[: len(self.inputs)], refs[len(self.inputs) : len(self.inputs) + len(self.outputs)]
         send, recv = refs[-2:]
-        ranks = {axis: lax.axis_index(axis) for axis in ("fsdp", "tp")}
-        partner = lambda place: {place[0]: ranks[place[0]] ^ place[1]}
-        barrier = pltpu.get_barrier_semaphore()
-        places = sorted({step[2] for step in self.steps if step[2]})
-        for place in places:
-            pl.semaphore_signal(barrier, inc=1, device_id=partner(place), device_id_type=pl.DeviceIdType.MESH)
-        pl.semaphore_wait(barrier, len(places))
-
-        def view(spot):
-            (kind, number), index = spot
-            ref = (ins if kind == "in" else outs)[number]
-            return ref.at[index] if index else ref
-
+        self.meet()
         started, arrived = {}, set()
 
         def arrive(number):
             if number not in arrived:
                 arrived.add(number)
-                copy, place = started[number]
-                if place:
-                    copy.wait_recv()
+                if self.steps[number][2]:
+                    started[number].wait_recv()
                 else:
-                    copy.wait()
+                    started[number].wait()
 
         for number in sorted(range(len(self.steps)), key=lambda i: self.steps[i][4]):
-            source, target, place, needs, _, _ = self.steps[number]
-            for need in needs:
+            for need in self.steps[number][3]:
                 arrive(need)
-            if place:
-                copy = pltpu.make_async_remote_copy(
-                    src_ref=view(source),
-                    dst_ref=view(target),
-                    send_sem=send.at[number],
-                    recv_sem=recv.at[number],
-                    device_id=partner(place),
-                    device_id_type=pl.DeviceIdType.MESH,
-                )
-            else:
-                copy = pltpu.make_async_copy(view(source), view(target), send.at[number])
-            copy.start()
-            started[number] = (copy, place)
+            started[number] = self.describe(number, ins, outs, send, recv)
+            started[number].start()
         for number in sorted(range(len(self.steps)), key=lambda i: self.steps[i][5]):
             arrive(number)
             if self.steps[number][2]:
-                started[number][0].wait_send()
+                started[number].wait_send()
+
+    def semaphores(self):
+        return [pltpu.SemaphoreType.DMA((len(self.steps),)), pltpu.SemaphoreType.DMA((len(self.steps),))]
 
     def run(self, number, time, name):
         count = len(self.steps)
@@ -981,41 +1034,6 @@
 
 def trade_slots(blocks, axis):
     return [blocks[0]] + [exchange(blocks[slot], axis, slot) for slot in range(1, len(blocks))]
-
-
-def scatter_slots(blocks):
-    if len(blocks) == 2:
-        return [blocks[0], exchange(blocks[1], "tp", 1), jnp.zeros_like(blocks[0])]
-    met = exchange(blocks[3], "tp", 1)
-    near = exchange(blocks[1], "tp", 1)
-    joined = (blocks[2].astype(f32) + met.astype(f32)).astype(bf16)
-    return [blocks[0], near, exchange(joined, "tp", 2)]
-
-
-def scatter_spans(keep, send):
-    bit = 1
-    while True:
-        came = exchange(send, "fsdp", bit)
-        half = keep.shape[0] // 2
-        if half == 0:
-            return keep[0].astype(f32) + came[0].astype(f32)
-        send = (keep[half:].astype(f32) + came[half:].astype(f32)).astype(bf16)
-        keep = (keep[:half].astype(f32) + came[:half].astype(f32)).astype(bf16)
-        bit *= 2
-
-
-def scatter_columns(values):
-    for axis in ("fsdp", "tp"):
-        rank = lax.axis_index(axis)
-        bit = lax.axis_size(axis) // 2
-        while bit:
-            half = values.shape[1] // 2
-            upper = (rank // bit) % 2 == 1
-            low, high = values[:, :half], values[:, half:]
-            came = exchange(jnp.where(upper, low, high), axis, bit)
-            values = jnp.where(upper, high, low) + came
-            bit //= 2
-    return values
 
 
 def after(value, *others):
@@ -1064,7 +1082,6 @@
         .transpose(0, 2, 1, 3, 4)
         .reshape(shard_width, 3 * experts * hidden)
     )
-    expert_full = lax.all_gather(expert_local, "fsdp", axis=0, tiled=True)
 
     row_place = jnp.arange(rows, dtype=jnp.int32)
     span_pos = jnp.concatenate([shard_rank * span + rank * rows + row_place for rank in slot_ranks])
@@ -1084,15 +1101,16 @@
         if m == 0:
             wanted["weights"] = moves.gather_fsdp(qkv_local)
             wanted["small"] = moves.gather_both(small)
+            wanted["out"] = moves.gather_both(output_weight.T)
         if m == micro:
             wanted["gm"] = moves.gather_tp(own_grads[0])
-            wanted["out"] = moves.gather_both(output_weight.T)
         moves.run(m, 25, "open")
         if m == 0:
             qkv_full, router_full, gains = place_weights(
                 info_all, moves.get(wanted["weights"]), moves.get(wanted["small"]), experts
             )
             gain_attn, gain_moe = gains[0:1], gains[1:2]
+            out_all = moves.get(wanted["out"])
         if m:
             kv_alls.append(moves.get(wanted["kv"]))
         if m < micro:
@@ -1102,10 +1120,10 @@
             kvs.append(kv)
         else:
             gm_slots.append([own_grads[0]] + moves.get(wanted["gm"]))
-            out_all = moves.get(wanted["out"])
     for m in range(1, micro):
-        gm_slots.append(gather_slots(after(own_grads[m], gm_slots[m - 1][-1]), "tp"))
-
+        gm_slots.append(trade_slots([after(own_grads[m], gm_slots[m - 1][-1])] * slots, "tp"))
+
+    expert_full = lax.all_gather(after(expert_local, kv_alls[-1]), "fsdp", axis=0, tiled=True)
     order = kv_alls[-1]
     attended, logs, att_owns, middles, normeds, moe_slots = [], [], [], [], [], []
     for m in steps:
@@ -1124,63 +1142,90 @@
         att_owns.append(att_own)
         middles.append(middle)
         normeds.append(normed)
-        moe_slots.append(gather_slots(normed, "tp"))
+        if m == 0:
+            moe_slots.append(trade_slots([normed] * slots, "tp"))
 
     expert_outs, gin_parts = [], []
     for m in steps:
+        ride = Moves()
+        ahead = ride.share_tp(normeds[m + 1]) if m + 1 < micro else None
+        behind = ride.trade_tp(expert_outs[m - 1][:slots]) if m else None
         results = experts_both(
-            after(infos[m], order), routes[m], router_full, expert_full, moe_slots[m], gm_slots[m]
+            after(infos[m], order),
+            routes[m],
+            router_full,
+            expert_full,
+            moe_slots[m],
+            gm_slots[m],
+            ride,
+            2 * micro + 4 + m,
         )
         expert_outs.append(results)
-        gin_parts.append(scatter_slots(results[:slots]))
+        if ahead:
+            moe_slots.append([normeds[m + 1]] + ride.get(ahead))
+        if behind:
+            gin_parts.append([expert_outs[m - 1][0]] + ride.get(behind))
         order = results[2 * slots]
     lows_g = [results[2 * slots + 1] for results in expert_outs]
     lows_h = [results[2 * slots + 2] for results in expert_outs]
+    ride = Moves()
+    behind = ride.trade_tp(expert_outs[-1][:slots])
+    expert_grad = expert_grads(moe_slots, gm_slots, lows_g, lows_h, ride, 3 * micro + 4)
+    gin_parts.append([expert_outs[-1][0]] + ride.get(behind))
+    expert_sum = lax.psum_scatter(expert_grad, "fsdp", scatter_dimension=0, tiled=True)
 
     sums = 0.0
+    order = expert_grad
     grad_middles, grad_attns, grad_slots = [], [], []
-    expert_sums = []
-    pieces = 2
-    for m in range(max(pieces, micro)):
-        if m < pieces:
-            some_grad = expert_grads(
-                [[after(moe_slots[0][0], order)] + moe_slots[0][1:]] + moe_slots[1:], gm_slots, lows_g, lows_h, m, pieces
-            )
-            expert_sums.append(lax.psum_scatter(some_grad, "fsdp", scatter_dimension=0, tiled=True))
-            order = some_grad
-        if m < micro:
-            grad_middle, grad_attn, sums_moe, *grads = moe_back(
-                after(infos[m], order),
-                gin_parts[m],
-                expert_outs[m][2 * slots],
-                router_full,
-                middles[m],
-                normeds[m],
-                gain_moe,
-                cotangent[m],
-                out_full,
-                slots,
-            )
-            order = sums_moe
-            sums = sums + sums_moe
-            grad_middles.append(grad_middle)
-            grad_attns.append(grad_attn)
-            grad_slots.append(trade_slots(grads, "tp"))
+    moves = Moves()
+    for m in steps:
+        grad_middle, grad_attn, sums_moe, *grads = moe_back(
+            after(infos[m], order),
+            gin_parts[m],
+            expert_outs[m][2 * slots],
+            router_full,
+            middles[m],
+            normeds[m],
+            gain_moe,
+            cotangent[m],
+            out_full,
+            slots,
+        )
+        order = sums_moe
+        sums = sums + sums_moe
+        grad_middles.append(grad_middle)
+        grad_attns.append(grad_attn)
+        grad_slots.append((grads[0], moves.trade_tp(grads)))
+    moves.run(3 * micro + 5, 12, "trade_back")
+    grad_slots = [[own] + moves.get(spots) for own, spots in grad_slots]
     out_keep, out_send = weight_grad(after(info_all, order), grad_attns, att_owns, blocks)
     order = out_keep
 
+    out_met = exchange(out_send, "fsdp", 1)
+    out_stack = (out_keep.astype(f32) + out_met.astype(f32)).astype(bf16)
+
     dqs, dkvs, mixed_parts = [], [], []
     for m in steps:
-        dq, keep, send = attend_back(
+        dq, *dkv = attend_back(
             after(infos[m], order), queries[m], kv_alls[m], logs[m], cos_row, sin_row, attended[m], grad_slots[m]
         )
-        mixed_parts.append(scatter_slots([after(part, order) for part in expert_outs[m][slots : 2 * slots]]))
+        mixed = expert_outs[m][slots : 2 * slots]
+        mixed_parts.append(trade_slots([mixed[0]] + [after(part, order) for part in mixed[1:]], "tp"))
         order = dq
         dqs.append(dq)
-        dkvs.append(scatter_spans(keep, send))
+        if m + 1 < micro:
+            dkv = [dkv[0]] + [exchange(dkv[j], "fsdp", reversed_bits(j, blocks)) for j in range(1, blocks)]
+        dkvs.append(dkv)
 
     normed_all, qkv_grads, normed_parts = [], [], []
     for m in steps:
+        if m + 1 == micro:
+            moves = Moves()
+            came = moves.trade_fsdp(dkvs[m])
+            met = [moves.trade_tp(parts) for parts in normed_parts]
+            moves.run(2 * micro + 1, 24, "close_keys")
+            dkvs[m] = [dkvs[m][0]] + moves.get(came)
+            normed_parts = [[parts[0]] + moves.get(spots) for parts, spots in zip(normed_parts, met)]
         *parts, grads, normed_attn, sums_attn = qkv_back(
             dqs[m], dkvs[m], cos_row, sin_row, after(gain_attn, order), qkv_full, x_slots[m]
         )
@@ -1188,25 +1233,41 @@
         sums = sums + jnp.pad(sums_attn[0:1], ((1, 22), (0, 0)))
         normed_all.append(normed_attn)
         qkv_grads.append(grads)
-        normed_parts.append(scatter_slots(parts))
+        normed_parts.append(parts)
     qkv_keep, qkv_send = weight_grad(after(info_all, order), normed_all, qkv_grads, blocks)
-    qkv_sum = scatter_spans(qkv_keep, qkv_send)
-    small_sum = scatter_columns(sums)
-    out_sum = scatter_spans(out_keep, out_send).astype(bf16)
-    head_cols = output_weight.shape[0]
+    table = jnp.pad(sums, ((0, LANES - sums.shape[0]), (0, 0))).T
+
+    moves = Moves()
+    met = moves.trade_tp(normed_parts[-1])
+    near, far = moves.trade_stack(qkv_keep, 0, blocks), moves.trade_stack(qkv_send, blocks // 2, blocks)
+    out_spot = moves.trade_stack(out_stack, 0, blocks)
+    table_spot = moves.trade_rows(table, blocks)
+    moves.run(2 * micro + 2, 24, "close_weights")
+    normed_parts[-1] = [normed_parts[-1][0]] + moves.get(met)
+    total = lambda first, *stacks: first.astype(f32) + sum(jnp.sum(stack.astype(f32), axis=0) for stack in stacks)
+    out_sum = total(out_stack[0], moves.get(out_spot)).astype(bf16)
+    own_rows = lax.dynamic_slice_in_dim(table, shard_rank * shard_width, shard_width, 0)
+    table_sum = total(own_rows, moves.get(table_spot))
+    qkv_sum = total(qkv_keep[0], moves.get(near), moves.get(far))
+    head_cols, few = output_weight.shape[0], small.shape[0]
     out_parts = [out_sum[:, slot * head_cols : (slot + 1) * head_cols] for slot in range(slots)]
-    out_final = sum(part.astype(f32) for part in scatter_slots(out_parts))
-    outputs = close_outputs(after(info_all, qkv_keep), mixed_parts, middles, slots)
-    expert_sums[0] = after(expert_sums[0], outputs)
-    gate_sum, up_sum, down_sum = unpack_experts(expert_sums)
-    input_grad = close_input_grad(normed_parts, grad_middles, inputs, after(gain_attn, gate_sum))
+    table_parts = [lax.dynamic_slice_in_dim(table_sum, rank * few, few, 0) for rank in slot_ranks]
+    moves = Moves()
+    out_spots, table_spots = moves.trade_tp(out_parts), moves.trade_tp(table_parts)
+    moves.run(2 * micro + 3, 6, "close_small")
+    out_final = sum(part.astype(f32) for part in [out_parts[0]] + moves.get(out_spots))
+    small_sum = sum([table_parts[0]] + moves.get(table_spots))
+
+    outputs = close_outputs(after(info_all, normed_parts[-1][-1]), mixed_parts, middles, slots)
+    gate_sum, up_sum, down_sum = unpack_experts(expert_sum)
+    input_grad = close_input_grad(normed_parts, grad_middles, inputs, gain_attn)
     q_cols, k_cols = query_weight.shape[1], key_weight.shape[1]
     return (
         outputs,
         input_grad,
-        small_sum[1],
-        small_sum[0],
-        small_sum[8 : 8 + experts].T,
+        small_sum[:, 1],
+        small_sum[:, 0],
+        small_sum[:, 8 : 8 + experts],
         qkv_sum[:, :q_cols],
         qkv_sum[:, q_cols : q_cols + k_cols],
         qkv_sum[:, q_cols + k_cols : qkv_cols],

time: 579 us -> 566 us (0.978); the launches traced: 584 us -> 558 us
  Pallas kernels: 303 us -> 429 us
  waiting for transfers between devices: 107 us -> 0.76 us
  starting transfers between devices: 115 us -> 71.6 us
    pallas_call x5 -> x9, Pallas kernels: 119 us -> 227 us  [run(): pl.pallas_call(self.kernel, out_shape=self.outputs, in_specs=[anywhere] *...]
    ppermute x53 -> x20, waiting for transfers between devices: 107 us -> 0.7 us  [exchange(): return lax.ppermute(values, axis, [(i, i ^ bit) for i in range(count)])]
    ppermute x53 -> x20, starting transfers between devices: 115 us -> 71 us  [exchange(): return lax.ppermute(values, axis, [(i, i ^ bit) for i in range(count)])]
    pallas_call x8 -> x7, Pallas kernels: 98.7 us -> 116 us  [the longest x2 64 us: experts_both(): pl.pallas_call(functools.partial(expert_kernel, slots, ride), grid_spec=p...]
  transfers between devices with their start and end apart: 56 -> 22, of which waited for: 18 -> 1; matrix products, arithmetic and copies ran while one was open for 5% -> 4% of each run, Pallas kernels for 45% -> 48%
where the time goes in v1:
time: 566 us; the launch traced here: 558 us
  Pallas kernels  429 us (76%)
  starting transfers between devices  71.6 us (13%)
  local copies, waits for them, and re-layouts  22.8 us (4%)
  other arithmetic  19 us (3%)
  between operations  15.3 us (3%)
    pallas_call x9, Pallas kernels, run(): pl.pallas_call(self.kernel, out_shape=self.outputs, in_specs=[anywhere] *...  227 us
    ppermute x20, starting transfers between devices, exchange(): return lax.ppermute(values, axis, [(i, i ^ bit) for i in range(count)])  71 us
    pallas_call x2, Pallas kernels, experts_both(): pl.pallas_call(functools.partial(expert_kernel, slots, ride), grid_spec=p...  64 us
    pallas_call x1, Pallas kernels, expert_grads(): pl.pallas_call(functools.partial(expert_grad_kernel, micro, slots, ride),...  32 us
    pallas_call x2, Pallas kernels, attend_back(): pl.pallas_call(functools.partial(attend_back_kernel, slots), grid_spec=pl...  24.3 us
    pallas_call x2, Pallas kernels, attend(): pl.pallas_call(attend_kernel, grid_spec=pltpu.PrefetchScalarGridSpec(num_...  18.2 us
  transfers between devices with their start and end apart: 22, of which 1 were waited for; matrix products, arithmetic and copies ran while one was open for 4% of the time, Pallas kernels for 48%

profile of v1, /device:TPU:0, one launch (start us, length us, event | category | flops | bytes accessed | tf_op | source)
XLA Modules:
  0.0 558.4 jit_solution(9684952761875143012)
XLA Ops:
  9.4 1.9 slice_bitcast_fusion.5
  14.3 38.7 %open.3 = (bf16[128,1024]{1,0:T(8,128)(2,1)}, bf16[128,1024]{1,0:T(8,128)(2,1)}, bf16[128,1024]{1,0:T(8,128)(2,1)}, bf16[8,128,512]{2,1,0:T(8,128)(2,1)}, f32[8,...) custom-call(bf16[128,1024]{1,0:T(8,128)(2,1)} %get-tuple-element.415.refs_0_.x_ref.refs_8_, ...), custom_call_target="tpu_custom_call" | custom-call | flops 1500000000 | bytes 1024 | tf_op jit(solution)/shard_map/open/pallas_call | solution.py:1019
  53.0 3.3 place_weights.1
  56.3 1.4 fusion.13
  58.7 3.4 project_qkv.2
  62.1 21.8 %open.4 = (bf16[128,1024]{1,0:T(8,128)(2,1)}, bf16[128,1024]{1,0:T(8,128)(2,1)}, bf16[128,1024]{1,0:T(8,128)(2,1)}, bf16[8,512,256]{2,1,0:T(8,128)(2,1)}) custom-call(bf16[128,1024]{1,0:T(8,128)(2,1)} %get-tuple-element.200.refs_0_.x_ref.refs_8_, bf16[512,256]{1,0:T(8,128)(2,1)} %get-tuple-element.199.refs_1_), custom_call_target="tpu_custom_call" | custom-call | flops 1500000000 | bytes 1024 | tf_op jit(solution)/shard_map/open/pallas_call | solution.py:1019
  87.3 3.5 maximum_bitcast_fusion
  90.8 2.1 reshape.101
  92.9 3.4 project_qkv.3
  96.3 21.2 %open.5 = (bf16[8,512,256]{2,1,0:T(8,128)(2,1)}, bf16[128,1024]{1,0:T(8,128)(2,1)}, bf16[128,1024]{1,0:T(8,128)(2,1)}, bf16[128,1024]{1,0:T(8,128)(2,1)}) custom-call(bf16[512,256]{1,0:T(8,128)(2,1)} %get-tuple-element.204.refs_0_, bf16[128,1024]{1,0:T(8,128)(2,1)} %get-tuple-element.413.refs_1_.refs_4_.refs_8_), custom_call_target="tpu_custom_call" | custom-call | flops 1500000000 | bytes 1024 | tf_op jit(solution)/shard_map/open/pallas_call | solution.py:1019
  119.9 9.1 %attend.2 = (bf16[128,256]{1,0:T(8,128)(2,1)}, bf16[128,256]{1,0:T(8,128)(2,1)}, bf16[128,256]{1,0:T(8,128)(2,1)}, bf16[128,256]{1,0:T(8,128)(2,1)}, f32[8,512]{1,0:T(8,128)}) custom-call(s32[3]{0:T(128)} %pad_add_fusion.4.info_ref, bf16[512,256]{1,0:T(8,128)(2,1)} %get-tuple-element.207.q_ref, bf16[8,512,256]{2,1,0:T(8,128)(2,1)} %get-tuple-element.208.kv_ref), custom_call_target="tpu_custom_call" | custom-call | flops 720000000 | bytes 1024 | tf_op jit(solution)/shard_map/attend/pallas_call | solution.py:212
  129.0 3.8 place_output_weight.1.w_ref.refs_10_
  132.8 9.4 %trade.2 = (bf16[128,256]{1,0:T(8,128)(2,1)}, bf16[128,256]{1,0:T(8,128)(2,1)}, bf16[128,256]{1,0:T(8,128)(2,1)}) custom-call(bf16[128,256]{1,0:T(8,128)(2,1)} %get-tuple-element.213.refs_0_.refs_1_, bf16[128,256]{1,0:T(8,128)(2,1)} %get-tuple-element.214.refs_1_.refs_2_, bf16[128,256]{1,0:T(8,128)(2,1)} %get-tuple-element.215.refs_2_.refs_3_), custom_call_target="tpu_custom_call" | custom-call | flops 480000000 | bytes 1024 | tf_op jit(solution)/shard_map/trade/pallas_call | solution.py:1019
  142.2 3.5 middle.2
  145.7 2.2 collective-permute-start.1
  147.8 2.2 collective-permute-start.2
  150.1 2.2 collective-permute-start.4
  153.5 9.1 %attend.3 = (bf16[128,256]{1,0:T(8,128)(2,1)}, bf16[128,256]{1,0:T(8,128)(2,1)}, bf16[128,256]{1,0:T(8,128)(2,1)}, bf16[128,256]{1,0:T(8,128)(2,1)}, f32[8,512]{1,0:T(8,128)}) custom-call(s32[3]{0:T(128)} %pad_add_fusion.2.info_ref, bf16[512,256]{1,0:T(8,128)(2,1)} %get-tuple-element.222.q_ref, bf16[8,512,256]{2,1,0:T(8,128)(2,1)} %get-tuple-element.205.kv_ref), custom_call_target="tpu_custom_call" | custom-call | flops 720000000 | bytes 1024 | tf_op jit(solution)/shard_map/attend/pallas_call | solution.py:212
  162.6 25.2 %trade.3 = (bf16[128,256]{1,0:T(8,128)(2,1)}, bf16[128,256]{1,0:T(8,128)(2,1)}, bf16[128,256]{1,0:T(8,128)(2,1)}) custom-call(bf16[128,256]{1,0:T(8,128)(2,1)} %get-tuple-element.224.refs_0_.refs_1_, bf16[128,256]{1,0:T(8,128)(2,1)} %get-tuple-element.225.refs_1_.refs_2_, bf16[128,256]{1,0:T(8,128)(2,1)} %get-tuple-element.226.refs_2_.refs_3_), custom_call_target="tpu_custom_call" | custom-call | flops 480000000 | bytes 1024 | tf_op jit(solution)/shard_map/trade/pallas_call | solution.py:1019
  187.8 3.5 middle.3
  195.0 31.4 %experts.2 = (bf16[128,1152]{1,0:T(8,128)(2,1)}, bf16[128,1152]{1,0:T(8,128)(2,1)}, bf16[128,1152]{1,0:T(8,128)(2,1)}, bf16[128,1152]{1,0:T(8,128)(2,1)}, bf16[1...) custom-call(s32[3]{0:T(128)} %pad_add_fusion.4.info_ref, ...), custom_call_target="tpu_custom_call" | custom-call | flops 1440000000 | bytes 1024 | tf_op jit(solution)/shard_map/experts/pallas_call | solution.py:453
  227.3 32.6 %experts.3 = (bf16[128,1152]{1,0:T(8,128)(2,1)}, bf16[128,1152]{1,0:T(8,128)(2,1)}, bf16[128,1152]{1,0:T(8,128)(2,1)}, bf16[128,1152]{1,0:T(8,128)(2,1)}, bf16[1...) custom-call(s32[3]{0:T(128)} %pad_add_fusion.2.info_ref, ...), custom_call_target="tpu_custom_call" | custom-call | flops 1440000000 | bytes 1024 | tf_op jit(solution)/shard_map/experts/pallas_call | solution.py:453
  259.9 32.0 %expert_grads.1 = (bf16[1024,6144]{1,0:T(8,128)(2,1)}, bf16[128,1152]{1,0:T(8,128)(2,1)}, bf16[128,1152]{1,0:T(8,128)(2,1)}, bf16[128,1152]{1,0:T(8,128)(2,1)}) custom-call(bf16[128,1024]{1,0:T(8,128)(2,1)} %get-tuple-element.219.refs_0_.refs_7_, bf16[128,1024]{1,0:T(8,128)(2,1)} %copy-done.2, bf16[128,1024]{1,0:T(8,128)(2,1)} %copy-done.3, ...), custom_call_target="tpu_custom_call" | custom-call | flops 720000000 | bytes 1024 | tf_op jit(solution)/shard_map/expert_grads/pallas_call | solution.py:536
  292.8 4.8 moe_back.2
  297.6 4.7 moe_back.3
  302.3 4.2 weight_grad.2
  306.5 16.0 %trade_back.1 = (bf16[128,256]{1,0:T(8,128)(2,1)}, bf16[128,256]{1,0:T(8,128)(2,1)}, bf16[128,256]{1,0:T(8,128)(2,1)}, bf16[128,256]{1,0:T(8,128)(2,1)}, bf16[12...) custom-call(bf16[128,256]{1,0:T(8,128)(2,1)} %get-tuple-element.276.refs_0_, bf16[128,256]{1,0:T(8,128)(2,1)} %get-tuple-element.277.refs_1_, ...), custom_call_target="tpu_custom_call" | custom-call | flops 720000000 | bytes 1024 | tf_op jit(solution)/shard_map/trade_back/pallas_call | solution.py:1019
  322.6 12.2 %attend_back.2 = (bf16[512,256]{1,0:T(8,128)(2,1)}, bf16[512,256]{1,0:T(8,128)(2,1)}, bf16[512,256]{1,0:T(8,128)(2,1)}, bf16[512,256]{1,0:T(8,128)(2,1)}, bf16[5...) custom-call(s32[3]{0:T(128)} %pad_add_fusion.4.info_ref, ...), custom_call_target="tpu_custom_call" | custom-call | flops 1080000000 | bytes 1024 | tf_op jit(solution)/shard_map/attend_back/pallas_call | solution.py:315
  334.8 15.0 %collective-permute-start.10 = (bf16[512,256]{1,0:T(8,128)(2,1)}, bf16[512,256]{1,0:T(8,128)(2,1)S(1)}, u32[]{:S(2)}, u32[]{:S(2)}) collective-permute-start(bf16[512,256]{1,0:T(8,128)(2,1)} %get-tuple-element.299), channel_id=1, source_target_pairs={{0,20},{4,16},{8,28},{12,24},{16,4},{20,0},{24,12},{28,8},{1,21},{... | collective-permute-start | bytes 786440 | tf_op jit(solution)/shard_map/ppermute | solution.py:839
  349.8 15.4 %collective-permute-start.11 = (bf16[512,256]{1,0:T(8,128)(2,1)}, bf16[512,256]{1,0:T(8,128)(2,1)S(1)}, u32[]{:S(2)}, u32[]{:S(2)}) collective-permute-start(bf16[512,256]{1,0:T(8,128)(2,1)} %get-tuple-element.300), channel_id=1, source_target_pairs={{0,12},{4,8},{8,4},{12,0},{16,28},{20,24},{24,20},{28,16},{1,13},{... | collective-permute-start | bytes 786440 | tf_op jit(solution)/shard_map/ppermute | solution.py:839
  365.3 1.5 collective-permute-start.6
  366.7 9.6 %collective-permute-start.7 = (bf16[512,256]{1,0:T(8,128)(2,1)}, bf16[512,256]{1,0:T(8,128)(2,1)S(1)}, u32[]{:S(2)}, u32[]{:S(2)}) collective-permute-start(bf16[512,256]{1,0:T(8,128)(2,1)} %get-tuple-element.296), channel_id=1, source_target_pairs={{0,8},{4,12},{8,0},{12,4},{16,24},{20,28},{24,16},{28,20},{1,9},{5... | collective-permute-start | bytes 786440 | tf_op jit(solution)/shard_map/ppermute | solution.py:839
  377.0 7.2 %collective-permute-start.8 = (bf16[512,256]{1,0:T(8,128)(2,1)}, bf16[512,256]{1,0:T(8,128)(2,1)S(1)}, u32[]{:S(2)}, u32[]{:S(2)}) collective-permute-start(bf16[512,256]{1,0:T(8,128)(2,1)} %get-tuple-element.297), channel_id=1, source_target_pairs={{0,24},{4,28},{8,16},{12,20},{16,8},{20,12},{24,0},{28,4},{1,25},{... | collective-permute-start | bytes 786440 | tf_op jit(solution)/shard_map/ppermute | solution.py:839
  384.4 12.0 %attend_back.3 = (bf16[512,256]{1,0:T(8,128)(2,1)}, bf16[512,256]{1,0:T(8,128)(2,1)}, bf16[512,256]{1,0:T(8,128)(2,1)}, bf16[512,256]{1,0:T(8,128)(2,1)}, bf16[5...) custom-call(s32[3]{0:T(128)} %pad_add_fusion.2.info_ref, ...), custom_call_target="tpu_custom_call" | custom-call | flops 1080000000 | bytes 1024 | tf_op jit(solution)/shard_map/attend_back/pallas_call | solution.py:315
  396.5 3.0 collective-permute-start.19
  399.6 1.4 collective-permute-start.17
  401.0 3.0 collective-permute-start.16
  404.0 5.2 qkv_back.2
  410.1 40.8 %close_keys.1 = (bf16[512,256]{1,0:T(8,128)(2,1)}, bf16[512,256]{1,0:T(8,128)(2,1)}, bf16[512,256]{1,0:T(8,128)(2,1)}, bf16[512,256]{1,0:T(8,128)(2,1)}, bf16[51...) custom-call(bf16[512,256]{1,0:T(8,128)(2,1)} %get-tuple-element.305., ...), custom_call_target="tpu_custom_call" | custom-call | flops 1440000000 | bytes 1024 | tf_op jit(solution)/shard_map/close_keys/pallas_call | solution.py:1019
  450.9 5.2 qkv_back.3
  457.0 5.1 weight_grad.3
  463.3 6.3 %collective-permute-start.15 = (bf16[128,1024]{1,0:T(8,128)(2,1)}, bf16[128,1024]{1,0:T(8,128)(2,1)S(1)}, u32[]{:S(2)}, u32[]{:S(2)}) collective-permute-start(bf16[128,1024]{1,0:T(8,128)(2,1)} %get-tuple-element.340), channel_id=1, source_target_pairs={{0,2},{1,3},{2,0},{3,1},{4,6},{5,7},{6,4},{7,5},{8,10},{9,11},{10,... | collective-permute-start | bytes 786440 | tf_op jit(solution)/shard_map/ppermute | solution.py:839
  469.6 1.4 add_convert_fusion.refs_5_
  471.0 43.1 %close_weights.1 = (bf16[128,1024]{1,0:T(8,128)(2,1)}, bf16[128,1024]{1,0:T(8,128)(2,1)}, bf16[128,1024]{1,0:T(8,128)(2,1)}, bf16[3,128,512]{2,1,0:T(8,128)(2,1)...) custom-call(bf16[128,1024]{1,0:T(8,128)(2,1)} %get-tuple-element.322.refs_0_, ...), custom_call_target="tpu_custom_call" | custom-call | flops 1440000000 | bytes 1024 | tf_op jit(solution)/shard_map/close_weights/pallas_call | solution.py:1019
  519.0 11.2 %close_small.1 = (bf16[128,256]{1,0:T(8,128)(2,1)}, bf16[128,256]{1,0:T(8,128)(2,1)}, bf16[128,256]{1,0:T(8,128)(2,1)}, f32[32,128]{1,0:T(8,128)}, f32[32,128]{1,0:T(8,128)}, /*index=5*/f32[32,128]{1,0:T(8,128)}) custom-call(bf16[128,256]{1,0:T(8,128)(2,1)} %get-tuple-element.420.refs_0_, bf16[128,256]{1,0:T(8,128)(2,1)} %get-tuple-element.419.refs_1_, ...), custom_call_target="tpu_custom_call" | custom-call | flops 360000000 | bytes 1024 | tf_op jit(solution)/shard_map/close_small/pallas_call | solution.py:1019
  535.8 3.6 input_grad.1
  540.3 3.6 outputs.1
  545.2 5.8 %unpack.1 = (f32[16,128,128]{2,1,0:T(8,128)}, f32[16,128,128]{2,1,0:T(8,128)}, f32[16,128,128]{2,1,0:T(8,128)}) custom-call(bf16[128,6144]{1,0:T(8,128)(2,1)} %reduce-scatter.2.cloned.1.call-done.sum_ref), custom_call_target="tpu_custom_call" | custom-call | flops 300000000 | bytes 1024 | tf_op jit(solution)/shard_map/unpack/pallas_call | solution.py:817
  (152 shorter events, 34.9 us)
Async XLA Ops:
  7.2 4.0 copy-start.24
  7.2 4.8 copy-start.30
  7.2 4.8 copy-start.31
  7.2 4.9 copy-start.32
  7.2 5.0 copy-start.29
  7.2 5.7 %copy-start.25 = (bf16[128,256]{1,0:T(8,128)(2,1)S(1)}, bf16[128,256]{1,0:T(8,128)(2,1)}, u32[]{:S(2)}) copy-start(bf16[128,256]{1,0:T(8,128)(2,1)} %param.21) | copy-start | bytes 196612
  7.2 5.7 %copy-start.28 = (bf16[128,128]{1,0:T(8,128)(2,1)S(1)}, bf16[128,128]{1,0:T(8,128)(2,1)}, u32[]{:S(2)}) copy-start(bf16[128,128]{1,0:T(8,128)(2,1)} %param.22) | copy-start | bytes 98308
  7.3 5.7 %copy-start.27 = (bf16[128,128]{1,0:T(8,128)(2,1)S(1)}, bf16[128,128]{1,0:T(8,128)(2,1)}, u32[]{:S(2)}) copy-start(bf16[128,128]{1,0:T(8,128)(2,1)} %param.23) | copy-start | bytes 98308
  7.3 187.0 %all-gather.2.cloned.1.call-start = ((), (), s32[]{:S(2)}) async-start(), calls=%async_computation.1 | async-start | bytes 14155776 | tf_op jit(solution)/shard_map/all_gather | solution.py:1126
  62.1 21.9 %copy-start.1 = (bf16[2,128,1024]{2,1,0:T(8,128)(2,1)S(1)}, bf16[2,128,1024]{2,1,0:T(8,128)(2,1)}, u32[]{:S(2)}) copy-start(bf16[2,128,1024]{2,1,0:T(8,128)(2,1)} %param.15) | copy-start | bytes 1572868
  84.0 1.6 copy-start.12
  84.0 2.1 copy-start.13
  84.9 106.5 %copy-start = (bf16[128,1024]{1,0:T(8,128)(2,1)}, bf16[128,1024]{1,0:T(8,128)(2,1)S(1)}, u32[]{:S(2)}) copy-start(bf16[128,1024]{1,0:T(8,128)(2,1)S(1)} %get-tuple-element.241.refs_4_.refs_12_) | copy-start | bytes 786436
  117.5 427.7 %reduce-scatter.2.cloned.1.call-start = ((), (), s32[]{:S(2)}) async-start(), calls=%async_computation.2 | async-start | bytes 14155776 | tf_op jit(solution)/shard_map/reduce_scatter | solution.py:1175
  145.7 45.7 %collective-permute-start = (bf16[128,1024]{1,0:T(8,128)(2,1)}, bf16[128,1024]{1,0:T(8,128)(2,1)S(1)}, u32[]{:S(2)}, u32[]{:S(2)}) collective-permute-start(bf16[128,1024]{1,0:T(8,128)(2,1)} %get-tuple-element.219.refs_0_.refs_7_), channel_id=1, source_target_pairs={{0,1},{1,0},{2,3},{3,2},{4,5},{5,4},{6,7},{7,6},{8,9},{9,8},{10,11... | collective-permute-start | bytes 786440 | tf_op jit(solution)/shard_map/ppermute | solution.py:839
  145.7 48.6 %collective-permute-start.1 = (bf16[128,1024]{1,0:T(8,128)(2,1)}, bf16[128,1024]{1,0:T(8,128)(2,1)S(1)}, u32[]{:S(2)}, u32[]{:S(2)}) collective-permute-start(bf16[128,1024]{1,0:T(8,128)(2,1)} %get-tuple-element.219.refs_0_.refs_7_), channel_id=1, source_target_pairs={{0,2},{1,3},{2,0},{3,1},{4,6},{5,7},{6,4},{7,5},{8,10},{9,11},{10,... | collective-permute-start | bytes 786440 | tf_op jit(solution)/shard_map/ppermute | solution.py:839
  147.8 46.4 %collective-permute-start.2 = (bf16[128,1024]{1,0:T(8,128)(2,1)}, bf16[128,1024]{1,0:T(8,128)(2,1)S(1)}, u32[]{:S(2)}, u32[]{:S(2)}) collective-permute-start(bf16[128,1024]{1,0:T(8,128)(2,1)} %get-tuple-element.219.refs_0_.refs_7_), channel_id=1, source_target_pairs={{0,3},{1,2},{2,1},{3,0},{4,7},{5,6},{6,5},{7,4},{8,11},{9,10},{10,... | collective-permute-start | bytes 786440 | tf_op jit(solution)/shard_map/ppermute | solution.py:839
  150.1 76.4 %collective-permute-start.3 = (bf16[128,1024]{1,0:T(8,128)(2,1)S(1)}, bf16[128,1024]{1,0:T(8,128)(2,1)S(1)}, u32[]{:S(2)}, u32[]{:S(2)}) collective-permute-start(bf16[128,1024]{1,0:T(8,128)(2,1)S(1)} %get-tuple-element.241.refs_4_.refs_12_), channel_id=1, source_target_pairs={{0,1},{1,0},{2,3},{3,2},{4,5},{5,4},{6,7},{7,6},{8,9},{9,8},{10,11... | collective-permute-start | bytes 786440 | tf_op jit(solution)/shard_map/ppermute | solution.py:839
  150.1 76.4 %collective-permute-start.4 = (bf16[128,1024]{1,0:T(8,128)(2,1)S(1)}, bf16[128,1024]{1,0:T(8,128)(2,1)S(1)}, u32[]{:S(2)}, u32[]{:S(2)}) collective-permute-start(bf16[128,1024]{1,0:T(8,128)(2,1)S(1)} %get-tuple-element.241.refs_4_.refs_12_), channel_id=1, source_target_pairs={{0,2},{1,3},{2,0},{3,1},{4,6},{5,7},{6,4},{7,5},{8,10},{9,11},{10,... | collective-permute-start | bytes 786440 | tf_op jit(solution)/shard_map/ppermute | solution.py:839
  162.6 29.9 %copy-start.26 = (s32[2,512,8]{1,2,0:T(8,128)S(1)}, s32[2,512,8]{1,2,0:T(8,128)}, u32[]{:S(2)}) copy-start(s32[2,512,8]{1,2,0:T(8,128)} %param.17) | copy-start | bytes 98308
  191.4 3.0 copy-start.2
  191.4 35.1 %collective-permute-start.5 = (bf16[128,1024]{1,0:T(8,128)(2,1)S(1)}, bf16[128,1024]{1,0:T(8,128)(2,1)S(1)}, u32[]{:S(2)}, u32[]{:S(2)}) collective-permute-start(bf16[128,1024]{1,0:T(8,128)(2,1)S(1)} %get-tuple-element.241.refs_4_.refs_12_), channel_id=1, source_target_pairs={{0,3},{1,2},{2,1},{3,0},{4,7},{5,6},{6,5},{7,4},{8,11},{9,10},{10,... | collective-permute-start | bytes 786440 | tf_op jit(solution)/shard_map/ppermute | solution.py:839
  322.6 61.6 %copy-start.22 = (f32[24,1024]{1,0:T(8,128)S(1)}, f32[24,1024]{1,0:T(8,128)}, u32[]{:S(2)}) copy-start(f32[24,1024]{1,0:T(8,128)} %get-tuple-element.260) | copy-start | bytes 294916
  322.6 61.6 %copy-start.23 = (f32[24,1024]{1,0:T(8,128)S(1)}, f32[24,1024]{1,0:T(8,128)}, u32[]{:S(2)}) copy-start(f32[24,1024]{1,0:T(8,128)} %get-tuple-element.267) | copy-start | bytes 294916
  334.8 31.9 %collective-permute-start.10 = (bf16[512,256]{1,0:T(8,128)(2,1)}, bf16[512,256]{1,0:T(8,128)(2,1)S(1)}, u32[]{:S(2)}, u32[]{:S(2)}) collective-permute-start(bf16[512,256]{1,0:T(8,128)(2,1)} %get-tuple-element.299), channel_id=1, source_target_pairs={{0,20},{4,16},{8,28},{12,24},{16,4},{20,0},{24,12},{28,8},{1,21},{... | collective-permute-start | bytes 786440 | tf_op jit(solution)/shard_map/ppermute | solution.py:839
  349.8 27.2 %collective-permute-start.11 = (bf16[512,256]{1,0:T(8,128)(2,1)}, bf16[512,256]{1,0:T(8,128)(2,1)S(1)}, u32[]{:S(2)}, u32[]{:S(2)}) collective-permute-start(bf16[512,256]{1,0:T(8,128)(2,1)} %get-tuple-element.300), channel_id=1, source_target_pairs={{0,12},{4,8},{8,4},{12,0},{16,28},{20,24},{24,20},{28,16},{1,13},{... | collective-permute-start | bytes 786440 | tf_op jit(solution)/shard_map/ppermute | solution.py:839
  365.3 18.9 %collective-permute-start.12 = (bf16[512,256]{1,0:T(8,128)(2,1)}, bf16[512,256]{1,0:T(8,128)(2,1)S(1)}, u32[]{:S(2)}, u32[]{:S(2)}) collective-permute-start(bf16[512,256]{1,0:T(8,128)(2,1)} %get-tuple-element.301), channel_id=1, source_target_pairs={{0,28},{4,24},{8,20},{12,16},{16,12},{20,8},{24,4},{28,0},{1,29},{... | collective-permute-start | bytes 786440 | tf_op jit(solution)/shard_map/ppermute | solution.py:839
  365.3 98.0 %collective-permute-start.13 = (bf16[4,128,1024]{2,1,0:T(8,128)(2,1)}, bf16[4,128,1024]{2,1,0:T(8,128)(2,1)S(1)}, u32[]{:S(2)}, u32[]{:S(2)}) collective-permute-start(bf16[4,128,1024]{2,1,0:T(8,128)(2,1)} %get-tuple-element.333), channel_id=1, source_target_pairs={{0,4},{4,0},{8,12},{12,8},{16,20},{20,16},{24,28},{28,24},{1,5},{5... | collective-permute-start | bytes 3145736 | tf_op jit(solution)/shard_map/ppermute | solution.py:839
  365.3 31.2 %collective-permute-start.6 = (bf16[512,256]{1,0:T(8,128)(2,1)}, bf16[512,256]{1,0:T(8,128)(2,1)S(1)}, u32[]{:S(2)}, u32[]{:S(2)}) collective-permute-start(bf16[512,256]{1,0:T(8,128)(2,1)} %get-tuple-element.295), channel_id=1, source_target_pairs={{0,16},{4,20},{8,24},{12,28},{16,0},{20,4},{24,8},{28,12},{1,17},{... | collective-permute-start | bytes 786440 | tf_op jit(solution)/shard_map/ppermute | solution.py:839
  366.7 29.8 %copy-start.14 = (bf16[512,256]{1,0:T(8,128)(2,1)}, bf16[512,256]{1,0:T(8,128)(2,1)S(1)}, u32[]{:S(2)}) copy-start(bf16[512,256]{1,0:T(8,128)(2,1)S(1)} %collective-permute-done.10.refs_5_) | copy-start | bytes 786436
  366.7 32.8 %collective-permute-start.7 = (bf16[512,256]{1,0:T(8,128)(2,1)}, bf16[512,256]{1,0:T(8,128)(2,1)S(1)}, u32[]{:S(2)}, u32[]{:S(2)}) collective-permute-start(bf16[512,256]{1,0:T(8,128)(2,1)} %get-tuple-element.296), channel_id=1, source_target_pairs={{0,8},{4,12},{8,0},{12,4},{16,24},{20,28},{24,16},{28,20},{1,9},{5... | collective-permute-start | bytes 786440 | tf_op jit(solution)/shard_map/ppermute | solution.py:839
  377.0 19.5 %copy-start.15 = (bf16[512,256]{1,0:T(8,128)(2,1)}, bf16[512,256]{1,0:T(8,128)(2,1)S(1)}, u32[]{:S(2)}) copy-start(bf16[512,256]{1,0:T(8,128)(2,1)S(1)} %collective-permute-done.11.refs_6_) | copy-start | bytes 786436
  377.0 22.6 %collective-permute-start.8 = (bf16[512,256]{1,0:T(8,128)(2,1)}, bf16[512,256]{1,0:T(8,128)(2,1)S(1)}, u32[]{:S(2)}, u32[]{:S(2)}) collective-permute-start(bf16[512,256]{1,0:T(8,128)(2,1)} %get-tuple-element.297), channel_id=1, source_target_pairs={{0,24},{4,28},{8,16},{12,20},{16,8},{20,12},{24,0},{28,4},{1,25},{... | collective-permute-start | bytes 786440 | tf_op jit(solution)/shard_map/ppermute | solution.py:839
  384.2 12.3 %copy-start.16 = (bf16[512,256]{1,0:T(8,128)(2,1)}, bf16[512,256]{1,0:T(8,128)(2,1)S(1)}, u32[]{:S(2)}) copy-start(bf16[512,256]{1,0:T(8,128)(2,1)S(1)} %collective-permute-done.12.refs_7_) | copy-start | bytes 786436
  384.2 16.8 %collective-permute-start.9 = (bf16[512,256]{1,0:T(8,128)(2,1)}, bf16[512,256]{1,0:T(8,128)(2,1)}, u32[]{:S(2)}, u32[]{:S(2)}) collective-permute-start(bf16[512,256]{1,0:T(8,128)(2,1)} %get-tuple-element.298), channel_id=1, source_target_pairs={{0,4},{4,0},{8,12},{12,8},{16,20},{20,16},{24,28},{28,24},{1,5},{5... | collective-permute-start | bytes 786440 | tf_op jit(solution)/shard_map/ppermute | solution.py:839
  396.5 7.4 %copy-start.17 = (bf16[512,256]{1,0:T(8,128)(2,1)}, bf16[512,256]{1,0:T(8,128)(2,1)S(1)}, u32[]{:S(2)}) copy-start(bf16[512,256]{1,0:T(8,128)(2,1)S(1)} %collective-permute-done.6.refs_1_) | copy-start | bytes 786436
  396.5 134.6 %collective-permute-start.19 = (bf16[128,1024]{1,0:T(8,128)(2,1)}, bf16[128,1024]{1,0:T(8,128)(2,1)}, u32[]{:S(2)}, u32[]{:S(2)}) collective-permute-start(bf16[128,1024]{1,0:T(8,128)(2,1)} %get-tuple-element.349), channel_id=1, source_target_pairs={{0,3},{1,2},{2,1},{3,0},{4,7},{5,6},{6,5},{7,4},{8,11},{9,10},{10,... | collective-permute-start | bytes 786440 | tf_op jit(solution)/shard_map/ppermute | solution.py:839
  399.6 4.4 copy-start.18
  399.6 139.9 %collective-permute-start.18 = (bf16[128,1024]{1,0:T(8,128)(2,1)}, bf16[128,1024]{1,0:T(8,128)(2,1)}, u32[]{:S(2)}, u32[]{:S(2)}) collective-permute-start(bf16[128,1024]{1,0:T(8,128)(2,1)} %get-tuple-element.347), channel_id=1, source_target_pairs={{0,2},{1,3},{2,0},{3,1},{4,6},{5,7},{6,4},{7,5},{8,10},{9,11},{10,... | collective-permute-start | bytes 786440 | tf_op jit(solution)/shard_map/ppermute | solution.py:839
  399.6 4.4 copy-start.19
  399.6 139.9 %collective-permute-start.17 = (bf16[128,1024]{1,0:T(8,128)(2,1)}, bf16[128,1024]{1,0:T(8,128)(2,1)}, u32[]{:S(2)}, u32[]{:S(2)}) collective-permute-start(bf16[128,1024]{1,0:T(8,128)(2,1)} %get-tuple-element.345), channel_id=1, source_target_pairs={{0,1},{1,0},{2,3},{3,2},{4,5},{5,4},{6,7},{7,6},{8,9},{9,8},{10,11... | collective-permute-start | bytes 786440 | tf_op jit(solution)/shard_map/ppermute | solution.py:839
  401.0 138.4 %collective-permute-start.16 = (bf16[128,1024]{1,0:T(8,128)(2,1)}, bf16[128,1024]{1,0:T(8,128)(2,1)}, u32[]{:S(2)}, u32[]{:S(2)}) collective-permute-start(bf16[128,1024]{1,0:T(8,128)(2,1)} %get-tuple-element.342), channel_id=1, source_target_pairs={{0,3},{1,2},{2,1},{3,0},{4,7},{5,6},{6,5},{7,4},{8,11},{9,10},{10,... | collective-permute-start | bytes 786440 | tf_op jit(solution)/shard_map/ppermute | solution.py:839
  462.1 7.5 %copy-start.8 = (bf16[4,128,1024]{2,1,0:T(8,128)(2,1)S(1)}, bf16[4,128,1024]{2,1,0:T(8,128)(2,1)}, u32[]{:S(2)}) copy-start(bf16[4,128,1024]{2,1,0:T(8,128)(2,1)} %get-tuple-element.273) | copy-start | bytes 3145732
  463.3 76.2 %collective-permute-start.15 = (bf16[128,1024]{1,0:T(8,128)(2,1)}, bf16[128,1024]{1,0:T(8,128)(2,1)S(1)}, u32[]{:S(2)}, u32[]{:S(2)}) collective-permute-start(bf16[128,1024]{1,0:T(8,128)(2,1)} %get-tuple-element.340), channel_id=1, source_target_pairs={{0,2},{1,3},{2,0},{3,1},{4,6},{5,7},{6,4},{7,5},{8,10},{9,11},{10,... | collective-permute-start | bytes 786440 | tf_op jit(solution)/shard_map/ppermute | solution.py:839
  514.1 2.9 copy-start.10
  514.1 3.0 copy-start.9
  517.2 13.9 %copy-start.33 = (bf16[128,1024]{1,0:T(8,128)(2,1)S(1)}, bf16[128,1024]{1,0:T(8,128)(2,1)}, u32[]{:S(2)}) copy-start(bf16[128,1024]{1,0:T(8,128)(2,1)} %get-tuple-element.338) | copy-start | bytes 786436
  531.2 8.3 %collective-permute-start.14 = (bf16[128,1024]{1,0:T(8,128)(2,1)S(1)}, bf16[128,1024]{1,0:T(8,128)(2,1)S(1)}, u32[]{:S(2)}, u32[]{:S(2)}) collective-permute-start(bf16[128,1024]{1,0:T(8,128)(2,1)S(1)} %copy-done.33), channel_id=1, source_target_pairs={{0,1},{1,0},{2,3},{3,2},{4,5},{5,4},{6,7},{7,6},{8,9},{9,8},{10,11... | collective-permute-start | bytes 786440 | tf_op jit(solution)/shard_map/ppermute | solution.py:839
  (8 other events, 6.3 us)
Sparse Core Ops, SparseCore 0:
  117.7 71.0 all-gather.1
  292.1 122.7 reduce-scatter.1

commit v2 on v1

--- a/solution.py
+++ b/solution.py
@@ -236,9 +236,7 @@
 
 def attend_back_kernel(slots, info_ref, q_ref, kv_ref, log_ref, cos_ref, sin_ref, *refs):
     out_refs, grad_refs = refs[:slots], refs[slots : 2 * slots]
-    blocks = BLOCKS[0]
-    dq_ref, dkv_refs = refs[2 * slots], refs[2 * slots + 1 : 2 * slots + 1 + blocks]
-    heads, grads, delta, accum, dkv = refs[2 * slots + 1 + blocks :]
+    dq_ref, keep_ref, send_ref, heads, grads, delta, accum, dkv = refs[2 * slots :]
     j = pl.program_id(0)
     count = pl.num_programs(0)
     mine, rank, length = info_ref[0], info_ref[1], info_ref[2]
@@ -291,11 +289,13 @@
     def _():
         dkv[...] = jnp.zeros(dkv.shape, bf16)
 
-    for place in range(blocks):
-
-        @pl.when(j == place)
-        def _():
-            dkv_refs[place][...] = dkv[...]
+    @pl.when(j < count // 2)
+    def _():
+        keep_ref[0] = dkv[...]
+
+    @pl.when(j >= count // 2)
+    def _():
+        send_ref[0] = dkv[...]
 
     @pl.when(j == count - 1)
     def _():
@@ -309,7 +309,7 @@
 def attend_back(info, query, kv_all, log_total, cos_row, sin_row, att_slots, grad_slots):
     span, cols = query.shape
     blocks, slots = kv_all.shape[0], len(att_slots)
-    rows = span // slots
+    rows, half = span // slots, blocks // 2
     BLOCKS[0] = blocks
     fixed = lambda *dims: pl.BlockSpec(dims, lambda j, info_ref: (0,) * len(dims))
     return pl.pallas_call(
@@ -325,7 +325,11 @@
                 fixed(span, LANES),
             ]
             + [fixed(rows, cols)] * (2 * slots),
-            out_specs=[fixed(span, cols)] + [fixed(span, 2 * LANES)] * blocks,
+            out_specs=[
+                fixed(span, cols),
+                pl.BlockSpec((1, span, 2 * LANES), lambda j, info_ref: (jnp.minimum(j, half - 1), 0, 0)),
+                pl.BlockSpec((1, span, 2 * LANES), lambda j, info_ref: (jnp.maximum(j - half, 0), 0, 0)),
+            ],
             scratch_shapes=[
                 pltpu.VMEM((4, span, LANES), bf16),
                 pltpu.VMEM((4, span, LANES), bf16),
@@ -334,7 +338,7 @@
                 pltpu.VMEM((span, 2 * LANES), bf16),
             ],
         ),
-        out_shape=[shape((span, cols), bf16)] + [shape((span, 2 * LANES), bf16)] * blocks,
+        out_shape=[shape((span, cols), bf16)] + [shape((half, span, 2 * LANES), bf16)] * 2,
         compiler_params=params(),
         cost_estimate=cost(18),
         name="attend_back",
@@ -888,11 +892,16 @@
             self.copy((held, ()), (made[-1], ()), ("tp", slot), [], value.size * 4)
         return made
 
+    def swap(self, value):
+        held, target = self.take(value), self.make(value.shape, value.dtype)
+        self.copy((held, ()), (target, ()), ("fsdp", 1), [], value.size * 2)
+        return target
+
     def trade_fsdp(self, blocks):
         made = []
         for place in range(1, len(blocks)):
             made.append(self.make(blocks[place].shape, blocks[place].dtype))
-            slot = reversed_bits(place, len(blocks))
+            slot = 2 * reversed_bits(place, len(blocks))
             self.copy((self.take(blocks[place]), ()), (made[-1], ()), ("fsdp", slot), [], blocks[place].size * 4)
         return made
 
@@ -1125,25 +1134,28 @@
 
     expert_full = lax.all_gather(after(expert_local, kv_alls[-1]), "fsdp", axis=0, tiled=True)
     order = kv_alls[-1]
-    attended, logs, att_owns, middles, normeds, moe_slots = [], [], [], [], [], []
+    attended, logs, att_owns, middles, normeds = [], [], [], [], []
+    moves, spots = Moves(), []
     for m in steps:
         *att_slots, log_total = attend(after(infos[m], order), queries[m], kv_alls[m], rows)
-        if m == 0:
-            out_full = place_output_weight(after(info_all, log_total), out_all)
-        moves = Moves()
-        traded = moves.trade_tp(att_slots)
-        moves.run(micro + 1 + m, 8, "trade")
+        order = log_total
+        attended.append(att_slots)
+        logs.append(log_total)
+        spots.append(moves.trade_tp(att_slots))
+    out_full = place_output_weight(after(info_all, logs[0]), out_all)
+    moves.run(micro + 1, 12, "trade")
+    for m in steps:
         att_own, middle, normed = close_attention(
-            inputs[m], gain_moe, out_full, [att_slots[0]] + moves.get(traded)
+            inputs[m], gain_moe, out_full, [attended[m][0]] + moves.get(spots[m])
         )
         order = middle
-        attended.append(att_slots)
-        logs.append(log_total)
         att_owns.append(att_own)
         middles.append(middle)
         normeds.append(normed)
-        if m == 0:
-            moe_slots.append(trade_slots([normed] * slots, "tp"))
+    moves = Moves()
+    spot = moves.gather_tp(normeds[0])
+    moves.run(micro + 2, 18, "gather_normed")
+    moe_slots = [[normeds[0]] + moves.get(spot)]
 
     expert_outs, gin_parts = [], []
     for m in steps:
@@ -1196,25 +1208,27 @@
         grad_middles.append(grad_middle)
         grad_attns.append(grad_attn)
         grad_slots.append((grads[0], moves.trade_tp(grads)))
+    out_keep, out_send = weight_grad(after(info_all, order), grad_attns, att_owns, blocks)
+    out_spot = moves.swap(out_send)
     moves.run(3 * micro + 5, 12, "trade_back")
     grad_slots = [[own] + moves.get(spots) for own, spots in grad_slots]
-    out_keep, out_send = weight_grad(after(info_all, order), grad_attns, att_owns, blocks)
     order = out_keep
-
-    out_met = exchange(out_send, "fsdp", 1)
-    out_stack = (out_keep.astype(f32) + out_met.astype(f32)).astype(bf16)
+    out_stack = (out_keep.astype(f32) + moves.get(out_spot).astype(f32)).astype(bf16)
 
     dqs, dkvs, mixed_parts = [], [], []
     for m in steps:
-        dq, *dkv = attend_back(
+        dq, keep, send = attend_back(
             after(infos[m], order), queries[m], kv_alls[m], logs[m], cos_row, sin_row, attended[m], grad_slots[m]
         )
         mixed = expert_outs[m][slots : 2 * slots]
         mixed_parts.append(trade_slots([mixed[0]] + [after(part, order) for part in mixed[1:]], "tp"))
         order = dq
         dqs.append(dq)
+        met = exchange(send, "fsdp", 1)
+        half = blocks // 2
+        dkv = [(keep[j].astype(f32) + met[j].astype(f32)).astype(bf16) for j in range(half)]
         if m + 1 < micro:
-            dkv = [dkv[0]] + [exchange(dkv[j], "fsdp", reversed_bits(j, blocks)) for j in range(1, blocks)]
+            dkv = [dkv[0]] + [exchange(dkv[j], "fsdp", 2 * reversed_bits(j, half)) for j in range(1, half)]
         dkvs.append(dkv)
 
     normed_all, qkv_grads, normed_parts = [], [], []
@@ -1241,7 +1255,7 @@
     met = moves.trade_tp(normed_parts[-1])
     near, far = moves.trade_stack(qkv_keep, 0, blocks), moves.trade_stack(qkv_send, blocks // 2, blocks)
     out_spot = moves.trade_stack(out_stack, 0, blocks)
-    table_spot = moves.trade_rows(table, blocks)
+    table_spot = moves.trade_rows(table.astype(bf16), blocks)
     moves.run(2 * micro + 2, 24, "close_weights")
     normed_parts[-1] = [normed_parts[-1][0]] + moves.get(met)
     total = lambda first, *stacks: first.astype(f32) + sum(jnp.sum(stack.astype(f32), axis=0) for stack in stacks)

time: 566 us -> 545 us (0.963); the launches traced: 558 us -> 552 us
  Pallas kernels: 429 us -> 412 us
  other arithmetic: 19 us -> 25.9 us
    pallas_call x9, Pallas kernels: 227 us -> 214 us  [run(): pl.pallas_call(self.kernel, out_shape=self.outputs, in_specs=[anywhere] *...]
    convert_element_type x1 -> x3, other arithmetic: 1.37 us -> 7.22 us  [the longest x2 4.59 us: local(): (keep[j].astype(f32) + met[j].astype(f32)).astype(bf16)]
    ppermute x20 -> x14, starting transfers between devices: 71 us -> 71.9 us  [exchange(): return lax.ppermute(values, axis, [(i, i ^ bit) for i in range(count)])]
  transfers between devices with their start and end apart: 22 -> 16, of which waited for: 1 -> 2; matrix products, arithmetic and copies ran while one was open for 4% -> 5% of each run, Pallas kernels for 48% -> 45%
where the time goes in v2:
time: 545 us; the launch traced here: 552 us
  Pallas kernels  412 us (76%)
  starting transfers between devices  71.9 us (13%)
  other arithmetic  25.9 us (5%)
  local copies, waits for them, and re-layouts  22.2 us (4%)
  between operations  15.2 us (3%)
    pallas_call x9, Pallas kernels, run(): pl.pallas_call(self.kernel, out_shape=self.outputs, in_specs=[anywhere] *...  214 us
    ppermute x14, starting transfers between devices, exchange(): return lax.ppermute(values, axis, [(i, i ^ bit) for i in range(count)])  71.9 us
    pallas_call x2, Pallas kernels, experts_both(): pl.pallas_call(functools.partial(expert_kernel, slots, ride), grid_spec=p...  60.3 us
    pallas_call x1, Pallas kernels, expert_grads(): pl.pallas_call(functools.partial(expert_grad_kernel, micro, slots, ride),...  32.1 us
    pallas_call x2, Pallas kernels, attend_back(): pl.pallas_call(functools.partial(attend_back_kernel, slots), grid_spec=pl...  24.5 us
    pallas_call x2, Pallas kernels, attend(): pl.pallas_call(attend_kernel, grid_spec=pltpu.PrefetchScalarGridSpec(num_...  18.6 us
  transfers between devices with their start and end apart: 16, of which 2 were waited for; matrix products, arithmetic and copies ran while one was open for 5% of the time, Pallas kernels for 45%

profile of v2, /device:TPU:0, one launch (start us, length us, event | category | flops | bytes accessed | tf_op | source)
XLA Modules:
  0.0 552.4 jit_solution(5460867543432812787)
XLA Ops:
  9.4 1.9 slice_bitcast_fusion.5
  14.4 38.7 %open.3 = (bf16[128,1024]{1,0:T(8,128)(2,1)}, bf16[128,1024]{1,0:T(8,128)(2,1)}, bf16[128,1024]{1,0:T(8,128)(2,1)}, bf16[8,128,512]{2,1,0:T(8,128)(2,1)}, f32[8,...) custom-call(bf16[128,1024]{1,0:T(8,128)(2,1)} %get-tuple-element.399.refs_0_.x_ref.refs_4_, ...), custom_call_target="tpu_custom_call" | custom-call | flops 1500000000 | bytes 1024 | tf_op jit(solution)/shard_map/open/pallas_call | solution.py:1028
  53.1 3.3 place_weights.1
  56.4 1.4 fusion.22
  58.8 3.4 project_qkv.2
  62.2 21.8 %open.4 = (bf16[128,1024]{1,0:T(8,128)(2,1)}, bf16[128,1024]{1,0:T(8,128)(2,1)}, bf16[128,1024]{1,0:T(8,128)(2,1)}, bf16[8,512,256]{2,1,0:T(8,128)(2,1)}) custom-call(bf16[128,1024]{1,0:T(8,128)(2,1)} %get-tuple-element.188.refs_0_.x_ref.refs_4_, bf16[512,256]{1,0:T(8,128)(2,1)} %get-tuple-element.187.refs_1_), custom_call_target="tpu_custom_call" | custom-call | flops 1500000000 | bytes 1024 | tf_op jit(solution)/shard_map/open/pallas_call | solution.py:1028
  87.4 3.5 maximum_bitcast_fusion
  90.9 2.1 reshape.133
  93.0 3.4 project_qkv.3
  96.4 21.2 %open.5 = (bf16[8,512,256]{2,1,0:T(8,128)(2,1)}, bf16[128,1024]{1,0:T(8,128)(2,1)}, bf16[128,1024]{1,0:T(8,128)(2,1)}, bf16[128,1024]{1,0:T(8,128)(2,1)}) custom-call(bf16[512,256]{1,0:T(8,128)(2,1)} %get-tuple-element.192.refs_0_, bf16[128,1024]{1,0:T(8,128)(2,1)} %get-tuple-element.397.refs_1_.refs_4_.refs_8_), custom_call_target="tpu_custom_call" | custom-call | flops 1500000000 | bytes 1024 | tf_op jit(solution)/shard_map/open/pallas_call | solution.py:1028
  117.7 1.7 collective-permute-start
  120.6 1.5 collective-permute-start.2
  124.0 9.5 %attend.2 = (bf16[128,256]{1,0:T(8,128)(2,1)}, bf16[128,256]{1,0:T(8,128)(2,1)}, bf16[128,256]{1,0:T(8,128)(2,1)}, bf16[128,256]{1,0:T(8,128)(2,1)}, f32[8,512]{1,0:T(8,128)}) custom-call(s32[3]{0:T(128)} %pad_add_fusion.4.info_ref, bf16[512,256]{1,0:T(8,128)(2,1)} %get-tuple-element.195.q_ref, bf16[8,512,256]{2,1,0:T(8,128)(2,1)} %get-tuple-element.196.kv_ref), custom_call_target="tpu_custom_call" | custom-call | flops 720000000 | bytes 1024 | tf_op jit(solution)/shard_map/attend/pallas_call | solution.py:212
  134.7 9.1 %attend.3 = (bf16[128,256]{1,0:T(8,128)(2,1)}, bf16[128,256]{1,0:T(8,128)(2,1)}, bf16[128,256]{1,0:T(8,128)(2,1)}, bf16[128,256]{1,0:T(8,128)(2,1)}, f32[8,512]{1,0:T(8,128)}) custom-call(s32[3]{0:T(128)} %pad_add_fusion.2.info_ref, bf16[512,256]{1,0:T(8,128)(2,1)} %get-tuple-element.205.q_ref, bf16[8,512,256]{2,1,0:T(8,128)(2,1)} %get-tuple-element.193.kv_ref), custom_call_target="tpu_custom_call" | custom-call | flops 720000000 | bytes 1024 | tf_op jit(solution)/shard_map/attend/pallas_call | solution.py:212
  143.8 12.2 %trade.1 = (bf16[128,256]{1,0:T(8,128)(2,1)}, bf16[128,256]{1,0:T(8,128)(2,1)}, bf16[128,256]{1,0:T(8,128)(2,1)}, bf16[128,256]{1,0:T(8,128)(2,1)}, bf16[128,256]{1,0:T(8,128)(2,1)}, /*index=5*/bf16[128,256]{1,0:T(8,128)(2,1)}) custom-call(bf16[128,256]{1,0:T(8,128)(2,1)} %get-tuple-element.201.refs_0_.refs_1_, ...), custom_call_target="tpu_custom_call" | custom-call | flops 720000000 | bytes 1024 | tf_op jit(solution)/shard_map/trade/pallas_call | solution.py:1028
  156.1 3.8 place_output_weight.1.w_ref.refs_10_
  159.8 3.5 middle.3
  165.0 3.5 middle.2
  168.5 21.4 %gather_normed.1 = (bf16[128,1024]{1,0:T(8,128)(2,1)}, bf16[128,1024]{1,0:T(8,128)(2,1)}, bf16[128,1024]{1,0:T(8,128)(2,1)}) custom-call(bf16[128,1024]{1,0:T(8,128)(2,1)} %get-tuple-element.212.refs_0_.refs_7_), custom_call_target="tpu_custom_call" | custom-call | flops 1080000000 | bytes 1024 | tf_op jit(solution)/shard_map/gather_normed/pallas_call | solution.py:1028
  189.9 28.1 %experts.2 = (bf16[128,1152]{1,0:T(8,128)(2,1)}, bf16[128,1152]{1,0:T(8,128)(2,1)}, bf16[128,1152]{1,0:T(8,128)(2,1)}, bf16[128,1152]{1,0:T(8,128)(2,1)}, bf16[1...) custom-call(s32[3]{0:T(128)} %pad_add_fusion.4.info_ref, ...), custom_call_target="tpu_custom_call" | custom-call | flops 1440000000 | bytes 1024 | tf_op jit(solution)/shard_map/experts/pallas_call | solution.py:457
  218.9 32.2 %experts.3 = (bf16[128,1152]{1,0:T(8,128)(2,1)}, bf16[128,1152]{1,0:T(8,128)(2,1)}, bf16[128,1152]{1,0:T(8,128)(2,1)}, bf16[128,1152]{1,0:T(8,128)(2,1)}, bf16[1...) custom-call(s32[3]{0:T(128)} %pad_add_fusion.2.info_ref, ...), custom_call_target="tpu_custom_call" | custom-call | flops 1440000000 | bytes 1024 | tf_op jit(solution)/shard_map/experts/pallas_call | solution.py:457
  251.1 32.1 %expert_grads.1 = (bf16[1024,6144]{1,0:T(8,128)(2,1)}, bf16[128,1152]{1,0:T(8,128)(2,1)}, bf16[128,1152]{1,0:T(8,128)(2,1)}, bf16[128,1152]{1,0:T(8,128)(2,1)}) custom-call(bf16[128,1024]{1,0:T(8,128)(2,1)} %get-tuple-element.212.refs_0_.refs_7_, bf16[128,1024]{1,0:T(8,128)(2,1)} %get-tuple-element.213.refs_1_, ...), custom_call_target="tpu_custom_call" | custom-call | flops 720000000 | bytes 1024 | tf_op jit(solution)/shard_map/expert_grads/pallas_call | solution.py:540
  284.1 4.7 moe_back.2
  288.8 4.7 moe_back.3
  293.6 4.2 weight_grad.2
  297.8 17.1 %trade_back.1 = (bf16[128,256]{1,0:T(8,128)(2,1)}, bf16[128,256]{1,0:T(8,128)(2,1)}, bf16[128,256]{1,0:T(8,128)(2,1)}, bf16[128,256]{1,0:T(8,128)(2,1)}, bf16[12...) custom-call(bf16[128,256]{1,0:T(8,128)(2,1)} %get-tuple-element.267.refs_0_, ...), custom_call_target="tpu_custom_call" | custom-call | flops 720000000 | bytes 1024 | tf_op jit(solution)/shard_map/trade_back/pallas_call | solution.py:1028
  314.9 12.2 %attend_back.2 = (bf16[512,256]{1,0:T(8,128)(2,1)}, bf16[4,512,256]{2,1,0:T(8,128)(2,1)}, bf16[4,512,256]{2,1,0:T(8,128)(2,1)}) custom-call(s32[3]{0:T(128)} %pad_add_fusion.4.info_ref, bf16[512,256]{1,0:T(8,128)(2,1)} %get-tuple-element.195.q_ref, bf16[8,512,256]{2,1,0:T(8,128)(2,1)} %get-tuple-element.196.kv_ref, f32[8,512]{1,0:T(8,128)} %get-tuple-element.197.log_ref, ...), custom_call_target="tpu_custom_call" | custom-call | flops 1080000000 | bytes 1024 | tf_op jit(solution)/shard_map/attend_back/pallas_call | solution.py:315
  327.1 1.5 collective-permute-start.3
  328.6 12.3 %attend_back.3 = (bf16[512,256]{1,0:T(8,128)(2,1)}, bf16[4,512,256]{2,1,0:T(8,128)(2,1)}, bf16[4,512,256]{2,1,0:T(8,128)(2,1)}) custom-call(s32[3]{0:T(128)} %pad_add_fusion.2.info_ref, bf16[512,256]{1,0:T(8,128)(2,1)} %get-tuple-element.205.q_ref, bf16[8,512,256]{2,1,0:T(8,128)(2,1)} %get-tuple-element.193.kv_ref, f32[8,512]{1,0:T(8,128)} %get-tuple-element.279.log_ref, ...), custom_call_target="tpu_custom_call" | custom-call | flops 1080000000 | bytes 1024 | tf_op jit(solution)/shard_map/attend_back/pallas_call | solution.py:315
  341.0 2.8 collective-permute-start.7
  343.9 2.9 collective-permute-start.13
  347.4 2.6 add_convert_fusion.refs_5_
  350.0 2.2 fusion.5
  352.2 36.5 %collective-permute-start.4 = (bf16[512,256]{1,0:T(8,128)(2,1)S(1)}, bf16[512,256]{1,0:T(8,128)(2,1)S(1)}, u32[]{:S(2)}, u32[]{:S(2)}) collective-permute-start(bf16[512,256]{1,0:T(8,128)(2,1)S(1)} %get-tuple-element.392), channel_id=1, source_target_pairs={{0,16},{4,20},{8,24},{12,28},{16,0},{20,4},{24,8},{28,12},{1,17},{... | collective-permute-start | bytes 786440 | tf_op jit(solution)/shard_map/ppermute | solution.py:843
  388.8 16.0 %collective-permute-start.5 = (bf16[512,256]{1,0:T(8,128)(2,1)S(1)}, bf16[512,256]{1,0:T(8,128)(2,1)S(1)}, u32[]{:S(2)}, u32[]{:S(2)}) collective-permute-start(bf16[512,256]{1,0:T(8,128)(2,1)S(1)} %get-tuple-element.391), channel_id=1, source_target_pairs={{0,8},{4,12},{8,0},{12,4},{16,24},{20,28},{24,16},{28,20},{1,9},{5... | collective-permute-start | bytes 786440 | tf_op jit(solution)/shard_map/ppermute | solution.py:843
  404.8 2.4 fusion.9
  408.2 3.8 collective-permute-done.5.refs_2_
  411.9 2.9 collective-permute-start.10
  416.1 2.5 collective-permute-start.9
  418.6 4.7 qkv_back.2
  424.2 29.9 %close_keys.1 = (bf16[512,256]{1,0:T(8,128)(2,1)}, bf16[512,256]{1,0:T(8,128)(2,1)}, bf16[512,256]{1,0:T(8,128)(2,1)}, bf16[128,1024]{1,0:T(8,128)(2,1)}, bf16[1...) custom-call(bf16[512,256]{1,0:T(8,128)(2,1)} %get-tuple-element.388.refs_0_, bf16[512,256]{1,0:T(8,128)(2,1)} %get-tuple-element.387.refs_1_, ...), custom_call_target="tpu_custom_call" | custom-call | flops 1440000000 | bytes 1024 | tf_op jit(solution)/shard_map/close_keys/pallas_call | solution.py:1028
  454.1 4.8 qkv_back.3
  459.8 5.1 weight_grad.3
  466.0 41.1 %close_weights.1 = (bf16[128,1024]{1,0:T(8,128)(2,1)}, bf16[128,1024]{1,0:T(8,128)(2,1)}, bf16[128,1024]{1,0:T(8,128)(2,1)}, bf16[3,128,512]{2,1,0:T(8,128)(2,1)...) custom-call(bf16[128,1024]{1,0:T(8,128)(2,1)} %get-tuple-element.298.refs_0_, ...), custom_call_target="tpu_custom_call" | custom-call | flops 1440000000 | bytes 1024 | tf_op jit(solution)/shard_map/close_weights/pallas_call | solution.py:1028
  513.0 10.9 %close_small.1 = (bf16[128,256]{1,0:T(8,128)(2,1)}, bf16[128,256]{1,0:T(8,128)(2,1)}, bf16[128,256]{1,0:T(8,128)(2,1)}, f32[32,128]{1,0:T(8,128)}, f32[32,128]{1,0:T(8,128)}, /*index=5*/f32[32,128]{1,0:T(8,128)}) custom-call(bf16[128,256]{1,0:T(8,128)(2,1)} %get-tuple-element.404.refs_0_, bf16[128,256]{1,0:T(8,128)(2,1)} %get-tuple-element.403.refs_1_, ...), custom_call_target="tpu_custom_call" | custom-call | flops 360000000 | bytes 1024 | tf_op jit(solution)/shard_map/close_small/pallas_call | solution.py:1028
  529.6 3.6 input_grad.1
  534.2 3.6 outputs.1
  539.2 5.8 %unpack.1 = (f32[16,128,128]{2,1,0:T(8,128)}, f32[16,128,128]{2,1,0:T(8,128)}, f32[16,128,128]{2,1,0:T(8,128)}) custom-call(bf16[128,6144]{1,0:T(8,128)(2,1)} %reduce-scatter.2.cloned.1.call-done.sum_ref), custom_call_target="tpu_custom_call" | custom-call | flops 300000000 | bytes 1024 | tf_op jit(solution)/shard_map/unpack/pallas_call | solution.py:821
  (140 shorter events, 36.9 us)
Async XLA Ops:
  7.2 4.1 copy-start.23
  7.2 4.8 copy-start.29
  7.2 4.9 copy-start.30
  7.2 5.0 copy-start.31
  7.2 5.1 copy-start.28
  7.2 5.8 %copy-start.24 = (bf16[128,256]{1,0:T(8,128)(2,1)S(1)}, bf16[128,256]{1,0:T(8,128)(2,1)}, u32[]{:S(2)}) copy-start(bf16[128,256]{1,0:T(8,128)(2,1)} %param.21) | copy-start | bytes 196612
  7.2 5.8 %copy-start.27 = (bf16[128,128]{1,0:T(8,128)(2,1)S(1)}, bf16[128,128]{1,0:T(8,128)(2,1)}, u32[]{:S(2)}) copy-start(bf16[128,128]{1,0:T(8,128)(2,1)} %param.22) | copy-start | bytes 98308
  7.3 5.8 %copy-start.26 = (bf16[128,128]{1,0:T(8,128)(2,1)S(1)}, bf16[128,128]{1,0:T(8,128)(2,1)}, u32[]{:S(2)}) copy-start(bf16[128,128]{1,0:T(8,128)(2,1)} %param.23) | copy-start | bytes 98308
  7.3 182.6 %all-gather.2.cloned.1.call-start = ((), (), s32[]{:S(2)}) async-start(), calls=%async_computation.1 | async-start | bytes 14155776 | tf_op jit(solution)/shard_map/all_gather | solution.py:1135
  62.2 21.9 %copy-start.1 = (bf16[2,128,1024]{2,1,0:T(8,128)(2,1)S(1)}, bf16[2,128,1024]{2,1,0:T(8,128)(2,1)}, u32[]{:S(2)}) copy-start(bf16[2,128,1024]{2,1,0:T(8,128)(2,1)} %param.15) | copy-start | bytes 1572868
  84.1 1.0 copy-start.9
  84.1 1.6 copy-start.10
  84.1 2.1 copy-start.11
  85.0 35.7 %copy-start = (bf16[128,1024]{1,0:T(8,128)(2,1)}, bf16[128,1024]{1,0:T(8,128)(2,1)S(1)}, u32[]{:S(2)}) copy-start(bf16[128,1024]{1,0:T(8,128)(2,1)S(1)} %get-tuple-element.231.refs_4_.refs_12_) | copy-start | bytes 786436
  117.6 421.6 %reduce-scatter.2.cloned.1.call-start = ((), (), s32[]{:S(2)}) async-start(), calls=%async_computation.2 | async-start | bytes 14155776 | tf_op jit(solution)/shard_map/reduce_scatter | solution.py:1187
  117.7 100.4 %collective-permute-start = (bf16[128,1024]{1,0:T(8,128)(2,1)S(1)}, bf16[128,1024]{1,0:T(8,128)(2,1)S(1)}, u32[]{:S(2)}, u32[]{:S(2)}) collective-permute-start(bf16[128,1024]{1,0:T(8,128)(2,1)S(1)} %get-tuple-element.231.refs_4_.refs_12_), channel_id=1, source_target_pairs={{0,1},{1,0},{2,3},{3,2},{4,5},{5,4},{6,7},{7,6},{8,9},{9,8},{10,11... | collective-permute-start | bytes 786440 | tf_op jit(solution)/shard_map/ppermute | solution.py:843
  119.4 98.7 %collective-permute-start.1 = (bf16[128,1024]{1,0:T(8,128)(2,1)S(1)}, bf16[128,1024]{1,0:T(8,128)(2,1)S(1)}, u32[]{:S(2)}, u32[]{:S(2)}) collective-permute-start(bf16[128,1024]{1,0:T(8,128)(2,1)S(1)} %get-tuple-element.231.refs_4_.refs_12_), channel_id=1, source_target_pairs={{0,2},{1,3},{2,0},{3,1},{4,6},{5,7},{6,4},{7,5},{8,10},{9,11},{10,... | collective-permute-start | bytes 786440 | tf_op jit(solution)/shard_map/ppermute | solution.py:843
  120.6 97.4 %collective-permute-start.2 = (bf16[128,1024]{1,0:T(8,128)(2,1)S(1)}, bf16[128,1024]{1,0:T(8,128)(2,1)S(1)}, u32[]{:S(2)}, u32[]{:S(2)}) collective-permute-start(bf16[128,1024]{1,0:T(8,128)(2,1)S(1)} %get-tuple-element.231.refs_4_.refs_12_), channel_id=1, source_target_pairs={{0,3},{1,2},{2,1},{3,0},{4,7},{5,6},{6,5},{7,4},{8,11},{9,10},{10,... | collective-permute-start | bytes 786440 | tf_op jit(solution)/shard_map/ppermute | solution.py:843
  134.7 21.3 %copy-start.25 = (s32[2,512,8]{1,2,0:T(8,128)S(1)}, s32[2,512,8]{1,2,0:T(8,128)}, u32[]{:S(2)}) copy-start(s32[2,512,8]{1,2,0:T(8,128)} %param.17) | copy-start | bytes 98308
  218.0 0.7 copy-start.2
  218.1 0.8 copy-start.3
  218.1 0.8 copy-start.4
  327.1 16.6 %copy-start.21 = (f32[24,1024]{1,0:T(8,128)S(1)}, f32[24,1024]{1,0:T(8,128)}, u32[]{:S(2)}) copy-start(f32[24,1024]{1,0:T(8,128)} %get-tuple-element.251) | copy-start | bytes 294916
  327.1 16.6 %copy-start.22 = (f32[24,1024]{1,0:T(8,128)S(1)}, f32[24,1024]{1,0:T(8,128)}, u32[]{:S(2)}) copy-start(f32[24,1024]{1,0:T(8,128)} %get-tuple-element.258) | copy-start | bytes 294916
  327.1 22.9 %collective-permute-start.3 = (bf16[4,512,256]{2,1,0:T(8,128)(2,1)}, bf16[4,512,256]{2,1,0:T(8,128)(2,1)}, u32[]{:S(2)}, u32[]{:S(2)}) collective-permute-start(bf16[4,512,256]{2,1,0:T(8,128)(2,1)} %get-tuple-element.287), channel_id=1, source_target_pairs={{0,4},{4,0},{8,12},{12,8},{16,20},{20,16},{24,28},{28,24},{1,5},{5... | collective-permute-start | bytes 3145736 | tf_op jit(solution)/shard_map/ppermute | solution.py:843
  328.6 18.7 %copy-start.5 = (bf16[4,128,1024]{2,1,0:T(8,128)(2,1)S(1)}, bf16[4,128,1024]{2,1,0:T(8,128)(2,1)}, u32[]{:S(2)}) copy-start(bf16[4,128,1024]{2,1,0:T(8,128)(2,1)} %get-tuple-element.264) | copy-start | bytes 3145732
  340.9 9.1 %copy-start.7 = (bf16[4,512,256]{2,1,0:T(8,128)(2,1)S(1)}, bf16[4,512,256]{2,1,0:T(8,128)(2,1)}, u32[]{:S(2)}) copy-start(bf16[4,512,256]{2,1,0:T(8,128)(2,1)} %get-tuple-element.286) | copy-start | bytes 3145732
  341.0 63.8 %collective-permute-start.7 = (bf16[4,512,256]{2,1,0:T(8,128)(2,1)}, bf16[4,512,256]{2,1,0:T(8,128)(2,1)}, u32[]{:S(2)}, u32[]{:S(2)}) collective-permute-start(bf16[4,512,256]{2,1,0:T(8,128)(2,1)} %get-tuple-element.291), channel_id=1, source_target_pairs={{0,4},{4,0},{8,12},{12,8},{16,20},{20,16},{24,28},{28,24},{1,5},{5... | collective-permute-start | bytes 3145736 | tf_op jit(solution)/shard_map/ppermute | solution.py:843
  343.9 180.9 %collective-permute-start.13 = (bf16[128,1024]{1,0:T(8,128)(2,1)}, bf16[128,1024]{1,0:T(8,128)(2,1)S(1)}, u32[]{:S(2)}, u32[]{:S(2)}) collective-permute-start(bf16[128,1024]{1,0:T(8,128)(2,1)} %get-tuple-element.325), channel_id=1, source_target_pairs={{0,3},{1,2},{2,1},{3,0},{4,7},{5,6},{6,5},{7,4},{8,11},{9,10},{10,... | collective-permute-start | bytes 786440 | tf_op jit(solution)/shard_map/ppermute | solution.py:843
  346.8 186.3 %collective-permute-start.12 = (bf16[128,1024]{1,0:T(8,128)(2,1)}, bf16[128,1024]{1,0:T(8,128)(2,1)S(1)}, u32[]{:S(2)}, u32[]{:S(2)}) collective-permute-start(bf16[128,1024]{1,0:T(8,128)(2,1)} %get-tuple-element.323), channel_id=1, source_target_pairs={{0,2},{1,3},{2,0},{3,1},{4,6},{5,7},{6,4},{7,5},{8,10},{9,11},{10,... | collective-permute-start | bytes 786440 | tf_op jit(solution)/shard_map/ppermute | solution.py:843
  350.0 54.8 %copy-start.6 = (bf16[4,512,256]{2,1,0:T(8,128)(2,1)S(1)}, bf16[4,512,256]{2,1,0:T(8,128)(2,1)}, u32[]{:S(2)}) copy-start(bf16[4,512,256]{2,1,0:T(8,128)(2,1)} %get-tuple-element.290) | copy-start | bytes 3145732
  352.2 54.9 %collective-permute-start.4 = (bf16[512,256]{1,0:T(8,128)(2,1)S(1)}, bf16[512,256]{1,0:T(8,128)(2,1)S(1)}, u32[]{:S(2)}, u32[]{:S(2)}) collective-permute-start(bf16[512,256]{1,0:T(8,128)(2,1)S(1)} %get-tuple-element.392), channel_id=1, source_target_pairs={{0,16},{4,20},{8,24},{12,28},{16,0},{20,4},{24,8},{28,12},{1,17},{... | collective-permute-start | bytes 786440 | tf_op jit(solution)/shard_map/ppermute | solution.py:843
  388.8 23.2 %collective-permute-start.5 = (bf16[512,256]{1,0:T(8,128)(2,1)S(1)}, bf16[512,256]{1,0:T(8,128)(2,1)S(1)}, u32[]{:S(2)}, u32[]{:S(2)}) collective-permute-start(bf16[512,256]{1,0:T(8,128)(2,1)S(1)} %get-tuple-element.391), channel_id=1, source_target_pairs={{0,8},{4,12},{8,0},{12,4},{16,24},{20,28},{24,16},{28,20},{1,9},{5... | collective-permute-start | bytes 786440 | tf_op jit(solution)/shard_map/ppermute | solution.py:843
  404.8 11.3 %collective-permute-start.6 = (bf16[512,256]{1,0:T(8,128)(2,1)S(1)}, bf16[512,256]{1,0:T(8,128)(2,1)S(1)}, u32[]{:S(2)}, u32[]{:S(2)}) collective-permute-start(bf16[512,256]{1,0:T(8,128)(2,1)S(1)} %get-tuple-element.390), channel_id=1, source_target_pairs={{0,24},{4,28},{8,16},{12,20},{16,8},{20,12},{24,0},{28,4},{1,25},{... | collective-permute-start | bytes 786440 | tf_op jit(solution)/shard_map/ppermute | solution.py:843
  407.2 11.4 %copy-start.12 = (bf16[512,256]{1,0:T(8,128)(2,1)}, bf16[512,256]{1,0:T(8,128)(2,1)S(1)}, u32[]{:S(2)}) copy-start(bf16[512,256]{1,0:T(8,128)(2,1)S(1)} %collective-permute-done.4.refs_1_) | copy-start | bytes 786436
  407.2 126.0 %collective-permute-start.11 = (bf16[128,1024]{1,0:T(8,128)(2,1)}, bf16[128,1024]{1,0:T(8,128)(2,1)S(1)}, u32[]{:S(2)}, u32[]{:S(2)}) collective-permute-start(bf16[128,1024]{1,0:T(8,128)(2,1)} %get-tuple-element.321), channel_id=1, source_target_pairs={{0,1},{1,0},{2,3},{3,2},{4,5},{5,4},{6,7},{7,6},{8,9},{9,8},{10,11... | collective-permute-start | bytes 786440 | tf_op jit(solution)/shard_map/ppermute | solution.py:843
  411.9 6.6 %copy-start.13 = (bf16[512,256]{1,0:T(8,128)(2,1)}, bf16[512,256]{1,0:T(8,128)(2,1)S(1)}, u32[]{:S(2)}) copy-start(bf16[512,256]{1,0:T(8,128)(2,1)S(1)} %collective-permute-done.5.refs_2_) | copy-start | bytes 786436
  411.9 121.3 %collective-permute-start.10 = (bf16[128,1024]{1,0:T(8,128)(2,1)}, bf16[128,1024]{1,0:T(8,128)(2,1)S(1)}, u32[]{:S(2)}, u32[]{:S(2)}) collective-permute-start(bf16[128,1024]{1,0:T(8,128)(2,1)} %get-tuple-element.318), channel_id=1, source_target_pairs={{0,3},{1,2},{2,1},{3,0},{4,7},{5,6},{6,5},{7,4},{8,11},{9,10},{10,... | collective-permute-start | bytes 786440 | tf_op jit(solution)/shard_map/ppermute | solution.py:843
  416.1 2.5 copy-start.14
  416.1 117.2 %collective-permute-start.9 = (bf16[128,1024]{1,0:T(8,128)(2,1)}, bf16[128,1024]{1,0:T(8,128)(2,1)S(1)}, u32[]{:S(2)}, u32[]{:S(2)}) collective-permute-start(bf16[128,1024]{1,0:T(8,128)(2,1)} %get-tuple-element.316), channel_id=1, source_target_pairs={{0,2},{1,3},{2,0},{3,1},{4,6},{5,7},{6,4},{7,5},{8,10},{9,11},{10,... | collective-permute-start | bytes 786440 | tf_op jit(solution)/shard_map/ppermute | solution.py:843
  507.1 3.9 copy-start.8
  511.2 13.7 %copy-start.32 = (bf16[128,1024]{1,0:T(8,128)(2,1)S(1)}, bf16[128,1024]{1,0:T(8,128)(2,1)}, u32[]{:S(2)}) copy-start(bf16[128,1024]{1,0:T(8,128)(2,1)} %get-tuple-element.314) | copy-start | bytes 786436
  524.9 8.3 %copy-start.15 = (bf16[128,1024]{1,0:T(8,128)(2,1)}, bf16[128,1024]{1,0:T(8,128)(2,1)S(1)}, u32[]{:S(2)}) copy-start(bf16[128,1024]{1,0:T(8,128)(2,1)S(1)} %collective-permute-done.13.refs_7_) | copy-start | bytes 786436
  524.9 8.4 %collective-permute-start.8 = (bf16[128,1024]{1,0:T(8,128)(2,1)S(1)}, bf16[128,1024]{1,0:T(8,128)(2,1)S(1)}, u32[]{:S(2)}, u32[]{:S(2)}) collective-permute-start(bf16[128,1024]{1,0:T(8,128)(2,1)S(1)} %copy-done.32), channel_id=1, source_target_pairs={{0,1},{1,0},{2,3},{3,2},{4,5},{5,4},{6,7},{7,6},{8,9},{9,8},{10,11... | collective-permute-start | bytes 786440 | tf_op jit(solution)/shard_map/ppermute | solution.py:843
  533.2 0.8 copy-start.17
  533.2 0.8 copy-start.18
  533.2 0.9 copy-start.19
  533.3 1.0 copy-start.20
  (1 other events, 0.7 us)
Sparse Core Ops, SparseCore 0:
  117.7 71.0 all-gather.1
  283.4 122.8 reduce-scatter.1

commit v3 on v2

--- a/solution.py
+++ b/solution.py
@@ -1228,7 +1228,10 @@
         half = blocks // 2
         dkv = [(keep[j].astype(f32) + met[j].astype(f32)).astype(bf16) for j in range(half)]
         if m + 1 < micro:
-            dkv = [dkv[0]] + [exchange(dkv[j], "fsdp", 2 * reversed_bits(j, half)) for j in range(1, half)]
+            moves = Moves()
+            came = moves.trade_fsdp(dkv)
+            moves.run(3 * micro + 6 + m, 12, "early_keys")
+            dkv = [dkv[0]] + moves.get(came)
         dkvs.append(dkv)
 
     normed_all, qkv_grads, normed_parts = [], [], []
@@ -1237,7 +1240,9 @@
             moves = Moves()
             came = moves.trade_fsdp(dkvs[m])
             met = [moves.trade_tp(parts) for parts in normed_parts]
+            out_spot = moves.trade_stack(out_stack, 0, blocks)
             moves.run(2 * micro + 1, 24, "close_keys")
+            out_came = moves.get(out_spot)
             dkvs[m] = [dkvs[m][0]] + moves.get(came)
             normed_parts = [[parts[0]] + moves.get(spots) for parts, spots in zip(normed_parts, met)]
         *parts, grads, normed_attn, sums_attn = qkv_back(
@@ -1251,26 +1256,23 @@
     qkv_keep, qkv_send = weight_grad(after(info_all, order), normed_all, qkv_grads, blocks)
     table = jnp.pad(sums, ((0, LANES - sums.shape[0]), (0, 0))).T
 
+    total = lambda first, *stacks: first.astype(f32) + sum(jnp.sum(stack.astype(f32), axis=0) for stack in stacks)
+    head_cols, few = output_weight.shape[0], small.shape[0]
     moves = Moves()
     met = moves.trade_tp(normed_parts[-1])
     near, far = moves.trade_stack(qkv_keep, 0, blocks), moves.trade_stack(qkv_send, blocks // 2, blocks)
-    out_spot = moves.trade_stack(out_stack, 0, blocks)
+    out_sum = total(out_stack[0], out_came).astype(bf16)
+    out_parts = [out_sum[:, slot * head_cols : (slot + 1) * head_cols] for slot in range(slots)]
+    out_spots = moves.trade_tp(out_parts)
     table_spot = moves.trade_rows(table.astype(bf16), blocks)
     moves.run(2 * micro + 2, 24, "close_weights")
     normed_parts[-1] = [normed_parts[-1][0]] + moves.get(met)
-    total = lambda first, *stacks: first.astype(f32) + sum(jnp.sum(stack.astype(f32), axis=0) for stack in stacks)
-    out_sum = total(out_stack[0], moves.get(out_spot)).astype(bf16)
     own_rows = lax.dynamic_slice_in_dim(table, shard_rank * shard_width, shard_width, 0)
     table_sum = total(own_rows, moves.get(table_spot))
     qkv_sum = total(qkv_keep[0], moves.get(near), moves.get(far))
-    head_cols, few = output_weight.shape[0], small.shape[0]
-    out_parts = [out_sum[:, slot * head_cols : (slot + 1) * head_cols] for slot in range(slots)]
     table_parts = [lax.dynamic_slice_in_dim(table_sum, rank * few, few, 0) for rank in slot_ranks]
-    moves = Moves()
-    out_spots, table_spots = moves.trade_tp(out_parts), moves.trade_tp(table_parts)
-    moves.run(2 * micro + 3, 6, "close_small")
     out_final = sum(part.astype(f32) for part in [out_parts[0]] + moves.get(out_spots))
-    small_sum = sum([table_parts[0]] + moves.get(table_spots))
+    small_sum = sum(trade_slots(table_parts, "tp"))
 
     outputs = close_outputs(after(info_all, normed_parts[-1][-1]), mixed_parts, middles, slots)
     gate_sum, up_sum, down_sum = unpack_experts(expert_sum)

time: 545 us -> 540 us (level); the launches traced: 552 us -> 533 us
  starting transfers between devices: 71.9 us -> 22 us
  Pallas kernels: 412 us -> 451 us
    ppermute x14, starting transfers between devices: 71.9 us -> 22 us  [exchange(): return lax.ppermute(values, axis, [(i, i ^ bit) for i in range(count)])]
    pallas_call x9, Pallas kernels: 214 us -> 253 us  [run(): pl.pallas_call(self.kernel, out_shape=self.outputs, in_specs=[anywhere] *...]
  transfers between devices with their start and end apart: 16 -> 16, of which waited for: 2 -> 0; matrix products, arithmetic and copies ran while one was open for 5% -> 5% of each run, Pallas kernels for 45% -> 54%
where the time goes in v3:
time: 540 us; the launch traced here: 533 us
  Pallas kernels  451 us (84%)
  other arithmetic  23.1 us (4%)
  starting transfers between devices  22 us (4%)
  local copies, waits for them, and re-layouts  21.3 us (4%)
  between operations  15.1 us (3%)
    pallas_call x9, Pallas kernels, run(): pl.pallas_call(self.kernel, out_shape=self.outputs, in_specs=[anywhere] *...  253 us
    pallas_call x2, Pallas kernels, experts_both(): pl.pallas_call(functools.partial(expert_kernel, slots, ride), grid_spec=p...  60.1 us
    pallas_call x1, Pallas kernels, expert_grads(): pl.pallas_call(functools.partial(expert_grad_kernel, micro, slots, ride),...  32.1 us
    pallas_call x2, Pallas kernels, attend_back(): pl.pallas_call(functools.partial(attend_back_kernel, slots), grid_spec=pl...  24.8 us
    ppermute x14, starting transfers between devices, exchange(): return lax.ppermute(values, axis, [(i, i ^ bit) for i in range(count)])  22 us
    pallas_call x2, Pallas kernels, attend(): pl.pallas_call(attend_kernel, grid_spec=pltpu.PrefetchScalarGridSpec(num_...  18.6 us
  transfers between devices with their start and end apart: 16, of which 0 were waited for; matrix products, arithmetic and copies ran while one was open for 5% of the time, Pallas kernels for 54%

profile of v3, /device:TPU:0, one launch (start us, length us, event | category | flops | bytes accessed | tf_op | source)
XLA Modules:
  0.0 532.5 jit_solution(381571817619197441)
XLA Ops:
  9.4 1.8 slice_bitcast_fusion.5
  14.3 38.7 %open.3 = (bf16[128,1024]{1,0:T(8,128)(2,1)}, bf16[128,1024]{1,0:T(8,128)(2,1)}, bf16[128,1024]{1,0:T(8,128)(2,1)}, bf16[8,128,512]{2,1,0:T(8,128)(2,1)}, f32[8,...) custom-call(bf16[128,1024]{1,0:T(8,128)(2,1)} %get-tuple-element.399.refs_0_.x_ref.refs_4_, ...), custom_call_target="tpu_custom_call" | custom-call | flops 1500000000 | bytes 1024 | tf_op jit(solution)/shard_map/open/pallas_call | solution.py:1028
  53.0 3.3 place_weights.1
  56.3 1.4 fusion.22
  58.7 3.4 project_qkv.2
  62.1 21.8 %open.4 = (bf16[128,1024]{1,0:T(8,128)(2,1)}, bf16[128,1024]{1,0:T(8,128)(2,1)}, bf16[128,1024]{1,0:T(8,128)(2,1)}, bf16[8,512,256]{2,1,0:T(8,128)(2,1)}) custom-call(bf16[128,1024]{1,0:T(8,128)(2,1)} %get-tuple-element.188.refs_0_.x_ref.refs_4_, bf16[512,256]{1,0:T(8,128)(2,1)} %get-tuple-element.187.refs_1_), custom_call_target="tpu_custom_call" | custom-call | flops 1500000000 | bytes 1024 | tf_op jit(solution)/shard_map/open/pallas_call | solution.py:1028
  87.3 3.5 maximum_bitcast_fusion
  90.8 2.1 reshape.133
  92.9 3.4 project_qkv.3
  96.3 21.2 %open.5 = (bf16[8,512,256]{2,1,0:T(8,128)(2,1)}, bf16[128,1024]{1,0:T(8,128)(2,1)}, bf16[128,1024]{1,0:T(8,128)(2,1)}, bf16[128,1024]{1,0:T(8,128)(2,1)}) custom-call(bf16[512,256]{1,0:T(8,128)(2,1)} %get-tuple-element.192.refs_0_, bf16[128,1024]{1,0:T(8,128)(2,1)} %get-tuple-element.397.refs_1_.refs_4_.refs_8_), custom_call_target="tpu_custom_call" | custom-call | flops 1500000000 | bytes 1024 | tf_op jit(solution)/shard_map/open/pallas_call | solution.py:1028
  117.6 1.7 collective-permute-start
  120.6 1.5 collective-permute-start.2
  122.6 1.3 pad_add_fusion.4.info_ref
  123.9 9.5 %attend.2 = (bf16[128,256]{1,0:T(8,128)(2,1)}, bf16[128,256]{1,0:T(8,128)(2,1)}, bf16[128,256]{1,0:T(8,128)(2,1)}, bf16[128,256]{1,0:T(8,128)(2,1)}, f32[8,512]{1,0:T(8,128)}) custom-call(s32[3]{0:T(128)} %pad_add_fusion.4.info_ref, bf16[512,256]{1,0:T(8,128)(2,1)} %get-tuple-element.195.q_ref, bf16[8,512,256]{2,1,0:T(8,128)(2,1)} %get-tuple-element.196.kv_ref), custom_call_target="tpu_custom_call" | custom-call | flops 720000000 | bytes 1024 | tf_op jit(solution)/shard_map/attend/pallas_call | solution.py:212
  133.4 1.3 pad_add_fusion.2.info_ref
  134.7 9.1 %attend.3 = (bf16[128,256]{1,0:T(8,128)(2,1)}, bf16[128,256]{1,0:T(8,128)(2,1)}, bf16[128,256]{1,0:T(8,128)(2,1)}, bf16[128,256]{1,0:T(8,128)(2,1)}, f32[8,512]{1,0:T(8,128)}) custom-call(s32[3]{0:T(128)} %pad_add_fusion.2.info_ref, bf16[512,256]{1,0:T(8,128)(2,1)} %get-tuple-element.205.q_ref, bf16[8,512,256]{2,1,0:T(8,128)(2,1)} %get-tuple-element.193.kv_ref), custom_call_target="tpu_custom_call" | custom-call | flops 720000000 | bytes 1024 | tf_op jit(solution)/shard_map/attend/pallas_call | solution.py:212
  143.8 12.2 %trade.1 = (bf16[128,256]{1,0:T(8,128)(2,1)}, bf16[128,256]{1,0:T(8,128)(2,1)}, bf16[128,256]{1,0:T(8,128)(2,1)}, bf16[128,256]{1,0:T(8,128)(2,1)}, bf16[128,256]{1,0:T(8,128)(2,1)}, /*index=5*/bf16[128,256]{1,0:T(8,128)(2,1)}) custom-call(bf16[128,256]{1,0:T(8,128)(2,1)} %get-tuple-element.201.refs_0_.refs_1_, ...), custom_call_target="tpu_custom_call" | custom-call | flops 720000000 | bytes 1024 | tf_op jit(solution)/shard_map/trade/pallas_call | solution.py:1028
  156.1 3.8 place_output_weight.1.w_ref.refs_10_
  159.8 3.5 middle.3
  165.0 3.5 middle.2
  168.4 21.4 %gather_normed.1 = (bf16[128,1024]{1,0:T(8,128)(2,1)}, bf16[128,1024]{1,0:T(8,128)(2,1)}, bf16[128,1024]{1,0:T(8,128)(2,1)}) custom-call(bf16[128,1024]{1,0:T(8,128)(2,1)} %get-tuple-element.212.refs_0_.refs_7_), custom_call_target="tpu_custom_call" | custom-call | flops 1080000000 | bytes 1024 | tf_op jit(solution)/shard_map/gather_normed/pallas_call | solution.py:1028
  189.9 28.0 %experts.2 = (bf16[128,1152]{1,0:T(8,128)(2,1)}, bf16[128,1152]{1,0:T(8,128)(2,1)}, bf16[128,1152]{1,0:T(8,128)(2,1)}, bf16[128,1152]{1,0:T(8,128)(2,1)}, bf16[1...) custom-call(s32[3]{0:T(128)} %pad_add_fusion.4.info_ref, ...), custom_call_target="tpu_custom_call" | custom-call | flops 1440000000 | bytes 1024 | tf_op jit(solution)/shard_map/experts/pallas_call | solution.py:457
  218.8 32.1 %experts.3 = (bf16[128,1152]{1,0:T(8,128)(2,1)}, bf16[128,1152]{1,0:T(8,128)(2,1)}, bf16[128,1152]{1,0:T(8,128)(2,1)}, bf16[128,1152]{1,0:T(8,128)(2,1)}, bf16[1...) custom-call(s32[3]{0:T(128)} %pad_add_fusion.2.info_ref, ...), custom_call_target="tpu_custom_call" | custom-call | flops 1440000000 | bytes 1024 | tf_op jit(solution)/shard_map/experts/pallas_call | solution.py:457
  250.9 32.1 %expert_grads.1 = (bf16[1024,6144]{1,0:T(8,128)(2,1)}, bf16[128,1152]{1,0:T(8,128)(2,1)}, bf16[128,1152]{1,0:T(8,128)(2,1)}, bf16[128,1152]{1,0:T(8,128)(2,1)}) custom-call(bf16[128,1024]{1,0:T(8,128)(2,1)} %get-tuple-element.212.refs_0_.refs_7_, bf16[128,1024]{1,0:T(8,128)(2,1)} %get-tuple-element.213.refs_1_, ...), custom_call_target="tpu_custom_call" | custom-call | flops 720000000 | bytes 1024 | tf_op jit(solution)/shard_map/expert_grads/pallas_call | solution.py:540
  283.9 4.7 moe_back.2
  288.6 4.7 moe_back.3
  293.4 4.2 weight_grad.2
  297.5 17.1 %trade_back.1 = (bf16[128,256]{1,0:T(8,128)(2,1)}, bf16[128,256]{1,0:T(8,128)(2,1)}, bf16[128,256]{1,0:T(8,128)(2,1)}, bf16[128,256]{1,0:T(8,128)(2,1)}, bf16[12...) custom-call(bf16[128,256]{1,0:T(8,128)(2,1)} %get-tuple-element.267.refs_0_, ...), custom_call_target="tpu_custom_call" | custom-call | flops 720000000 | bytes 1024 | tf_op jit(solution)/shard_map/trade_back/pallas_call | solution.py:1028
  314.6 12.2 %attend_back.2 = (bf16[512,256]{1,0:T(8,128)(2,1)}, bf16[4,512,256]{2,1,0:T(8,128)(2,1)}, bf16[4,512,256]{2,1,0:T(8,128)(2,1)}) custom-call(s32[3]{0:T(128)} %pad_add_fusion.4.info_ref, bf16[512,256]{1,0:T(8,128)(2,1)} %get-tuple-element.195.q_ref, bf16[8,512,256]{2,1,0:T(8,128)(2,1)} %get-tuple-element.196.kv_ref, f32[8,512]{1,0:T(8,128)} %get-tuple-element.197.log_ref, ...), custom_call_target="tpu_custom_call" | custom-call | flops 1080000000 | bytes 1024 | tf_op jit(solution)/shard_map/attend_back/pallas_call | solution.py:315
  326.9 1.9 collective-permute-start.3
  328.8 12.6 %attend_back.3 = (bf16[512,256]{1,0:T(8,128)(2,1)}, bf16[4,512,256]{2,1,0:T(8,128)(2,1)}, bf16[4,512,256]{2,1,0:T(8,128)(2,1)}) custom-call(s32[3]{0:T(128)} %pad_add_fusion.2.info_ref, bf16[512,256]{1,0:T(8,128)(2,1)} %get-tuple-element.205.q_ref, bf16[8,512,256]{2,1,0:T(8,128)(2,1)} %get-tuple-element.193.kv_ref, f32[8,512]{1,0:T(8,128)} %get-tuple-element.279.log_ref, ...), custom_call_target="tpu_custom_call" | custom-call | flops 1080000000 | bytes 1024 | tf_op jit(solution)/shard_map/attend_back/pallas_call | solution.py:315
  341.3 3.0 collective-permute-start.4
  344.6 1.9 collective-permute-start.10
  346.5 1.5 collective-permute-start.9
  349.1 2.6 add_convert_fusion.refs_6_
  351.7 1.9 collective-permute-start.7
  353.5 2.3 fusion.5
  355.9 50.2 %early_keys.1 = (bf16[512,256]{1,0:T(8,128)(2,1)}, bf16[512,256]{1,0:T(8,128)(2,1)}, bf16[512,256]{1,0:T(8,128)(2,1)}) custom-call(bf16[512,256]{1,0:T(8,128)(2,1)} %get-tuple-element.392.refs_0_, bf16[512,256]{1,0:T(8,128)(2,1)} %get-tuple-element.391.refs_1_, bf16[512,256]{1,0:T(8,128)(2,1)} %get-tuple-element.390.refs_2_), custom_call_target="tpu_custom_call" | custom-call | flops 720000000 | bytes 1024 | tf_op jit(solution)/shard_map/early_keys/pallas_call | solution.py:1028
  406.1 4.8 qkv_back.2
  413.4 28.0 %close_keys.1 = (bf16[512,256]{1,0:T(8,128)(2,1)}, bf16[512,256]{1,0:T(8,128)(2,1)}, bf16[512,256]{1,0:T(8,128)(2,1)}, bf16[128,1024]{1,0:T(8,128)(2,1)}, bf16[1...) custom-call(bf16[512,256]{1,0:T(8,128)(2,1)} %get-tuple-element.388.refs_0_, ...), custom_call_target="tpu_custom_call" | custom-call | flops 1440000000 | bytes 1024 | tf_op jit(solution)/shard_map/close_keys/pallas_call | solution.py:1028
  441.4 4.8 qkv_back.3
  447.2 5.1 weight_grad.3
  455.2 42.4 %close_weights.1 = (bf16[128,1024]{1,0:T(8,128)(2,1)}, bf16[128,1024]{1,0:T(8,128)(2,1)}, bf16[128,1024]{1,0:T(8,128)(2,1)}, bf16[3,128,512]{2,1,0:T(8,128)(2,1)...) custom-call(bf16[128,1024]{1,0:T(8,128)(2,1)} %get-tuple-element.302, ...), custom_call_target="tpu_custom_call" | custom-call | flops 1440000000 | bytes 1024 | tf_op jit(solution)/shard_map/close_weights/pallas_call | solution.py:1028
  502.6 1.5 collective-permute-start.5
  505.9 2.7 collective-permute-start.13
  508.5 3.6 input_grad.1
  514.3 3.6 outputs.1
  519.4 5.8 %unpack.1 = (f32[16,128,128]{2,1,0:T(8,128)}, f32[16,128,128]{2,1,0:T(8,128)}, f32[16,128,128]{2,1,0:T(8,128)}) custom-call(bf16[128,6144]{1,0:T(8,128)(2,1)} %reduce-scatter.2.cloned.1.call-done.sum_ref), custom_call_target="tpu_custom_call" | custom-call | flops 300000000 | bytes 1024 | tf_op jit(solution)/shard_map/unpack/pallas_call | solution.py:821
  (132 shorter events, 32.6 us)
Async XLA Ops:
  7.2 4.0 copy-start.16
  7.2 4.7 copy-start.25
  7.2 4.8 copy-start.26
  7.2 4.9 copy-start.27
  7.2 5.0 copy-start.24
  7.2 5.7 %copy-start.17 = (bf16[128,256]{1,0:T(8,128)(2,1)S(1)}, bf16[128,256]{1,0:T(8,128)(2,1)}, u32[]{:S(2)}) copy-start(bf16[128,256]{1,0:T(8,128)(2,1)} %param.21) | copy-start | bytes 196612
  7.2 5.7 %copy-start.23 = (bf16[128,128]{1,0:T(8,128)(2,1)S(1)}, bf16[128,128]{1,0:T(8,128)(2,1)}, u32[]{:S(2)}) copy-start(bf16[128,128]{1,0:T(8,128)(2,1)} %param.22) | copy-start | bytes 98308
  7.3 5.7 %copy-start.22 = (bf16[128,128]{1,0:T(8,128)(2,1)S(1)}, bf16[128,128]{1,0:T(8,128)(2,1)}, u32[]{:S(2)}) copy-start(bf16[128,128]{1,0:T(8,128)(2,1)} %param.23) | copy-start | bytes 98308
  7.3 182.7 %all-gather.2.cloned.1.call-start = ((), (), s32[]{:S(2)}) async-start(), calls=%async_computation.1 | async-start | bytes 14155776 | tf_op jit(solution)/shard_map/all_gather | solution.py:1135
  62.1 21.9 %copy-start.1 = (bf16[2,128,1024]{2,1,0:T(8,128)(2,1)S(1)}, bf16[2,128,1024]{2,1,0:T(8,128)(2,1)}, u32[]{:S(2)}) copy-start(bf16[2,128,1024]{2,1,0:T(8,128)(2,1)} %param.15) | copy-start | bytes 1572868
  84.0 1.0 copy-start.9
  84.0 1.6 copy-start.10
  84.0 2.1 copy-start.11
  84.9 35.7 %copy-start = (bf16[128,1024]{1,0:T(8,128)(2,1)}, bf16[128,1024]{1,0:T(8,128)(2,1)S(1)}, u32[]{:S(2)}) copy-start(bf16[128,1024]{1,0:T(8,128)(2,1)S(1)} %get-tuple-element.231.refs_4_.refs_12_) | copy-start | bytes 786436
  117.5 401.8 %reduce-scatter.2.cloned.1.call-start = ((), (), s32[]{:S(2)}) async-start(), calls=%async_computation.2 | async-start | bytes 14155776 | tf_op jit(solution)/shard_map/reduce_scatter | solution.py:1187
  117.6 100.4 %collective-permute-start = (bf16[128,1024]{1,0:T(8,128)(2,1)S(1)}, bf16[128,1024]{1,0:T(8,128)(2,1)S(1)}, u32[]{:S(2)}, u32[]{:S(2)}) collective-permute-start(bf16[128,1024]{1,0:T(8,128)(2,1)S(1)} %get-tuple-element.231.refs_4_.refs_12_), channel_id=1, source_target_pairs={{0,1},{1,0},{2,3},{3,2},{4,5},{5,4},{6,7},{7,6},{8,9},{9,8},{10,11... | collective-permute-start | bytes 786440 | tf_op jit(solution)/shard_map/ppermute | solution.py:843
  119.3 98.7 %collective-permute-start.1 = (bf16[128,1024]{1,0:T(8,128)(2,1)S(1)}, bf16[128,1024]{1,0:T(8,128)(2,1)S(1)}, u32[]{:S(2)}, u32[]{:S(2)}) collective-permute-start(bf16[128,1024]{1,0:T(8,128)(2,1)S(1)} %get-tuple-element.231.refs_4_.refs_12_), channel_id=1, source_target_pairs={{0,2},{1,3},{2,0},{3,1},{4,6},{5,7},{6,4},{7,5},{8,10},{9,11},{10,... | collective-permute-start | bytes 786440 | tf_op jit(solution)/shard_map/ppermute | solution.py:843
  120.6 97.5 %collective-permute-start.2 = (bf16[128,1024]{1,0:T(8,128)(2,1)S(1)}, bf16[128,1024]{1,0:T(8,128)(2,1)S(1)}, u32[]{:S(2)}, u32[]{:S(2)}) collective-permute-start(bf16[128,1024]{1,0:T(8,128)(2,1)S(1)} %get-tuple-element.231.refs_4_.refs_12_), channel_id=1, source_target_pairs={{0,3},{1,2},{2,1},{3,0},{4,7},{5,6},{6,5},{7,4},{8,11},{9,10},{10,... | collective-permute-start | bytes 786440 | tf_op jit(solution)/shard_map/ppermute | solution.py:843
  134.7 21.3 %copy-start.21 = (s32[2,512,8]{1,2,0:T(8,128)S(1)}, s32[2,512,8]{1,2,0:T(8,128)}, u32[]{:S(2)}) copy-start(s32[2,512,8]{1,2,0:T(8,128)} %param.17) | copy-start | bytes 98308
  218.0 0.7 copy-start.2
  218.0 0.8 copy-start.3
  218.0 0.8 copy-start.4
  326.9 17.5 %copy-start.14 = (f32[24,1024]{1,0:T(8,128)S(1)}, f32[24,1024]{1,0:T(8,128)}, u32[]{:S(2)}) copy-start(f32[24,1024]{1,0:T(8,128)} %get-tuple-element.251) | copy-start | bytes 294916
  326.9 17.5 %copy-start.15 = (f32[24,1024]{1,0:T(8,128)S(1)}, f32[24,1024]{1,0:T(8,128)}, u32[]{:S(2)}) copy-start(f32[24,1024]{1,0:T(8,128)} %get-tuple-element.258) | copy-start | bytes 294916
  326.9 24.8 %collective-permute-start.3 = (bf16[4,512,256]{2,1,0:T(8,128)(2,1)}, bf16[4,512,256]{2,1,0:T(8,128)(2,1)}, u32[]{:S(2)}, u32[]{:S(2)}) collective-permute-start(bf16[4,512,256]{2,1,0:T(8,128)(2,1)} %get-tuple-element.287), channel_id=1, source_target_pairs={{0,4},{4,0},{8,12},{12,8},{16,20},{20,16},{24,28},{28,24},{1,5},{5... | collective-permute-start | bytes 3145736 | tf_op jit(solution)/shard_map/ppermute | solution.py:843
  328.8 20.3 %copy-start.6 = (bf16[4,128,1024]{2,1,0:T(8,128)(2,1)S(1)}, bf16[4,128,1024]{2,1,0:T(8,128)(2,1)}, u32[]{:S(2)}) copy-start(bf16[4,128,1024]{2,1,0:T(8,128)(2,1)} %get-tuple-element.264) | copy-start | bytes 3145732
  341.3 70.5 %collective-permute-start.4 = (bf16[4,512,256]{2,1,0:T(8,128)(2,1)}, bf16[4,512,256]{2,1,0:T(8,128)(2,1)S(1)}, u32[]{:S(2)}, u32[]{:S(2)}) collective-permute-start(bf16[4,512,256]{2,1,0:T(8,128)(2,1)} %get-tuple-element.294), channel_id=1, source_target_pairs={{0,4},{4,0},{8,12},{12,8},{16,20},{20,16},{24,28},{28,24},{1,5},{5... | collective-permute-start | bytes 3145736 | tf_op jit(solution)/shard_map/ppermute | solution.py:843
  344.6 8.9 %copy-start.7 = (bf16[4,512,256]{2,1,0:T(8,128)(2,1)S(1)}, bf16[4,512,256]{2,1,0:T(8,128)(2,1)}, u32[]{:S(2)}) copy-start(bf16[4,512,256]{2,1,0:T(8,128)(2,1)} %get-tuple-element.286) | copy-start | bytes 3145732
  344.6 157.9 %collective-permute-start.10 = (bf16[128,1024]{1,0:T(8,128)(2,1)}, bf16[128,1024]{1,0:T(8,128)(2,1)S(1)}, u32[]{:S(2)}, u32[]{:S(2)}) collective-permute-start(bf16[128,1024]{1,0:T(8,128)(2,1)} %get-tuple-element.329), channel_id=1, source_target_pairs={{0,3},{1,2},{2,1},{3,0},{4,7},{5,6},{6,5},{7,4},{8,11},{9,10},{10,... | collective-permute-start | bytes 786440 | tf_op jit(solution)/shard_map/ppermute | solution.py:843
  346.5 157.5 %collective-permute-start.9 = (bf16[128,1024]{1,0:T(8,128)(2,1)}, bf16[128,1024]{1,0:T(8,128)(2,1)}, u32[]{:S(2)}, u32[]{:S(2)}) collective-permute-start(bf16[128,1024]{1,0:T(8,128)(2,1)} %get-tuple-element.327), channel_id=1, source_target_pairs={{0,2},{1,3},{2,0},{3,1},{4,6},{5,7},{6,4},{7,5},{8,10},{9,11},{10,... | collective-permute-start | bytes 786440 | tf_op jit(solution)/shard_map/ppermute | solution.py:843
  348.0 156.8 %collective-permute-start.8 = (bf16[128,1024]{1,0:T(8,128)(2,1)}, bf16[128,1024]{1,0:T(8,128)(2,1)}, u32[]{:S(2)}, u32[]{:S(2)}) collective-permute-start(bf16[128,1024]{1,0:T(8,128)(2,1)} %get-tuple-element.325), channel_id=1, source_target_pairs={{0,1},{1,0},{2,3},{3,2},{4,5},{5,4},{6,7},{7,6},{8,9},{9,8},{10,11... | collective-permute-start | bytes 786440 | tf_op jit(solution)/shard_map/ppermute | solution.py:843
  351.7 154.2 %collective-permute-start.7 = (bf16[128,1024]{1,0:T(8,128)(2,1)}, bf16[128,1024]{1,0:T(8,128)(2,1)}, u32[]{:S(2)}, u32[]{:S(2)}) collective-permute-start(bf16[128,1024]{1,0:T(8,128)(2,1)} %get-tuple-element.322), channel_id=1, source_target_pairs={{0,3},{1,2},{2,1},{3,0},{4,7},{5,6},{6,5},{7,4},{8,11},{9,10},{10,... | collective-permute-start | bytes 786440 | tf_op jit(solution)/shard_map/ppermute | solution.py:843
  406.1 6.2 %copy-start.5 = (bf16[4,512,256]{2,1,0:T(8,128)(2,1)S(1)}, bf16[4,512,256]{2,1,0:T(8,128)(2,1)}, u32[]{:S(2)}) copy-start(bf16[4,512,256]{2,1,0:T(8,128)(2,1)} %get-tuple-element.293) | copy-start | bytes 3145732
  411.9 101.7 %collective-permute-start.6 = (bf16[128,1024]{1,0:T(8,128)(2,1)}, bf16[128,1024]{1,0:T(8,128)(2,1)}, u32[]{:S(2)}, u32[]{:S(2)}) collective-permute-start(bf16[128,1024]{1,0:T(8,128)(2,1)} %get-tuple-element.320), channel_id=1, source_target_pairs={{0,2},{1,3},{2,0},{3,1},{4,6},{5,7},{6,4},{7,5},{8,10},{9,11},{10,... | collective-permute-start | bytes 786440 | tf_op jit(solution)/shard_map/ppermute | solution.py:843
  452.2 1.1 copy-start.8
  497.6 5.0 copy-start.28
  497.6 6.4 %copy-start.18 = (bf16[128,256]{1,0:T(8,128)(2,1)S(1)}, bf16[128,256]{1,0:T(8,128)(2,1)}, u32[]{:S(2)}) copy-start(bf16[128,256]{1,0:T(8,128)(2,1)} %get-tuple-element.342) | copy-start | bytes 196612
  497.6 6.4 %copy-start.19 = (bf16[128,256]{1,0:T(8,128)(2,1)S(1)}, bf16[128,256]{1,0:T(8,128)(2,1)}, u32[]{:S(2)}) copy-start(bf16[128,256]{1,0:T(8,128)(2,1)} %get-tuple-element.343) | copy-start | bytes 196612
  497.6 6.4 %copy-start.20 = (bf16[128,256]{1,0:T(8,128)(2,1)S(1)}, bf16[128,256]{1,0:T(8,128)(2,1)}, u32[]{:S(2)}) copy-start(bf16[128,256]{1,0:T(8,128)(2,1)} %get-tuple-element.344) | copy-start | bytes 196612
  502.5 9.6 %copy-start.12 = (bf16[128,1024]{1,0:T(8,128)(2,1)}, bf16[128,1024]{1,0:T(8,128)(2,1)S(1)}, u32[]{:S(2)}) copy-start(bf16[128,1024]{1,0:T(8,128)(2,1)S(1)} %collective-permute-done.10.refs_7_) | copy-start | bytes 786436
  502.6 11.0 %collective-permute-start.5 = (bf16[128,1024]{1,0:T(8,128)(2,1)S(1)}, bf16[128,1024]{1,0:T(8,128)(2,1)S(1)}, u32[]{:S(2)}, u32[]{:S(2)}) collective-permute-start(bf16[128,1024]{1,0:T(8,128)(2,1)S(1)} %copy-done.28), channel_id=1, source_target_pairs={{0,1},{1,0},{2,3},{3,2},{4,5},{5,4},{6,7},{7,6},{8,9},{9,8},{10,11... | collective-permute-start | bytes 786440 | tf_op jit(solution)/shard_map/ppermute | solution.py:843
  504.1 13.8 %collective-permute-start.11 = (f32[32,128]{1,0:T(8,128)S(1)}, f32[32,128]{1,0:T(8,128)S(1)}, u32[]{:S(2)}, u32[]{:S(2)}) collective-permute-start(f32[32,128]{1,0:T(8,128)S(1)} %get-tuple-element.405), channel_id=1, source_target_pairs={{0,1},{1,0},{2,3},{3,2},{4,5},{5,4},{6,7},{7,6},{8,9},{9,8},{10,11... | collective-permute-start | bytes 49160 | tf_op jit(solution)/shard_map/ppermute | solution.py:843
  504.8 13.1 %collective-permute-start.12 = (f32[32,128]{1,0:T(8,128)S(1)}, f32[32,128]{1,0:T(8,128)S(1)}, u32[]{:S(2)}, u32[]{:S(2)}) collective-permute-start(f32[32,128]{1,0:T(8,128)S(1)} %get-tuple-element.407), channel_id=1, source_target_pairs={{0,2},{1,3},{2,0},{3,1},{4,6},{5,7},{6,4},{7,5},{8,10},{9,11},{10,... | collective-permute-start | bytes 49160 | tf_op jit(solution)/shard_map/ppermute | solution.py:843
  505.9 12.0 %collective-permute-start.13 = (f32[32,128]{1,0:T(8,128)S(1)}, f32[32,128]{1,0:T(8,128)S(1)}, u32[]{:S(2)}, u32[]{:S(2)}) collective-permute-start(f32[32,128]{1,0:T(8,128)S(1)} %get-tuple-element.406), channel_id=1, source_target_pairs={{0,3},{1,2},{2,1},{3,0},{4,7},{5,6},{6,5},{7,4},{8,11},{9,10},{10,... | collective-permute-start | bytes 49160 | tf_op jit(solution)/shard_map/ppermute | solution.py:843
  513.6 0.7 copy-start.13
Sparse Core Ops, SparseCore 0:
  117.7 71.0 all-gather.1
  283.2 110.2 reduce-scatter.1
